TPU v7x, 32 devices: a whole 2x2x4 slice. The times are simulated.
32 devices in a mesh: dp: 4 (over z), mp: 8 (over y, x, core).
Axes of the slice: x: 2, y: 2, z: 4, core: 2. Of those that a mesh axis runs over, the one named last changes fastest.
Arguments:
- features: bfloat16 [256, 256, 1, 16, 64], P('mp', None, None, 'dp'), may hold values from -6 to 6
- out_grad: bfloat16 [256, 256, 1, 16, 64], P('mp', None, None, 'dp'), may hold values from -6 to 6
- spectral_weight: bfloat16 [16, 32, 32, 64, 128], P('dp', 'mp'), may hold values from -1.5 to 1.5
- local_weight: bfloat16 [64, 64], replicated, may hold values from -0.75 to 0.75
Outputs:
- layer_out: bfloat16 [256, 256, 1, 16, 64], P('mp', None, None, 'dp')
- feature_grad: bfloat16 [256, 256, 1, 16, 64], P('mp', None, None, 'dp')
- spectral_grad: float32 [16, 32, 32, 64, 128], P('dp', 'mp')
- local_grad: float32 [64, 64], replicated
All inputs are finite; a program needn't handle non-finite values.
Results may differ from a plain program's by a relative error of at most 0.03.
Values may be sent and summed in bfloat16 or wider, within the bound.
No kernel may reach another device: no remote copies, remote signals or barrier semaphores. Data moves between devices by JAX's collectives and lax.ppermute only.
A program may use at most 192 MiB of HBM per device.

v0:
```python
import math

import jax
import jax.numpy as jnp
from jax import lax
from jax.sharding import PartitionSpec as P

NX = 256
NY = 256
KX = 32
KY = 32
SNAP = 1


def make_tables(slab_count):
    y_index = jnp.arange(NY, dtype=jnp.int32)
    k_index = jnp.arange(KY, dtype=jnp.int32)
    y_angle = 2.0 * math.pi / NY * (k_index[:, None] * y_index[None, :] % NY).astype(jnp.float32)
    y_scale = 1.0 / math.sqrt(NY)
    y_table = jnp.stack([jnp.cos(y_angle) * y_scale, -jnp.sin(y_angle) * y_scale]).astype(
        jnp.bfloat16
    )
    k_weight = jnp.where(k_index == 0, 1.0, 2.0).astype(jnp.float32)
    y_back = (jnp.transpose(y_table.astype(jnp.float32), (2, 0, 1)) * k_weight).astype(jnp.bfloat16)
    stored_index = jnp.arange(NX, dtype=jnp.int32)
    slab_rows = NX // slab_count
    x_index = stored_index % slab_rows * slab_count + stored_index // slab_rows
    frequency = jnp.arange(KX, dtype=jnp.int32) - KX // 2
    x_angle = 2.0 * math.pi / NX * (frequency[:, None] * x_index[None, :] % NX).astype(jnp.float32)
    x_scale = 1.0 / math.sqrt(NX)
    x_cosine = jnp.cos(x_angle) * x_scale
    x_sine = jnp.sin(x_angle) * x_scale
    x_table = jnp.stack(
        [jnp.stack([x_cosine, x_sine], 1), jnp.stack([-x_sine, x_cosine], 1)]
    ).astype(jnp.bfloat16)
    x_back = jnp.transpose(x_table, (2, 3, 0, 1))
    return (y_table, y_back, x_table, x_back)


def product(form, left, right):
    return jnp.einsum(form, left, right, preferred_element_type=jnp.float32)


def block_weights(weights):
    channels = weights.shape[-1] // 2
    w_real = weights[..., :channels]
    w_imag = weights[..., channels:]
    upper = jnp.concatenate([w_real, w_imag], -1)
    lower = jnp.concatenate([-w_imag, w_real], -1)
    return jnp.concatenate([upper, lower], -2)


def to_items(coeffs, snaps, zcount):
    mode_rows, _, kx_count, columns = coeffs.shape
    channels = columns // (snaps * zcount)
    shaped = coeffs.reshape(mode_rows, 2, kx_count, snaps, zcount, channels).transpose(
        4, 0, 2, 3, 1, 5
    )
    return shaped.reshape(zcount, mode_rows * kx_count, snaps, 2 * channels)


def from_items(mode_items, mode_rows, snaps):
    zcount, total, _, double = mode_items.shape
    channels = double // 2
    kx_count = total // mode_rows
    shaped = mode_items.reshape(zcount, mode_rows, kx_count, snaps, 2, channels).transpose(
        1, 4, 2, 3, 0, 5
    )
    return shaped.reshape(mode_rows, 2, kx_count, snaps * zcount * channels)


def combine(gram_blocks, mode_rows):
    channels = gram_blocks.shape[-1] // 2
    top_left = gram_blocks[..., :channels, :channels]
    top_right = gram_blocks[..., :channels, channels:]
    low_left = gram_blocks[..., channels:, :channels]
    low_right = gram_blocks[..., channels:, channels:]
    joined = jnp.concatenate([top_left + low_right, top_right - low_left], -1)
    return joined.reshape(gram_blocks.shape[0], mode_rows, -1, channels, 2 * channels)


def activation(values):
    return jax.nn.gelu(values, approximate=True)


def body(features, out_grad, spectral_weight, local_weight):
    y_table, y_back, x_table, x_back = make_tables(lax.axis_size("mp"))
    rows_here, grid_y, snaps, zcount, channels = features.shape
    columns = snaps * zcount * channels
    mode_rows = spectral_weight.shape[1]
    offset = lax.axis_index("mp") * rows_here
    x_back_own = lax.dynamic_slice_in_dim(x_back, offset, rows_here, 1)
    x_table_own = lax.dynamic_slice_in_dim(x_table, offset, rows_here, 3)

    def to_modes(spectrum):
        return lax.psum_scatter(
            product("ojrx,xrkq->kojq", x_table_own, spectrum).astype(jnp.bfloat16),
            "mp",
            scatter_dimension=0,
            tiled=True,
        )

    def to_rows(coeffs):
        return product(
            "rxoj,kojq->xrkq", x_back_own, lax.all_gather(coeffs, "mp", axis=0, tiled=True)
        ).astype(jnp.bfloat16)

    flat_field = features.reshape(rows_here, grid_y, columns)
    spectrum_y = product("xyq,rky->xrkq", flat_field, y_table).astype(jnp.bfloat16)
    mode_coeffs = to_modes(spectrum_y)
    blocks = block_weights(spectral_weight).reshape(zcount, -1, 2 * channels, 2 * channels)
    mode_items = to_items(mode_coeffs, snaps, zcount)
    mixed_items = product("zmpi,zmio->zmpo", mode_items, blocks).astype(jnp.bfloat16)
    grid_rows = to_rows(from_items(mixed_items, mode_rows, snaps))
    local_part = jnp.dot(
        features.reshape(-1, channels), local_weight, preferred_element_type=jnp.float32
    )
    preact = product("yrk,xrkq->xyq", y_back, grid_rows) + local_part.reshape(
        rows_here, grid_y, columns
    )
    output, pullback = jax.vjp(activation, preact)
    preact_grad = pullback(out_grad.reshape(rows_here, grid_y, columns).astype(jnp.float32))[
        0
    ].astype(jnp.bfloat16)
    local_term = jnp.dot(
        features.reshape(-1, channels).T,
        preact_grad.reshape(-1, channels),
        preferred_element_type=jnp.float32,
    )
    grad_scale = 1.0 / math.sqrt(NX * NY * SNAP * lax.axis_size("dp") * zcount)
    local_grad = lax.psum(local_term, ("dp", "mp")) * grad_scale
    rows_grad = product("yrk,xyq->xrkq", y_back, preact_grad).astype(jnp.bfloat16)
    mixed_grad = to_modes(rows_grad)
    grad_items = to_items(mixed_grad, snaps, zcount)
    gram_blocks = product("zmpi,zmpo->zmio", mode_items, grad_items)
    spectral_grad = combine(gram_blocks, mode_rows)
    back_items = product("zmpo,zmio->zmpi", grad_items, blocks).astype(jnp.bfloat16)
    spectrum_grad = to_rows(from_items(back_items, mode_rows, snaps))
    local_back = jnp.dot(
        preact_grad.reshape(-1, channels), local_weight.T, preferred_element_type=jnp.float32
    )
    back_field = product("rky,xrkq->xyq", y_table, spectrum_grad) + local_back.reshape(
        rows_here, grid_y, columns
    )
    layer_out = output.astype(jnp.bfloat16).reshape(features.shape)
    feature_grad = back_field.astype(jnp.bfloat16).reshape(features.shape)
    return (layer_out, feature_grad, spectral_grad, local_grad)


def solution(mesh):
    placed = (
        P("mp", None, None, "dp", None),
        P("mp", None, None, "dp", None),
        P("dp", "mp", None, None, None),
        P(),
    )
    return jax.shard_map(
        body,
        mesh=mesh,
        in_specs=placed,
        out_specs=(
            P("mp", None, None, "dp", None),
            P("mp", None, None, "dp", None),
            P("dp", "mp", None, None, None),
            P(),
        ),
        check_vma=False,
    )
```

profile of v0, /device:TPU:0, one launch (start us, length us, event | category | flops | bytes accessed | tf_op | source)
XLA Modules:
  0.0 325.2 jit_solution(8694081158683600945)
XLA Ops:
  7.3 0.1 multiply_convert_fusion.3
  7.4 0.2 negate_convert_fusion
  7.6 0.1 fusion.38
  7.7 3.6 %fusion.16 = bf16[32,2,32,256,1]{3,2,0,1,4:T(8,128)(2,1)S(1)} fusion(bf16[32,256,256,1]{1,2,0,3:T(8,128)(2,1)} %bitcast.172, bf16[1,32,256]{2,1,0:T(8,128)(2,1)S(1)} %get-tuple-element.31, bf16[1,32,256]{2,1,0:T(8,128)(2,1)S(1)} %get-tuple-element.32), kind=kOutput, calls=%fused_computation.32 | convolution fusion | flops 269025280 | bytes 5275648 | tf_op jit(solution)/shard_map/xyq,rky->xrkq/dot_general | solution.py:41
  11.3 1.9 fusion.20
  13.2 9.1 %slice_negate_fusion = (bf16[4,4,32,64,64]{4,3,2,1,0:T(8,128)(2,1)S(1)}, bf16[4,4,32,64,64]{4,3,2,1,0:T(8,128)(2,1)S(1)}) fusion(bf16[4,4,32,64,128]{4,3,2,1,0:T(8,128)(2,1)} %param.6), kind=kLoop, calls=%fused_computation.23 | loop fusion | flops 2097152 | bytes 16777216 | tf_op jit(solution)/shard_map/neg | solution.py:49
  22.3 14.4 %maximum_maximum_fusion = bf16[4,4,32,128,128]{4,3,2,1,0:T(8,128)(2,1)} fusion(bf16[4,4,32,64,64]{4,3,2,1,0:T(8,128)(2,1)S(1)} %get-tuple-element.25, bf16[4,4,32,64,64]{4,3,2,1,0:T(8,128)(2,1)S(1)} %get-tuple-element.24, bf16[4,4,32,64,128]{4,3,2,1,0:T(8,128)(2,1)} %param.6), kind=kLoop, calls=%fused_computation.2 | loop fusion | flops 50331648 | bytes 33554432 | tf_op jit(solution)/shard_map/concatenate | solution.py:50
  36.7 15.4 %reduce-scatter.3.cloned.1.call-done = bf16[4,2,32,256]{3,2,1,0:T(8,128)(2,1)} async-done(((bf16[32,2,32,256]{3,2,1,0:T(8,128)(2,1)}), bf16[4,2,32,256]{3,2,1,0:T(8,128)(2,1)}) %reduce-scatter.3.cloned.1.call-update) | async-done | bytes 131088 | tf_op jit(solution)/shard_map/reduce_scatter | solution.py:96
  52.1 1.1 reshape.352
  53.1 0.3 copy.109
  53.4 0.2 reshape.391
  53.6 8.0 %fusion.55 = f32[4,128,1,128]{3,2,1,0:T(1,128)S(1)} fusion(bf16[4,128,128,1]{2,3,1,0:T(2,128)(2,1)S(1)} %reshape.391, bf16[4,128,128,128]{3,2,1,0:T(8,128)(2,1)} %bitcast.167), kind=kOutput, calls=%fused_computation.97 | convolution fusion | flops 16777216 | bytes 17170432 | tf_op jit(solution)/shard_map/zmpi,zmio->zmpo/dot_general | solution.py:41
  61.7 0.1 reshape.355
  61.8 0.2 copy.46
  62.0 0.9 reshape.356
  62.9 0.2 reduce-scatter.5.cloned.1.call-start
  63.1 12.6 %copy.49 = bf16[32,256,1,4,64]{4,3,1,0,2:T(4,128)(2,1)} copy(bf16[32,256,1,4,64]{1,4,3,2,0:T(8,128)(2,1)} %param.4) | data formatting | bytes 8388608 | tf_op args[0]
  75.8 11.9 %fusion.56 = f32[32768,64]{1,0:T(8,128)} fusion(bf16[32768,64]{1,0:T(8,128)(2,1)} %bitcast.169, bf16[64,64]{1,0:T(8,128)(2,1)S(1)} %copy-done), kind=kOutput, calls=%fused_computation.98 | convolution fusion | flops 268435456 | bytes 12591104 | tf_op jit(solution)/shard_map/dot_general | solution.py:115
  87.6 14.3 %reshape.358 = f32[32,256,256]{2,1,0:T(8,128)} reshape(f32[32768,64]{1,0:T(8,128)} %fusion.56) | data formatting | bytes 16777216 | tf_op jit(solution)/shard_map/reshape | solution.py:118
  102.0 8.9 %copy.51 = f32[32,256,256]{1,2,0:T(8,128)} copy(f32[32,256,256]{2,1,0:T(8,128)} %reshape.358) | data formatting | bytes 16777216 | tf_op jit(solution)/shard_map/reshape | solution.py:118
  110.9 0.1 reshape.353
  111.1 1.7 fusion.22
  112.8 12.0 %fusion.2 = (bf16[32,256,256]{1,2,0:T(8,128)(2,1)S(1)}, bf16[32,256,256]{1,2,0:T(8,128)(2,1)}) fusion(bf16[32,256,1,4,64]{1,4,3,2,0:T(8,128)(2,1)} %param.5, f32[32,256,256]{1,2,0:T(8,128)} %copy.51, f32[32]{0:T(128)S(1)} %compare_select_fusion, bf16[1,32,256]{2,1,0:T(8,128)(2,1)S(1)} %get-tuple-element.31, bf16[1,32,256]{2,1,0:T(8,128)(2,1)S(1)} %get-tuple-element.32, ...), kind=kOutput, calls=%fused_computation.11 | convolution fusion | flops 318832640 | bytes 22052992 | tf_op jit(solution)/shard_map/yrk,xrkq->xyq/dot_general | solution.py:41
  124.8 2.0 copy-done.2
  126.8 1.4 fusion.17
  128.2 6.4 %copy.58 = bf16[32,256,256]{2,1,0:T(8,128)(2,1)} copy(bf16[32,256,256]{1,2,0:T(8,128)(2,1)} %copy-done.2) | data formatting | bytes 8388608 | tf_op jit(solution)/shard_map/convert_element_type | solution.py:124
  134.6 1.9 fusion.21
  136.5 0.0 all-gather.5.cloned.1.call-start
  136.6 11.2 %reshape.364 = bf16[32768,64]{1,0:T(8,128)(2,1)} reshape(bf16[32,256,256]{2,1,0:T(8,128)(2,1)} %copy.58) | data formatting | bytes 8388608 | tf_op jit(solution)/shard_map/reshape | solution.py:140
  147.7 8.2 %convolution_bitcast_fusion = f32[64,64]{0,1:T(8,128)S(1)} fusion(bf16[32768,64]{1,0:T(8,128)(2,1)} %reshape.364, bf16[32768,64]{1,0:T(8,128)(2,1)} %bitcast.170), kind=kOutput, calls=%fused_computation.38 | convolution fusion | flops 268435456 | bytes 8404992 | tf_op jit(solution)/shard_map/dot_general | solution.py:125
  155.9 39.8 %psum.7 = f32[64,64]{0,1:T(8,128)S(1)} all-reduce(f32[64,64]{0,1:T(8,128)S(1)} %convolution_bitcast_fusion), channel_id=1, replica_groups=mesh['dp'=4,'mp'=8] {'dp','mp'}, use_global_device_ids=true, to_apply=%region_2.3 | all-reduce | flops 4096 | bytes 32768 | tf_op jit(solution)/shard_map/psum | solution.py:131
  195.7 0.7 copy.63
  196.4 11.9 %fusion.58 = f32[32768,64]{1,0:T(8,128)} fusion(bf16[32768,64]{1,0:T(8,128)(2,1)} %reshape.364, bf16[64,64]{1,0:T(8,128)(2,1)S(1)} %copy-done), kind=kOutput, calls=%fused_computation.100 | convolution fusion | flops 268435456 | bytes 12591104 | tf_op jit(solution)/shard_map/dot_general | solution.py:139
  208.2 14.4 %reshape.365 = f32[32,256,256]{2,1,0:T(8,128)} reshape(f32[32768,64]{1,0:T(8,128)} %fusion.58) | data formatting | bytes 16777216 | tf_op jit(solution)/shard_map/reshape | solution.py:142
  222.6 9.0 %copy.60 = f32[32,256,256]{1,2,0:T(8,128)} copy(f32[32,256,256]{2,1,0:T(8,128)} %reshape.365) | data formatting | bytes 16777216 | tf_op jit(solution)/shard_map/reshape | solution.py:142
  231.6 1.1 reshape.360
  232.7 0.3 copy.108
  233.0 0.1 reshape.361
  233.1 0.2 reshape.393
  233.3 12.2 %fusion.57 = f32[4,128,1,128]{3,2,1,0:T(1,128)S(1)} fusion(bf16[4,128,128,1]{2,3,1,0:T(2,128)(2,1)S(1)} %reshape.393, bf16[4,128,128,128]{3,2,1,0:T(8,128)(2,1)} %bitcast.168), kind=kOutput, calls=%fused_computation.99 | convolution fusion | flops 16777216 | bytes 17170432 | tf_op jit(solution)/shard_map/zmpo,zmio->zmpi/dot_general | solution.py:41
  245.5 0.1 reshape.362
  245.7 0.2 copy.55
  245.9 0.9 reshape.363
  246.8 11.4 %broadcast_multiply_fusion = f32[4,128,128,128]{3,2,1,0:T(8,128)} fusion(f32[4,128,128]{2,1,0:T(8,128)S(1)} %convert.35, f32[4,128,128]{2,1,0:T(8,128)S(1)} %convert.34), kind=kLoop, calls=%fused_computation.4 | loop fusion | flops 8388608 | bytes 34078720 | tf_op jit(solution)/shard_map/zmpi,zmpo->zmio/dot_general | solution.py:41
  258.3 34.2 %slice_add_fusion = (f32[4,128,64,64]{3,2,1,0:T(8,128)}, f32[4,128,64,64]{3,2,1,0:T(8,128)}) fusion(f32[4,128,128,128]{3,2,1,0:T(8,128)} %broadcast_multiply_fusion), kind=kLoop, calls=%fused_computation.1 | loop fusion | flops 4194304 | bytes 50331648 | tf_op jit(solution)/shard_map/add | solution.py:78
  292.5 17.0 %pad_maximum_fusion = f32[4,128,64,128]{3,2,1,0:T(8,128)} fusion(f32[4,128,64,64]{3,2,1,0:T(8,128)} %get-tuple-element.21, f32[4,128,64,64]{3,2,1,0:T(8,128)} %get-tuple-element.20), kind=kLoop, calls=%fused_computation.3 | loop fusion | flops 4194304 | bytes 33554432 | tf_op jit(solution)/shard_map/concatenate | solution.py:78
  309.5 1.7 fusion.23
  311.2 7.5 %fusion.10 = bf16[32,256,256]{1,2,0:T(8,128)(2,1)} fusion(f32[32,256,256]{1,2,0:T(8,128)} %copy.60, bf16[32,2,32,256]{3,0,1,2:T(8,128)(2,1)S(1)} %fusion.23, bf16[1,32,256]{2,1,0:T(8,128)(2,1)S(1)} %get-tuple-element.31, bf16[1,32,256]{2,1,0:T(8,128)(2,1)S(1)} %get-tuple-element.32), kind=kOutput, calls=%fused_computation.20 | convolution fusion | flops 272646144 | bytes 13664256 | tf_op jit(solution)/shard_map/rky,xrkq->xyq/dot_general | solution.py:41
  (23 shorter events, 0.3 us)
Async XLA Ops:
  7.2 68.6 %copy-start = (bf16[64,64]{1,0:T(8,128)(2,1)S(1)}, bf16[64,64]{1,0:T(8,128)(2,1)}, u32[]{:S(2)}) copy-start(bf16[64,64]{1,0:T(8,128)(2,1)} %param.7) | copy-start | bytes 24580
  7.2 44.9 %reduce-scatter.3.cloned.1.call-start = ((), (), s32[]{:S(2)}) async-start(), calls=%async_computation.2 | async-start | bytes 1179648 | tf_op jit(solution)/shard_map/reduce_scatter | solution.py:96
  13.2 97.9 %all-gather.3.cloned.1.call-start = ((), (), s32[]{:S(2)}) async-start(), calls=%async_computation.3 | async-start | bytes 1179648 | tf_op jit(solution)/shard_map/all_gather | solution.py:105
  62.9 168.7 %reduce-scatter.5.cloned.1.call-start = ((), (), s32[]{:S(2)}) async-start(), calls=%async_computation.4 | async-start | bytes 1179648 | tf_op jit(solution)/shard_map/reduce_scatter | solution.py:96
  124.8 2.0 copy-start.2
  136.5 173.0 %all-gather.5.cloned.1.call-start = ((), (), s32[]{:S(2)}) async-start(), calls=%async_computation.5 | async-start | bytes 1179648 | tf_op jit(solution)/shard_map/all_gather | solution.py:105
  292.5 26.2 %copy-start.1 = (bf16[64,64]{1,0:T(8,128)(2,1)S(1)}, bf16[64,64]{1,0:T(8,128)(2,1)}, u32[]{:S(2)}) copy-start(bf16[64,64]{1,0:T(8,128)(2,1)} %param.7) | copy-start | bytes 24580
Sparse Core Ops, SparseCore 0:
  13.3 38.7 reduce-scatter.2
  63.0 23.4 all-gather.2
  136.6 36.3 reduce-scatter.4
  246.9 24.1 all-gather.4
where the time goes:
time: 328 us; the launch traced here: 325 us
  other arithmetic  86.7 us (26%)
  local copies, waits for them, and re-layouts  85.2 us (26%)
  matrix products  83.7 us (26%)
  blocking collectives  39.8 us (12%)
  waiting for transfers between devices  15.5 us (5%)
  between operations  14 us (4%)
    dot_general x10, matrix products, product(): return jnp.einsum(form, left, right, preferred_element_type=jnp.float32)  51.8 us
    psum x1, blocking collectives, body(): local_grad = lax.psum(local_term, ('dp', 'mp')) * grad_scale  39.8 us
    add x1, other arithmetic, combine(): joined = jnp.concatenate([top_left + low_right, top_right - low_left], -1)  34.2 us
    reshape x2, local copies, waits for them, and re-layouts, body(): local_back.reshape(rows_here, grid_y, columns)  23.4 us
    reshape x2, local copies, waits for them, and re-layouts, body(): local_part.reshape(rows_here, grid_y, columns)  23.3 us
    concatenate x1, other arithmetic, combine(): joined = jnp.concatenate([top_left + low_right, top_right - low_left], -1)  17 us
    reduce_scatter x2, waiting for transfers between devices, to_modes(): lax.psum_scatter(product('ojrx,xrkq->kojq', x_table_own, spectrum).astype...  15.4 us
    unnamed x8, local copies, waits for them, and re-layouts  15.3 us
  transfers between devices with their start and end apart: 4, of which 1 were waited for; matrix products, arithmetic and copies ran while one was open for 58% of the time, Pallas kernels for 0%

commit v1 on v0

v1 whole, which is shorter than its diff:
```python
import functools
import math

import jax
import jax.numpy as jnp
import ml_dtypes
import numpy as np
from jax import lax
from jax.experimental import pallas as pl
from jax.experimental.pallas import tpu as pltpu
from jax.sharding import PartitionSpec as P

NX = 256
NY = 256
KX = 32
KY = 32
F32 = jnp.float32
BF16 = jnp.bfloat16
ROOT = math.sqrt(2.0 / math.pi)
CUBE = 0.044715


def to_bf16(values):
    return values.astype(np.float32).astype(ml_dtypes.bfloat16)


def y_tables(count):
    block = KY // count
    k_index = np.arange(KY)
    angle = 2.0 * math.pi / NY * (k_index[:, None] * np.arange(NY)[None, :] % NY)
    table = to_bf16(np.stack([np.cos(angle), -np.sin(angle)]) / math.sqrt(NY)).astype(np.float32)
    weight = np.where(k_index == 0, 1.0, 2.0)[None, :, None]

    def ordered(values):
        shaped = values.reshape(2, count // 2, 2, block, NY).transpose(2, 1, 0, 3, 4)
        return to_bf16(shaped.reshape(2 * KY, NY))

    return ordered(table), ordered(table * weight)


def x_tables(count):
    block = KY // count
    rows = NX // count
    stored = np.arange(NX)
    x_index = stored % rows * count + stored // rows
    frequency = np.arange(KX) - KX // 2
    angle = 2.0 * math.pi / NX * (frequency[:, None] * x_index[None, :] % NX)
    cosine = np.cos(angle) / math.sqrt(NX)
    sine = np.sin(angle) / math.sqrt(NX)
    table = np.stack([np.stack([cosine, sine], 1), np.stack([-sine, cosine], 1)])
    per = table.reshape(2, KX, 2, count, rows).transpose(3, 0, 1, 4, 2)
    spread = np.einsum("nojxr,ab->noajxrb", per, np.eye(block))
    spread = to_bf16(spread.reshape(count, 2 * block * KX, rows * 2 * block))
    return spread, np.ascontiguousarray(spread.transpose(0, 2, 1))


def dot(left, right):
    return lax.dot_general(left, right, (((1,), (0,)), ((), ())), preferred_element_type=F32)


def dot_nt(left, right):
    return lax.dot_general(left, right, (((1,), (1,)), ((), ())), preferred_element_type=F32)


def whole(shape):
    zeros = (0,) * len(shape)
    return pl.BlockSpec(shape, lambda *_: zeros)


def call(kernel, here, operands, grid, in_specs, out_specs, out_shape, scratch=(), flops=0, moved=0, name=None):
    return pl.pallas_call(
        kernel,
        out_shape=out_shape,
        grid_spec=pltpu.PrefetchScalarGridSpec(
            num_scalar_prefetch=1,
            grid=grid,
            in_specs=in_specs,
            out_specs=out_specs,
            scratch_shapes=list(scratch),
        ),
        compiler_params=pltpu.CompilerParams(
            dimension_semantics=("arbitrary",) * len(grid), vmem_limit_bytes=40 << 20
        ),
        cost_estimate=pl.CostEstimate(flops=flops, bytes_accessed=moved, transcendentals=0),
        name=name,
    )(here, *operands)


def store_spectrum(here, parts, keep_ref, send_ref):
    chips, width, _ = keep_ref.shape
    unit = width // len(parts)
    half = chips * unit
    own_first = here[0] % 2 == 0
    kept = [jnp.where(own_first, part[:half], part[half:]) for part in parts]
    sent = [jnp.where(own_first, part[half:], part[:half]) for part in parts]
    for chip in range(chips):
        rows = slice(chip * unit, (chip + 1) * unit)
        keep_ref[chip] = jnp.concatenate([part[rows] for part in kept], 0).astype(BF16)
        send_ref[chip] = jnp.concatenate([part[rows] for part in sent], 0).astype(BF16)


def forward_y(here, field_ref, table_ref, keep_ref, send_ref):
    table = table_ref[...]
    parts = [dot_nt(table, field_ref[x]) for x in range(field_ref.shape[0])]
    store_spectrum(here, parts, keep_ref, send_ref)


def forward_x(here, keep_ref, got_ref, own_ref, other_ref, *outs):
    chip = here[0] // 2
    for step, out in enumerate(outs):
        at = chip ^ step
        out[...] = (dot(own_ref[0], keep_ref[at]) + dot(other_ref[0], got_ref[at])).astype(BF16)


def total(refs):
    values = [ref[...].astype(F32) for ref in refs]
    while len(values) > 1:
        values = [a + b for a, b in zip(values[::2], values[1::2])]
    return values[0].astype(BF16).astype(F32)


def half_sign(shape):
    lane = lax.broadcasted_iota(jnp.int32, shape, 1)
    return jnp.where(lane % 128 < 64, -1.0, 1.0)


def low_half(shape):
    return lax.broadcasted_iota(jnp.int32, shape, 1) < 64


def mix_forward(count, zs, here, *refs):
    terms, (w_ref, out_ref, spread_ref, coeff, prod) = refs[:count], refs[count:]
    i, jc = pl.program_id(0), pl.program_id(1)
    per = w_ref.shape[2]
    modes = coeff.shape[0] // 2
    first = (i * pl.num_programs(1) + jc) * per

    @pl.when(first == 0)
    def _():
        coeff[...] = total(terms)

    shape = (2 * zs, zs * 64)
    row = lax.broadcasted_iota(jnp.int32, shape, 0)
    keep = lax.broadcasted_iota(jnp.int32, shape, 1) // 64 == row % zs
    is_real = row < zs
    for pair in range(per // 2):
        lefts, weights = [], []
        for sub in range(2):
            at = first + 2 * pair + sub
            real = jnp.broadcast_to(coeff[pl.ds(at, 1), :], shape)
            imag = jnp.broadcast_to(coeff[pl.ds(modes + at, 1), :], shape)
            lefts.append(jnp.where(keep, jnp.where(is_real, real, imag), 0.0))
            weights.append(w_ref[:, 0, 2 * pair + sub].reshape(zs * 64, 128))
        left = jnp.concatenate(lefts, 0).astype(BF16)
        base = pl.multiple_of((first + 2 * pair) * 2 * zs, 4 * zs)
        spread_ref[pl.ds(base, 4 * zs), :] = left
        got = dot(left, jnp.concatenate(weights, 1))
        prod[pl.ds(base, 2 * zs), :] = got[: 2 * zs, :128]
        prod[pl.ds(base + 2 * zs, 2 * zs), :] = got[2 * zs :, 128:]

    @pl.when(first + per == modes)
    def _():
        sign = half_sign((modes, 128))
        low = low_half((modes, 128))
        for tile in range(zs // 2):
            rows = []
            for z in (2 * tile, 2 * tile + 1):
                real = prod[pl.ds(z, modes, stride=2 * zs), :]
                imag = prod[pl.ds(zs + z, modes, stride=2 * zs), :]
                rows.append(real + sign * pltpu.roll(imag, 64, 1))
            lanes = slice(tile * 128, (tile + 1) * 128)
            out_ref[:modes, lanes] = jnp.where(low, rows[0], pltpu.roll(rows[1], 64, 1)).astype(BF16)
            out_ref[modes:, lanes] = jnp.where(low, pltpu.roll(rows[0], 64, 1), rows[1]).astype(BF16)


def mix_backward(count, zs, here, *refs):
    terms, (w_ref, out_ref, pair_ref, prod) = refs[:count], refs[count:]
    i, jc = pl.program_id(0), pl.program_id(1)
    per = w_ref.shape[2]
    modes = prod.shape[1] // (2 * zs)
    first = (i * pl.num_programs(1) + jc) * per

    @pl.when(first == 0)
    def _():
        grad = total(terms)
        sign = half_sign((modes, 128))
        low = low_half((modes, 128))
        for tile in range(zs // 2):
            lanes = slice(tile * 128, (tile + 1) * 128)
            real, imag = grad[:modes, lanes], grad[modes:, lanes]
            even = jnp.where(low, real, pltpu.roll(imag, 64, 1))
            odd = jnp.where(low, pltpu.roll(real, 64, 1), imag)
            for z, value in ((2 * tile, even), (2 * tile + 1, odd)):
                pair_ref[pl.ds(z, modes, stride=2 * zs), :] = value
                pair_ref[pl.ds(zs + z, modes, stride=2 * zs), :] = -sign * pltpu.roll(value, 64, 1)

    for mode in range(per):
        base = pl.multiple_of((first + mode) * 2 * zs, 2 * zs)
        left = pair_ref[pl.ds(base, 2 * zs), :].astype(BF16)
        got = dot_nt(left, w_ref[:, 0, mode].reshape(zs * 64, 128))
        for tile in range(zs // 2):
            prod[tile, pl.ds(base, 2 * zs), :] = got[:, tile * 128 : (tile + 1) * 128]

    @pl.when(first + per == modes)
    def _():
        low = low_half((modes, 128))
        for part in range(2):
            for tile in range(zs // 2):
                at = part * zs + 2 * tile
                even = prod[tile, pl.ds(at, modes, stride=2 * zs), :]
                odd = prod[tile, pl.ds(at + 1, modes, stride=2 * zs), :]
                out_ref[part * modes : (part + 1) * modes, tile * 128 : (tile + 1) * 128] = jnp.where(
                    low, even, odd
                ).astype(BF16)


def gram(zs, here, spread_ref, pair_ref, out_ref):
    i, jc = pl.program_id(0), pl.program_id(1)
    per = out_ref.shape[2]
    group = 4
    unit = 2 * zs
    first = (i * pl.num_programs(1) + jc) * per
    shape = (group * unit, 128)
    owner = lax.broadcasted_iota(jnp.int32, shape, 0) // unit
    for at in range(0, per, group):
        base = pl.multiple_of((first + at) * unit, group * unit)
        left = jnp.transpose(spread_ref[pl.ds(base, group * unit), :].astype(F32)).astype(BF16)
        grad = pair_ref[pl.ds(base, group * unit), :]
        right = jnp.concatenate([jnp.where(owner == t, grad, 0.0) for t in range(group)], 1)
        got = dot(left, right.astype(BF16))
        for t in range(group):
            out_ref[:, 0, at + t] = got[:, t * 128 : (t + 1) * 128].reshape(zs, 64, 128)


def grid_rows(here, blocks, x_ref, rows):
    chips = rows.shape[1]
    core, chip = here[0] % 2, here[0] // 2
    for slot, block in enumerate(blocks):
        at_core = core if slot < chips else 1 - core
        rows[at_core, chip ^ (slot % chips)] = dot(x_ref[0], block[...])


def row_at(rows, count, x):
    cores, chips, height, _ = rows.shape
    per = height // (pl.num_programs(0) * count)
    start = pl.multiple_of(pl.program_id(0) * (count * per), count * per)
    step = [rows[core, chip, pl.ds(start, count * per), :] for core in range(cores) for chip in range(chips)]
    joined = jnp.concatenate([value[x * per : (x + 1) * per] for value in step], 0)
    return jnp.transpose(joined).astype(BF16)


def middle(count, here, *refs):
    blocks, rest = refs[:count], refs[count:]
    x_ref, y_ref, mixing_ref, field_ref, cot_ref = rest[:5]
    out_ref, grad_ref, keep_ref, send_ref, rows = rest[5:]

    @pl.when(pl.program_id(0) == 0)
    def _():
        grid_rows(here, blocks, x_ref, rows)

    table = y_ref[...]
    mixing = mixing_ref[...]
    parts = []
    for x in range(field_ref.shape[0]):
        p = dot(row_at(rows, field_ref.shape[0], x), table) + dot(mixing, field_ref[x])
        square = p * p
        t = jnp.tanh(p * (ROOT + ROOT * CUBE * square))
        half = 0.5 + 0.5 * t
        out_ref[x] = (p * half).astype(BF16)
        slope = half + p * (1.0 - t * t) * (0.5 * ROOT + 1.5 * ROOT * CUBE * square)
        grad = (cot_ref[x].astype(F32) * slope).astype(BF16)
        grad_ref[x] = grad
        parts.append(dot_nt(table, grad))
    store_spectrum(here, parts, keep_ref, send_ref)


def local_sum(here, field_ref, grad_ref, out_ref, acc):
    step = pl.program_id(0)

    @pl.when(step == 0)
    def _():
        acc[...] = jnp.zeros_like(acc)

    got = dot_nt(field_ref[0], grad_ref[0])
    for x in range(1, field_ref.shape[0]):
        got += dot_nt(field_ref[x], grad_ref[x])
    acc[...] += got

    @pl.when(step == pl.num_programs(0) - 1)
    def _():
        value = acc[...]
        parts = [value[at : at + 64, at : at + 64] for at in range(0, value.shape[0], 64)]
        while len(parts) > 1:
            parts = [a + b for a, b in zip(parts[::2], parts[1::2])]
        out_ref[...] = parts[0]


def last(count, here, *refs):
    blocks, rest = refs[:count], refs[count:]
    x_ref, y_ref, mixing_ref, grad_ref, out_ref, rows = rest

    @pl.when(pl.program_id(0) == 0)
    def _():
        grid_rows(here, blocks, x_ref, rows)

    table = y_ref[...]
    mixing = mixing_ref[...]
    for x in range(grad_ref.shape[0]):
        value = dot(row_at(rows, grad_ref.shape[0], x), table) + dot(mixing, grad_ref[x])
        out_ref[x] = value.astype(BF16)


def flip(axis, size, bit):
    return functools.partial(lax.ppermute, axis_name=axis, perm=[(at, at ^ bit) for at in range(size)])


def exchange_sum(value, axis, size):
    parts = [value] + [flip(axis, size, bit)(value) for bit in range(1, size)]
    while len(parts) > 1:
        parts = [a + b for a, b in zip(parts[::2], parts[1::2])]
    return parts[0]


def body(features, out_grad, spectral_weight, local_weight):
    count = lax.axis_size("mp")
    dp_count = lax.axis_size("dp")
    chips = count // 2
    rows_here, grid_y, snaps, zs, channels = features.shape
    mode_rows = spectral_weight.shape[1]
    columns = snaps * zs * channels
    modes = mode_rows * KX
    unit = 2 * mode_rows
    here = lax.axis_index("mp").astype(jnp.int32).reshape(1)

    y_plain, y_weighted = y_tables(count)
    x_forward, x_back = x_tables(count)

    def inner(array):
        return jnp.transpose(array, (0, 2, 3, 4, 1)).reshape(rows_here, columns, grid_y)

    def outer(array):
        shaped = array.reshape(rows_here, snaps, zs, channels, grid_y)
        return jnp.transpose(shaped, (0, 4, 1, 2, 3))

    field, cot = inner(features), inner(out_grad)
    eye = jnp.eye(snaps * zs, dtype=BF16)
    mixing = jnp.kron(eye, local_weight)
    mixing_t = jnp.kron(eye, local_weight.T)

    chunk = 4
    steps = rows_here // chunk
    field_spec = pl.BlockSpec((chunk, columns, grid_y), lambda g, _: (g, 0, 0))
    field_shape = jax.ShapeDtypeStruct((rows_here, columns, grid_y), BF16)
    half_spec = pl.BlockSpec((chips, chunk * unit, columns), lambda g, _: (0, g, 0))
    half_shape = jax.ShapeDtypeStruct((chips, rows_here * unit, columns), BF16)
    y_spec = whole((2 * KY, grid_y))
    mode_shape = jax.ShapeDtypeStruct((2 * modes, columns), BF16)
    mode_spec = whole((2 * modes, columns))
    mixing_spec = whole((columns, columns))
    field_bytes = rows_here * columns * grid_y * 2
    mode_bytes = 4 * modes * columns

    def to_chips(keep, send):
        got = flip("mp", count, 1)(send)
        x_spec = (1, 2 * modes, rows_here * unit)
        outs = call(
            forward_x,
            here,
            (keep, got, x_forward, x_forward),
            (1,),
            [
                whole(keep.shape),
                whole(keep.shape),
                pl.BlockSpec(x_spec, lambda g, m: (m[0], 0, 0)),
                pl.BlockSpec(x_spec, lambda g, m: (m[0] ^ 1, 0, 0)),
            ],
            [mode_spec] * chips,
            [mode_shape] * chips,
            flops=8 * chips * modes * rows_here * unit * columns,
            moved=mode_bytes * 3 * chips,
            name="forward_x",
        )
        return [outs[0]] + [flip("mp", count, 2 * bit)(outs[bit]) for bit in range(1, chips)]

    def to_all(block):
        mine = [block] + [flip("mp", count, 2 * bit)(block) for bit in range(1, chips)]
        return mine + [flip("mp", count, 1)(value) for value in mine]

    per = 8
    mode_grid = (mode_rows, KX // per)
    weight_spec = pl.BlockSpec((zs, 1, per, channels, 2 * channels), lambda i, j, _: (0, i, j, 0, 0))
    spread_shape = (modes * 2 * zs, columns)
    pair_shape = (modes * 2 * zs, 2 * channels)
    weight_bytes = zs * modes * channels * 2 * channels * 2

    keep, send = call(
        forward_y,
        here,
        (field, y_plain),
        (steps,),
        [field_spec, y_spec],
        [half_spec] * 2,
        [half_shape] * 2,
        flops=field_bytes * 2 * KY,
        moved=field_bytes + mode_bytes * count,
        name="forward_y",
    )
    terms = to_chips(keep, send)
    mixed, spread = call(
        functools.partial(mix_forward, chips, zs),
        here,
        (*terms, spectral_weight),
        mode_grid,
        [mode_spec] * chips + [weight_spec],
        [mode_spec, whole(spread_shape)],
        [mode_shape, jax.ShapeDtypeStruct(spread_shape, BF16)],
        [pltpu.VMEM((2 * modes, columns), F32), pltpu.VMEM(pair_shape, F32)],
        flops=weight_bytes * 8,
        moved=weight_bytes + mode_bytes * chips,
        name="mix_forward",
    )
    blocks = to_all(mixed)
    x_back_spec = pl.BlockSpec((1, rows_here * unit, 2 * modes), lambda g, m: (m[0], 0, 0))
    rows_scratch = pltpu.VMEM((2, chips, rows_here * unit, columns), F32)
    output, preact_grad, keep, send = call(
        functools.partial(middle, count),
        here,
        (*blocks, x_back, y_weighted, mixing_t, field, cot),
        (steps,),
        [mode_spec] * count + [x_back_spec, y_spec, mixing_spec, field_spec, field_spec],
        [field_spec, field_spec, half_spec, half_spec],
        [field_shape, field_shape, half_shape, half_shape],
        [rows_scratch],
        flops=field_bytes * (4 * KY + columns),
        moved=field_bytes * 4 + mode_bytes * count * 2,
        name="middle",
    )
    terms = to_chips(keep, send)
    local_term = call(
        local_sum,
        here,
        (field, preact_grad),
        (steps,),
        [field_spec] * 2,
        whole((channels, channels)),
        jax.ShapeDtypeStruct((channels, channels), F32),
        [pltpu.VMEM((columns, columns), F32)],
        flops=field_bytes * columns,
        moved=field_bytes * 2,
        name="local_sum",
    )
    back, pairs = call(
        functools.partial(mix_backward, chips, zs),
        here,
        (*terms, spectral_weight),
        mode_grid,
        [mode_spec] * chips + [weight_spec],
        [mode_spec, whole(pair_shape)],
        [mode_shape, jax.ShapeDtypeStruct(pair_shape, F32)],
        [pltpu.VMEM((zs // 2, modes * 2 * zs, 128), F32)],
        flops=weight_bytes * 8,
        moved=weight_bytes + mode_bytes * chips,
        name="mix_backward",
    )
    blocks = to_all(back)
    spectral_grad = call(
        functools.partial(gram, zs),
        here,
        (spread, pairs),
        mode_grid,
        [whole(spread_shape), whole(pair_shape)],
        weight_spec,
        jax.ShapeDtypeStruct(spectral_weight.shape, F32),
        flops=weight_bytes * 8,
        moved=weight_bytes * 2,
        name="gram",
    )
    grad_scale = 1.0 / math.sqrt(NX * NY * snaps * dp_count * zs)
    local_grad = exchange_sum(exchange_sum(local_term, "mp", count), "dp", dp_count) * grad_scale
    back_field = call(
        functools.partial(last, count),
        here,
        (*blocks, x_back, y_plain, mixing, preact_grad),
        (steps,),
        [mode_spec] * count + [x_back_spec, y_spec, mixing_spec, field_spec],
        field_spec,
        field_shape,
        [rows_scratch],
        flops=field_bytes * (2 * KY + columns),
        moved=field_bytes * 2 + mode_bytes * count,
        name="last",
    )
    return (outer(output), outer(back_field), spectral_grad, local_grad)


def solution(mesh):
    placed = (
        P("mp", None, None, "dp", None),
        P("mp", None, None, "dp", None),
        P("dp", "mp", None, None, None),
        P(),
    )
    return jax.shard_map(
        body,
        mesh=mesh,
        in_specs=placed,
        out_specs=(
            P("mp", None, None, "dp", None),
            P("mp", None, None, "dp", None),
            P("dp", "mp", None, None, None),
            P(),
        ),
        check_vma=False,
    )
```

time: 328 us -> 116 us (0.35)
  other arithmetic: 86.7 us -> 1.61 us
  matrix products: 83.7 us -> 0 us
  local copies, waits for them, and re-layouts: 85.2 us -> 17.3 us
  Pallas kernels: 0 us -> 48.1 us
  blocking collectives: 39.8 us -> 0 us
  starting transfers between devices: 0.34 us -> 26.7 us
  between operations: 14 us -> 0.86 us
  waiting for transfers between devices: 15.5 us -> 21.2 us
    dot_general x13 -> x0, matrix products: 83.7 us -> none  [the longest x10 51.8 us: product(): return jnp.einsum(form, left, right, preferred_element_type=jnp.float32)]
    reshape x15 -> x0, local copies, waits for them, and re-layouts: 62.8 us -> none  [the longest x2 23.4 us: body(): local_back.reshape(rows_here, grid_y, columns)]
    pallas_call x0 -> x9, Pallas kernels: none -> 48.1 us  [call(): pl.pallas_call(kernel, out_shape=out_shape, grid_spec=pltpu.PrefetchScala...]
    psum x1 -> x0, blocking collectives: 39.8 us -> none  [body(): local_grad = lax.psum(local_term, ('dp', 'mp')) * grad_scale]
    add x2 -> x1, other arithmetic: 34.2 us -> 0.02 us  [exchange_sum(): parts = [a + b for a, b in zip(parts[::2], parts[1::2])]]
    concatenate x2 -> x0, other arithmetic: 31.4 us -> none  [the longest x1 17 us: combine(): joined = jnp.concatenate([top_left + low_right, top_right - low_left], -1)]
    ppermute x0 -> x32, starting transfers between devices: none -> 26.7 us  [the longest x10 9.56 us: exchange_sum(): parts = [value] + [flip(axis, size, bit)(value) for bit in range(1, size)]]
    ppermute x0 -> x32, waiting for transfers between devices: none -> 21.2 us  [the longest x10 6.86 us: exchange_sum(): parts = [value] + [flip(axis, size, bit)(value) for bit in range(1, size)]]
  transfers between devices with their start and end apart: 4 -> 32, of which waited for: 1 -> 12; matrix products, arithmetic and copies ran while one was open for 58% -> 3% of each run, Pallas kernels for 0% -> 16%
where the time goes in v1:
time: 116 us
  Pallas kernels  48.1 us (41%)
  starting transfers between devices  26.7 us (23%)
  waiting for transfers between devices  21.2 us (18%)
  local copies, waits for them, and re-layouts  17.3 us (15%)
  other arithmetic  1.61 us (1%)
    pallas_call x9, Pallas kernels, call(): pl.pallas_call(kernel, out_shape=out_shape, grid_spec=pltpu.PrefetchScala...  48.1 us
    unnamed x38, local copies, waits for them, and re-layouts  15.8 us
    ppermute x10, starting transfers between devices, exchange_sum(): parts = [value] + [flip(axis, size, bit)(value) for bit in range(1, size)]  9.56 us
    ppermute x6, starting transfers between devices, to_chips(): flip('mp', count, 2 * bit)(outs[bit])  8.02 us
    ppermute x6, starting transfers between devices, to_all(): flip('mp', count, 2 * bit)(block)  7.04 us
    ppermute x10, waiting for transfers between devices, exchange_sum(): parts = [value] + [flip(axis, size, bit)(value) for bit in range(1, size)]  6.86 us
    ppermute x6, waiting for transfers between devices, to_chips(): flip('mp', count, 2 * bit)(outs[bit])  6.54 us
    ppermute x6, waiting for transfers between devices, to_all(): flip('mp', count, 2 * bit)(block)  4.58 us
  transfers between devices with their start and end apart: 32, of which 12 were waited for; matrix products, arithmetic and copies ran while one was open for 3% of the time, Pallas kernels for 16%

profile of v1, /device:TPU:0, one launch (start us, length us, event | category | flops | bytes accessed | tf_op | source)
XLA Modules:
  0.0 115.8 jit_solution(12018835490122024759)
XLA Ops:
  0.6 2.2 %copy-done = bf16[32,256,1,4,64]{1,4,3,2,0:T(8,128)(2,1)S(1)} copy-done((bf16[32,256,1,4,64]{1,4,3,2,0:T(8,128)(2,1)S(1)}, bf16[32,256,1,4,64]{1,4,3,2,0:T(8,128)(2,1)}, u32[]{:S(2)}) %copy-start) | copy-done | bytes 4194328
  2.8 0.8 copy-done.13
  3.6 2.4 %forward_y.1 = (bf16[4,256,256]{2,1,0:T(8,128)(2,1)S(1)}, bf16[4,256,256]{2,1,0:T(8,128)(2,1)S(1)}) custom-call(s32[1]{0:T(128)} %bitcast.here, bf16[32,256,256]{2,1,0:T(8,128)(2,1)S(1)} %bitcast.18, bf16[64,256]{1,0:T(8,128)(2,1)S(1)} %copy-done.13), custom_call_target="tpu_custom_call" | custom-call | flops 268435456 | bytes 5242880 | tf_op jit(solution)/shard_map/forward_y/pallas_call | solution.py:71
  6.0 0.5 collective-permute-start
  6.5 1.5 %collective-permute-done.got_ref = bf16[4,256,256]{2,1,0:T(8,128)(2,1)S(1)} collective-permute-done((bf16[4,256,256]{2,1,0:T(8,128)(2,1)S(1)}, bf16[4,256,256]{2,1,0:T(8,128)(2,1)S(1)}, u32[]{:S(2)}, u32[]{:S(2)}) %collective-permute-start) | collective-permute-done | bytes 524320 | tf_op jit(solution)/shard_map/ppermute | solution.py:364
  8.5 2.9 %collective-permute-start.1 = (bf16[256,256]{1,0:T(8,128)(2,1)S(1)}, bf16[256,256]{1,0:T(8,128)(2,1)S(1)}, u32[]{:S(2)}, u32[]{:S(2)}) collective-permute-start(bf16[256,256]{1,0:T(8,128)(2,1)S(1)} %get-tuple-element.25), channel_id=1, source_target_pairs={{0,2},{1,3},{2,0},{3,1},{4,6},{5,7},{6,4},{7,5},{8,10},{9,11},{10,... | collective-permute-start | bytes 393224 | tf_op jit(solution)/shard_map/ppermute | solution.py:383
  11.5 1.5 %collective-permute-start.2 = (bf16[256,256]{1,0:T(8,128)(2,1)S(1)}, bf16[256,256]{1,0:T(8,128)(2,1)S(1)}, u32[]{:S(2)}, u32[]{:S(2)}) collective-permute-start(bf16[256,256]{1,0:T(8,128)(2,1)S(1)} %get-tuple-element.26), channel_id=1, source_target_pairs={{0,4},{1,5},{2,6},{3,7},{4,0},{5,1},{6,2},{7,3},{8,12},{9,13},{10,... | collective-permute-start | bytes 393224 | tf_op jit(solution)/shard_map/ppermute | solution.py:383
  13.0 2.4 %collective-permute-done.1.refs_1_ = bf16[256,256]{1,0:T(8,128)(2,1)S(1)} collective-permute-done((bf16[256,256]{1,0:T(8,128)(2,1)S(1)}, bf16[256,256]{1,0:T(8,128)(2,1)S(1)}, u32[]{:S(2)}, u32[]{:S(2)}) %collective-permute-start.1) | collective-permute-done | bytes 131104 | tf_op jit(solution)/shard_map/ppermute | solution.py:383
  15.4 4.2 %collective-permute-done.2.refs_2_ = bf16[256,256]{1,0:T(8,128)(2,1)S(1)} collective-permute-done((bf16[256,256]{1,0:T(8,128)(2,1)S(1)}, bf16[256,256]{1,0:T(8,128)(2,1)S(1)}, u32[]{:S(2)}, u32[]{:S(2)}) %collective-permute-start.2) | collective-permute-done | bytes 131104 | tf_op jit(solution)/shard_map/ppermute | solution.py:383
  19.5 3.4 %copy-done.3 = bf16[4,4,32,64,128]{4,3,2,1,0:T(8,128)(2,1)S(1)} copy-done((bf16[4,4,32,64,128]{4,3,2,1,0:T(8,128)(2,1)S(1)}, bf16[4,4,32,64,128]{4,3,2,1,0:T(8,128)(2,1)}, u32[]{:S(2)}) %copy-start.3) | copy-done | bytes 8388632
  22.9 4.0 %mix_forward.1 = (bf16[256,256]{1,0:T(8,128)(2,1)S(1)}, bf16[1024,256]{1,0:T(8,128)(2,1)S(1)}) custom-call(s32[1]{0:T(128)} %bitcast.here, bf16[256,256]{1,0:T(8,128)(2,1)S(1)} %get-tuple-element.24.refs_0_, bf16[256,256]{1,0:T(8,128)(2,1)S(1)} %collective-permute-done.1.refs_1_, bf16[256,256]{1,0:T(8,128)(2,1)S(1)} %collective-permute-done.2.refs_2_, ...), custom_call_target="tpu_custom_call" | custom-call | flops 67108864 | bytes 8912896 | tf_op jit(solution)/shard_map/mix_forward/pallas_call | solution.py:71
  26.9 1.6 %collective-permute-start.6 = (bf16[256,256]{1,0:T(8,128)(2,1)S(1)}, bf16[256,256]{1,0:T(8,128)(2,1)S(1)}, u32[]{:S(2)}, u32[]{:S(2)}) collective-permute-start(bf16[256,256]{1,0:T(8,128)(2,1)S(1)} %get-tuple-element.28.refs_0_), channel_id=1, source_target_pairs={{0,6},{1,7},{2,4},{3,5},{4,2},{5,3},{6,0},{7,1},{8,14},{9,15},{10,... | collective-permute-start | bytes 393224 | tf_op jit(solution)/shard_map/ppermute | solution.py:386
  28.5 1.2 %collective-permute-start.5 = (bf16[256,256]{1,0:T(8,128)(2,1)S(1)}, bf16[256,256]{1,0:T(8,128)(2,1)S(1)}, u32[]{:S(2)}, u32[]{:S(2)}) collective-permute-start(bf16[256,256]{1,0:T(8,128)(2,1)S(1)} %get-tuple-element.28.refs_0_), channel_id=1, source_target_pairs={{0,4},{1,5},{2,6},{3,7},{4,0},{5,1},{6,2},{7,3},{8,12},{9,13},{10,... | collective-permute-start | bytes 393224 | tf_op jit(solution)/shard_map/ppermute | solution.py:386
  29.7 0.8 collective-permute-start.4
  30.6 3.2 %collective-permute-done.6.refs_3_ = bf16[256,256]{1,0:T(8,128)(2,1)S(1)} collective-permute-done((bf16[256,256]{1,0:T(8,128)(2,1)S(1)}, bf16[256,256]{1,0:T(8,128)(2,1)S(1)}, u32[]{:S(2)}, u32[]{:S(2)}) %collective-permute-start.6) | collective-permute-done | bytes 131104 | tf_op jit(solution)/shard_map/ppermute | solution.py:386
  33.8 1.1 collective-permute-done.5.refs_2_
  35.5 1.0 broadcast_multiply_fusion
  36.7 2.2 %copy-done.1 = bf16[32,256,1,4,64]{1,4,3,2,0:T(8,128)(2,1)S(1)} copy-done((bf16[32,256,1,4,64]{1,4,3,2,0:T(8,128)(2,1)S(1)}, bf16[32,256,1,4,64]{1,4,3,2,0:T(8,128)(2,1)}, u32[]{:S(2)}) %copy-start.1) | copy-done | bytes 4194328
  38.9 16.2 %middle.1 = (bf16[32,256,256]{2,1,0:T(8,128)(2,1)}, bf16[32,256,256]{2,1,0:T(8,128)(2,1)S(1)}, bf16[4,256,256]{2,1,0:T(8,128)(2,1)S(1)}, bf16[4,256,256]{2,1,0:T(8,128)(2,1)S(1)}) custom-call(s32[1]{0:T(128)} %bitcast.here, bf16[256,256]{1,0:T(8,128)(2,1)S(1)} %get-tuple-element.28.refs_0_, bf16[256,256]{1,0:T(8,128)(2,1)S(1)} %collective-permute-done.4.refs_1_, ...), custom_call_target="tpu_custom_call" | custom-call | flops 1610612736 | bytes 18874368 | tf_op jit(solution)/shard_map/middle/pallas_call | solution.py:71
  55.1 2.0 %copy-done.4 = bf16[32,256,256]{2,1,0:T(8,128)(2,1)} copy-done((bf16[32,256,256]{2,1,0:T(8,128)(2,1)}, bf16[32,256,256]{2,1,0:T(8,128)(2,1)S(1)}, u32[]{:S(2)}) %copy-start.4) | copy-done | bytes 4194328
  57.3 1.6 %collective-permute-done.11.got_ref = bf16[4,256,256]{2,1,0:T(8,128)(2,1)S(1)} collective-permute-done((bf16[4,256,256]{2,1,0:T(8,128)(2,1)S(1)}, bf16[4,256,256]{2,1,0:T(8,128)(2,1)S(1)}, u32[]{:S(2)}, u32[]{:S(2)}) %collective-permute-start.11) | collective-permute-done | bytes 524320 | tf_op jit(solution)/shard_map/ppermute | solution.py:364
  59.0 1.2 %copy-done.8 = bf16[8,256,256]{2,1,0:T(8,128)(2,1)S(1)} copy-done((bf16[8,256,256]{2,1,0:T(8,128)(2,1)S(1)}, bf16[8,256,256]{2,1,0:T(8,128)(2,1)}, u32[]{:S(2)}) %copy-start.8) | copy-done | bytes 1048600
  60.7 1.7 %collective-permute-start.12 = (bf16[256,256]{1,0:T(8,128)(2,1)S(1)}, bf16[256,256]{1,0:T(8,128)(2,1)S(1)}, u32[]{:S(2)}, u32[]{:S(2)}) collective-permute-start(bf16[256,256]{1,0:T(8,128)(2,1)S(1)} %get-tuple-element.33), channel_id=1, source_target_pairs={{0,2},{1,3},{2,0},{3,1},{4,6},{5,7},{6,4},{7,5},{8,10},{9,11},{10,... | collective-permute-start | bytes 393224 | tf_op jit(solution)/shard_map/ppermute | solution.py:383
  62.4 0.6 collective-permute-start.13
  63.0 1.3 %collective-permute-start.14 = (bf16[256,256]{1,0:T(8,128)(2,1)S(1)}, bf16[256,256]{1,0:T(8,128)(2,1)S(1)}, u32[]{:S(2)}, u32[]{:S(2)}) collective-permute-start(bf16[256,256]{1,0:T(8,128)(2,1)S(1)} %get-tuple-element.35), channel_id=1, source_target_pairs={{0,6},{1,7},{2,4},{3,5},{4,2},{5,3},{6,0},{7,1},{8,14},{9,15},{10,... | collective-permute-start | bytes 393224 | tf_op jit(solution)/shard_map/ppermute | solution.py:383
  64.2 2.2 %copy-done.5 = bf16[32,256,256]{2,1,0:T(8,128)(2,1)S(1)} copy-done((bf16[32,256,256]{2,1,0:T(8,128)(2,1)S(1)}, bf16[32,256,256]{2,1,0:T(8,128)(2,1)}, u32[]{:S(2)}) %copy-start.5) | copy-done | bytes 4194328
  66.4 2.9 %local_sum.1 = f32[64,64]{1,0:T(8,128)S(1)} custom-call(s32[1]{0:T(128)} %bitcast.here, bf16[32,256,256]{2,1,0:T(8,128)(2,1)S(1)} %bitcast.20, bf16[32,256,256]{2,1,0:T(8,128)(2,1)S(1)} %copy-done.5), custom_call_target="tpu_custom_call" | custom-call | flops 1073741824 | bytes 8388608 | tf_op jit(solution)/shard_map/local_sum/pallas_call | solution.py:71
  69.3 0.6 collective-permute-start.28
  69.9 1.4 %collective-permute-start.27 = (f32[64,64]{1,0:T(8,128)S(1)}, f32[64,64]{1,0:T(8,128)S(1)}, u32[]{:S(2)}, u32[]{:S(2)}) collective-permute-start(f32[64,64]{1,0:T(8,128)S(1)} %local_sum.1), channel_id=1, source_target_pairs={{0,6},{1,7},{2,4},{3,5},{4,2},{5,3},{6,0},{7,1},{8,14},{9,15},{10,... | collective-permute-start | bytes 49160 | tf_op jit(solution)/shard_map/ppermute | solution.py:318
  71.3 2.3 %collective-permute-done.28 = f32[64,64]{1,0:T(8,128)S(1)} collective-permute-done((f32[64,64]{1,0:T(8,128)S(1)}, f32[64,64]{1,0:T(8,128)S(1)}, u32[]{:S(2)}, u32[]{:S(2)}) %collective-permute-start.28) | collective-permute-done | bytes 16416 | tf_op jit(solution)/shard_map/ppermute | solution.py:318
  73.6 0.5 collective-permute-start.26
  74.1 0.7 collective-permute-done.27
  74.8 1.5 %collective-permute-start.25 = (f32[64,64]{1,0:T(8,128)S(1)}, f32[64,64]{1,0:T(8,128)S(1)}, u32[]{:S(2)}, u32[]{:S(2)}) collective-permute-start(f32[64,64]{1,0:T(8,128)S(1)} %local_sum.1), channel_id=1, source_target_pairs={{0,4},{1,5},{2,6},{3,7},{4,0},{5,1},{6,2},{7,3},{8,12},{9,13},{10,... | collective-permute-start | bytes 49160 | tf_op jit(solution)/shard_map/ppermute | solution.py:318
  76.7 1.0 collective-permute-start.23
  78.2 5.0 %mix_backward.1 = (bf16[256,256]{1,0:T(8,128)(2,1)S(1)}, f32[1024,128]{1,0:T(8,128)S(1)}) custom-call(s32[1]{0:T(128)} %bitcast.here, bf16[256,256]{1,0:T(8,128)(2,1)S(1)} %get-tuple-element.32.refs_0_, bf16[256,256]{1,0:T(8,128)(2,1)S(1)} %collective-permute-done.12.refs_1_, bf16[256,256]{1,0:T(8,128)(2,1)S(1)} %collective-permute-done.13.refs_2_, ...), custom_call_target="tpu_custom_call" | custom-call | flops 67108864 | bytes 8912896 | tf_op jit(solution)/shard_map/mix_backward/pallas_call | solution.py:71
  83.2 0.8 copy-done.11
  84.0 1.4 %collective-permute-start.17 = (bf16[256,256]{1,0:T(8,128)(2,1)S(1)}, bf16[256,256]{1,0:T(8,128)(2,1)S(1)}, u32[]{:S(2)}, u32[]{:S(2)}) collective-permute-start(bf16[256,256]{1,0:T(8,128)(2,1)S(1)} %get-tuple-element.36.refs_0_), channel_id=1, source_target_pairs={{0,6},{1,7},{2,4},{3,5},{4,2},{5,3},{6,0},{7,1},{8,14},{9,15},{10,... | collective-permute-start | bytes 393224 | tf_op jit(solution)/shard_map/ppermute | solution.py:386
  85.4 0.7 collective-permute-start.16
  86.1 1.4 %collective-permute-start.15 = (bf16[256,256]{1,0:T(8,128)(2,1)S(1)}, bf16[256,256]{1,0:T(8,128)(2,1)S(1)}, u32[]{:S(2)}, u32[]{:S(2)}) collective-permute-start(bf16[256,256]{1,0:T(8,128)(2,1)S(1)} %get-tuple-element.36.refs_0_), channel_id=1, source_target_pairs={{0,2},{1,3},{2,0},{3,1},{4,6},{5,7},{6,4},{7,5},{8,10},{9,11},{10,... | collective-permute-start | bytes 393224 | tf_op jit(solution)/shard_map/ppermute | solution.py:386
  87.5 3.7 %collective-permute-start.31 = (f32[64,64]{1,0:T(8,128)S(1)}, f32[64,64]{1,0:T(8,128)S(1)}, u32[]{:S(2)}, u32[]{:S(2)}) collective-permute-start(f32[64,64]{1,0:T(8,128)S(1)} %add_add_fusion), channel_id=1, source_target_pairs={{0,24},{8,16},{16,8},{24,0},{1,25},{9,17},{17,9},{25,1},{2,26},{10... | collective-permute-start | bytes 49160 | tf_op jit(solution)/shard_map/ppermute | solution.py:318
  91.2 2.2 %collective-permute-done.31 = f32[64,64]{1,0:T(8,128)S(1)} collective-permute-done((f32[64,64]{1,0:T(8,128)S(1)}, f32[64,64]{1,0:T(8,128)S(1)}, u32[]{:S(2)}, u32[]{:S(2)}) %collective-permute-start.31) | collective-permute-done | bytes 16416 | tf_op jit(solution)/shard_map/ppermute | solution.py:318
  93.4 1.2 %mul.53.refs_10_ = bf16[256,256]{1,0:T(8,128)(2,1)S(1)} reshape(bf16[4,64,4,64]{3,2,1,0:T(4,128)(2,1)} %get-tuple-element.40) | data formatting | bytes 262144 | tf_op jit(solution)/shard_map/jit(kron)/mul | solution.py:347
  94.5 1.4 %collective-permute-done.30 = f32[64,64]{1,0:T(8,128)S(1)} collective-permute-done((f32[64,64]{1,0:T(8,128)S(1)}, f32[64,64]{1,0:T(8,128)S(1)}, u32[]{:S(2)}, u32[]{:S(2)}) %collective-permute-start.30) | collective-permute-done | bytes 16416 | tf_op jit(solution)/shard_map/ppermute | solution.py:318
  96.0 0.5 collective-permute-start.21
  97.3 0.6 add_multiply_fusion
  97.9 1.0 copy-done.12
  98.9 10.9 %gram.1 = f32[4,4,32,64,128]{4,3,2,1,0:T(8,128)} custom-call(s32[1]{0:T(128)} %bitcast.here, bf16[1024,256]{1,0:T(8,128)(2,1)S(1)} %get-tuple-element.38.spread_ref, f32[1024,128]{1,0:T(8,128)S(1)} %copy-done.12), custom_call_target="tpu_custom_call" | custom-call | flops 67108864 | bytes 16777216 | tf_op jit(solution)/shard_map/gram/pallas_call | solution.py:71
  109.9 5.9 %last.1 = bf16[32,256,256]{2,1,0:T(8,128)(2,1)} custom-call(s32[1]{0:T(128)} %bitcast.here, bf16[256,256]{1,0:T(8,128)(2,1)S(1)} %get-tuple-element.36.refs_0_, bf16[256,256]{1,0:T(8,128)(2,1)S(1)} %collective-permute-done.15.refs_1_, bf16[256,256]{1,0:T(8,128)(2,1)S(1)} %collective-permute-done.16.refs_2_, ...), custom_call_target="tpu_custom_call" | custom-call | flops 1342177280 | bytes 9437184 | tf_op jit(solution)/shard_map/last/pallas_call | solution.py:71
  (71 shorter events, 3.8 us)
Async XLA Ops:
  0.6 2.2 %copy-start = (bf16[32,256,1,4,64]{1,4,3,2,0:T(8,128)(2,1)S(1)}, bf16[32,256,1,4,64]{1,4,3,2,0:T(8,128)(2,1)}, u32[]{:S(2)}) copy-start(bf16[32,256,1,4,64]{1,4,3,2,0:T(8,128)(2,1)} %param.8) | copy-start | bytes 12582916
  3.6 4.5 %copy-start.7 = (bf16[8,256,256]{2,1,0:T(8,128)(2,1)S(1)}, bf16[8,256,256]{2,1,0:T(8,128)(2,1)}, u32[]{:S(2)}) copy-start(bf16[8,256,256]{2,1,0:T(8,128)(2,1)} %constant.15.clone.own_ref.other_ref) | copy-start | bytes 3145732
  6.0 2.1 %collective-permute-start = (bf16[4,256,256]{2,1,0:T(8,128)(2,1)S(1)}, bf16[4,256,256]{2,1,0:T(8,128)(2,1)S(1)}, u32[]{:S(2)}, u32[]{:S(2)}) collective-permute-start(bf16[4,256,256]{2,1,0:T(8,128)(2,1)S(1)} %get-tuple-element.23), channel_id=1, source_target_pairs={{0,1},{1,0},{2,3},{3,2},{4,5},{5,4},{6,7},{7,6},{8,9},{9,8},{10,11... | collective-permute-start | bytes 1572872 | tf_op jit(solution)/shard_map/ppermute | solution.py:364
  8.5 6.8 %collective-permute-start.1 = (bf16[256,256]{1,0:T(8,128)(2,1)S(1)}, bf16[256,256]{1,0:T(8,128)(2,1)S(1)}, u32[]{:S(2)}, u32[]{:S(2)}) collective-permute-start(bf16[256,256]{1,0:T(8,128)(2,1)S(1)} %get-tuple-element.25), channel_id=1, source_target_pairs={{0,2},{1,3},{2,0},{3,1},{4,6},{5,7},{6,4},{7,5},{8,10},{9,11},{10,... | collective-permute-start | bytes 393224 | tf_op jit(solution)/shard_map/ppermute | solution.py:383
  11.5 8.1 %collective-permute-start.2 = (bf16[256,256]{1,0:T(8,128)(2,1)S(1)}, bf16[256,256]{1,0:T(8,128)(2,1)S(1)}, u32[]{:S(2)}, u32[]{:S(2)}) collective-permute-start(bf16[256,256]{1,0:T(8,128)(2,1)S(1)} %get-tuple-element.26), channel_id=1, source_target_pairs={{0,4},{1,5},{2,6},{3,7},{4,0},{5,1},{6,2},{7,3},{8,12},{9,13},{10,... | collective-permute-start | bytes 393224 | tf_op jit(solution)/shard_map/ppermute | solution.py:383
  13.0 6.6 %collective-permute-start.3 = (bf16[256,256]{1,0:T(8,128)(2,1)S(1)}, bf16[256,256]{1,0:T(8,128)(2,1)S(1)}, u32[]{:S(2)}, u32[]{:S(2)}) collective-permute-start(bf16[256,256]{1,0:T(8,128)(2,1)S(1)} %get-tuple-element.27), channel_id=1, source_target_pairs={{0,6},{1,7},{2,4},{3,5},{4,2},{5,3},{6,0},{7,1},{8,14},{9,15},{10,... | collective-permute-start | bytes 393224 | tf_op jit(solution)/shard_map/ppermute | solution.py:383
  19.5 3.4 %copy-start.3 = (bf16[4,4,32,64,128]{4,3,2,1,0:T(8,128)(2,1)S(1)}, bf16[4,4,32,64,128]{4,3,2,1,0:T(8,128)(2,1)}, u32[]{:S(2)}) copy-start(bf16[4,4,32,64,128]{4,3,2,1,0:T(8,128)(2,1)} %refs_4_.3) | copy-start | bytes 25165828
  22.9 7.5 %copy-start.16 = (bf16[64,64]{1,0:T(8,128)(2,1)S(1)}, bf16[64,64]{1,0:T(8,128)(2,1)}, u32[]{:S(2)}) copy-start(bf16[64,64]{1,0:T(8,128)(2,1)} %param.11) | copy-start | bytes 24580
  22.9 13.8 %copy-start.9 = (bf16[8,256,256]{2,1,0:T(8,128)(2,1)S(1)}, bf16[8,256,256]{2,1,0:T(8,128)(2,1)}, u32[]{:S(2)}) copy-start(bf16[8,256,256]{2,1,0:T(8,128)(2,1)} %constant.16.clone.refs_8_) | copy-start | bytes 3145732
  22.9 13.8 %copy-start.15 = (bf16[64,256]{1,0:T(8,128)(2,1)S(1)}, bf16[64,256]{1,0:T(8,128)(2,1)}, u32[]{:S(2)}) copy-start(bf16[64,256]{1,0:T(8,128)(2,1)} %constant.17.clone.refs_9_) | copy-start | bytes 98308
  26.9 6.9 %collective-permute-start.6 = (bf16[256,256]{1,0:T(8,128)(2,1)S(1)}, bf16[256,256]{1,0:T(8,128)(2,1)S(1)}, u32[]{:S(2)}, u32[]{:S(2)}) collective-permute-start(bf16[256,256]{1,0:T(8,128)(2,1)S(1)} %get-tuple-element.28.refs_0_), channel_id=1, source_target_pairs={{0,6},{1,7},{2,4},{3,5},{4,2},{5,3},{6,0},{7,1},{8,14},{9,15},{10,... | collective-permute-start | bytes 393224 | tf_op jit(solution)/shard_map/ppermute | solution.py:386
  28.5 6.5 %collective-permute-start.5 = (bf16[256,256]{1,0:T(8,128)(2,1)S(1)}, bf16[256,256]{1,0:T(8,128)(2,1)S(1)}, u32[]{:S(2)}, u32[]{:S(2)}) collective-permute-start(bf16[256,256]{1,0:T(8,128)(2,1)S(1)} %get-tuple-element.28.refs_0_), channel_id=1, source_target_pairs={{0,4},{1,5},{2,6},{3,7},{4,0},{5,1},{6,2},{7,3},{8,12},{9,13},{10,... | collective-permute-start | bytes 393224 | tf_op jit(solution)/shard_map/ppermute | solution.py:386
  29.7 5.6 %collective-permute-start.4 = (bf16[256,256]{1,0:T(8,128)(2,1)S(1)}, bf16[256,256]{1,0:T(8,128)(2,1)S(1)}, u32[]{:S(2)}, u32[]{:S(2)}) collective-permute-start(bf16[256,256]{1,0:T(8,128)(2,1)S(1)} %get-tuple-element.28.refs_0_), channel_id=1, source_target_pairs={{0,2},{1,3},{2,0},{3,1},{4,6},{5,7},{6,4},{7,5},{8,10},{9,11},{10,... | collective-permute-start | bytes 393224 | tf_op jit(solution)/shard_map/ppermute | solution.py:386
  30.6 6.1 %collective-permute-start.7 = (bf16[256,256]{1,0:T(8,128)(2,1)S(1)}, bf16[256,256]{1,0:T(8,128)(2,1)S(1)}, u32[]{:S(2)}, u32[]{:S(2)}) collective-permute-start(bf16[256,256]{1,0:T(8,128)(2,1)S(1)} %get-tuple-element.28.refs_0_), channel_id=1, source_target_pairs={{0,1},{1,0},{2,3},{3,2},{4,5},{5,4},{6,7},{7,6},{8,9},{9,8},{10,11... | collective-permute-start | bytes 393224 | tf_op jit(solution)/shard_map/ppermute | solution.py:387
  33.8 2.8 %collective-permute-start.10 = (bf16[256,256]{1,0:T(8,128)(2,1)S(1)}, bf16[256,256]{1,0:T(8,128)(2,1)S(1)}, u32[]{:S(2)}, u32[]{:S(2)}) collective-permute-start(bf16[256,256]{1,0:T(8,128)(2,1)S(1)} %collective-permute-done.6.refs_3_), channel_id=1, source_target_pairs={{0,1},{1,0},{2,3},{3,2},{4,5},{5,4},{6,7},{7,6},{8,9},{9,8},{10,11... | collective-permute-start | bytes 393224 | tf_op jit(solution)/shard_map/ppermute | solution.py:387
  35.0 1.7 %collective-permute-start.9 = (bf16[256,256]{1,0:T(8,128)(2,1)S(1)}, bf16[256,256]{1,0:T(8,128)(2,1)S(1)}, u32[]{:S(2)}, u32[]{:S(2)}) collective-permute-start(bf16[256,256]{1,0:T(8,128)(2,1)S(1)} %collective-permute-done.5.refs_2_), channel_id=1, source_target_pairs={{0,1},{1,0},{2,3},{3,2},{4,5},{5,4},{6,7},{7,6},{8,9},{9,8},{10,11... | collective-permute-start | bytes 393224 | tf_op jit(solution)/shard_map/ppermute | solution.py:387
  35.2 1.5 %collective-permute-start.8 = (bf16[256,256]{1,0:T(8,128)(2,1)S(1)}, bf16[256,256]{1,0:T(8,128)(2,1)S(1)}, u32[]{:S(2)}, u32[]{:S(2)}) collective-permute-start(bf16[256,256]{1,0:T(8,128)(2,1)S(1)} %collective-permute-done.4.refs_1_), channel_id=1, source_target_pairs={{0,1},{1,0},{2,3},{3,2},{4,5},{5,4},{6,7},{7,6},{8,9},{9,8},{10,11... | collective-permute-start | bytes 393224 | tf_op jit(solution)/shard_map/ppermute | solution.py:387
  36.7 2.2 %copy-start.1 = (bf16[32,256,1,4,64]{1,4,3,2,0:T(8,128)(2,1)S(1)}, bf16[32,256,1,4,64]{1,4,3,2,0:T(8,128)(2,1)}, u32[]{:S(2)}) copy-start(bf16[32,256,1,4,64]{1,4,3,2,0:T(8,128)(2,1)} %param.8) | copy-start | bytes 12582916
  38.9 25.3 %copy-start.2 = (bf16[32,256,1,4,64]{1,4,3,2,0:T(8,128)(2,1)S(1)}, bf16[32,256,1,4,64]{1,4,3,2,0:T(8,128)(2,1)}, u32[]{:S(2)}) copy-start(bf16[32,256,1,4,64]{1,4,3,2,0:T(8,128)(2,1)} %param.8) | copy-start | bytes 12582916
  38.9 39.3 %slice-start = ((s8[8388608]{0:T(1024)(128)(4,1)}), s8[4194304]{0:T(1024)(128)(4,1)S(1)}, s32[]{:S(2)}) async-start(s8[8388608]{0:T(1024)(128)(4,1)} %bitcast.21), calls=%async_computation | async-start | bytes 8388608
  55.1 2.0 %copy-start.4 = (bf16[32,256,256]{2,1,0:T(8,128)(2,1)}, bf16[32,256,256]{2,1,0:T(8,128)(2,1)S(1)}, u32[]{:S(2)}) copy-start(bf16[32,256,256]{2,1,0:T(8,128)(2,1)S(1)} %get-tuple-element.37.refs_11_.grad_ref) | copy-start | bytes 12582916
  57.1 1.9 %collective-permute-start.11 = (bf16[4,256,256]{2,1,0:T(8,128)(2,1)S(1)}, bf16[4,256,256]{2,1,0:T(8,128)(2,1)S(1)}, u32[]{:S(2)}, u32[]{:S(2)}) collective-permute-start(bf16[4,256,256]{2,1,0:T(8,128)(2,1)S(1)} %get-tuple-element.31), channel_id=1, source_target_pairs={{0,1},{1,0},{2,3},{3,2},{4,5},{5,4},{6,7},{7,6},{8,9},{9,8},{10,11... | collective-permute-start | bytes 1572872 | tf_op jit(solution)/shard_map/ppermute | solution.py:364
  59.0 1.2 %copy-start.8 = (bf16[8,256,256]{2,1,0:T(8,128)(2,1)S(1)}, bf16[8,256,256]{2,1,0:T(8,128)(2,1)}, u32[]{:S(2)}) copy-start(bf16[8,256,256]{2,1,0:T(8,128)(2,1)} %constant.15.clone.own_ref.other_ref) | copy-start | bytes 3145732
  60.2 18.0 %slice-start.1 = ((s8[8388608]{0:T(1024)(128)(4,1)}), s8[4194304]{0:T(1024)(128)(4,1)S(1)}, s32[]{:S(2)}) async-start(s8[8388608]{0:T(1024)(128)(4,1)} %bitcast.21), calls=%async_computation.1 | async-start | bytes 8388608
  60.7 15.6 %collective-permute-start.12 = (bf16[256,256]{1,0:T(8,128)(2,1)S(1)}, bf16[256,256]{1,0:T(8,128)(2,1)S(1)}, u32[]{:S(2)}, u32[]{:S(2)}) collective-permute-start(bf16[256,256]{1,0:T(8,128)(2,1)S(1)} %get-tuple-element.33), channel_id=1, source_target_pairs={{0,2},{1,3},{2,0},{3,1},{4,6},{5,7},{6,4},{7,5},{8,10},{9,11},{10,... | collective-permute-start | bytes 393224 | tf_op jit(solution)/shard_map/ppermute | solution.py:383
  62.4 14.3 %collective-permute-start.13 = (bf16[256,256]{1,0:T(8,128)(2,1)S(1)}, bf16[256,256]{1,0:T(8,128)(2,1)S(1)}, u32[]{:S(2)}, u32[]{:S(2)}) collective-permute-start(bf16[256,256]{1,0:T(8,128)(2,1)S(1)} %get-tuple-element.34), channel_id=1, source_target_pairs={{0,4},{1,5},{2,6},{3,7},{4,0},{5,1},{6,2},{7,3},{8,12},{9,13},{10,... | collective-permute-start | bytes 393224 | tf_op jit(solution)/shard_map/ppermute | solution.py:383
  63.0 14.8 %collective-permute-start.14 = (bf16[256,256]{1,0:T(8,128)(2,1)S(1)}, bf16[256,256]{1,0:T(8,128)(2,1)S(1)}, u32[]{:S(2)}, u32[]{:S(2)}) collective-permute-start(bf16[256,256]{1,0:T(8,128)(2,1)S(1)} %get-tuple-element.35), channel_id=1, source_target_pairs={{0,6},{1,7},{2,4},{3,5},{4,2},{5,3},{6,0},{7,1},{8,14},{9,15},{10,... | collective-permute-start | bytes 393224 | tf_op jit(solution)/shard_map/ppermute | solution.py:383
  64.2 2.2 %copy-start.5 = (bf16[32,256,256]{2,1,0:T(8,128)(2,1)S(1)}, bf16[32,256,256]{2,1,0:T(8,128)(2,1)}, u32[]{:S(2)}) copy-start(bf16[32,256,256]{2,1,0:T(8,128)(2,1)} %copy-done.4) | copy-start | bytes 12582916
  69.3 4.3 %collective-permute-start.28 = (f32[64,64]{1,0:T(8,128)S(1)}, f32[64,64]{1,0:T(8,128)S(1)}, u32[]{:S(2)}, u32[]{:S(2)}) collective-permute-start(f32[64,64]{1,0:T(8,128)S(1)} %local_sum.1), channel_id=1, source_target_pairs={{0,7},{1,6},{2,5},{3,4},{4,3},{5,2},{6,1},{7,0},{8,15},{9,14},{10,... | collective-permute-start | bytes 49160 | tf_op jit(solution)/shard_map/ppermute | solution.py:318
  69.9 4.9 %collective-permute-start.27 = (f32[64,64]{1,0:T(8,128)S(1)}, f32[64,64]{1,0:T(8,128)S(1)}, u32[]{:S(2)}, u32[]{:S(2)}) collective-permute-start(f32[64,64]{1,0:T(8,128)S(1)} %local_sum.1), channel_id=1, source_target_pairs={{0,6},{1,7},{2,4},{3,5},{4,2},{5,3},{6,0},{7,1},{8,14},{9,15},{10,... | collective-permute-start | bytes 49160 | tf_op jit(solution)/shard_map/ppermute | solution.py:318
  73.6 10.4 %collective-permute-start.26 = (f32[64,64]{1,0:T(8,128)S(1)}, f32[64,64]{1,0:T(8,128)S(1)}, u32[]{:S(2)}, u32[]{:S(2)}) collective-permute-start(f32[64,64]{1,0:T(8,128)S(1)} %local_sum.1), channel_id=1, source_target_pairs={{0,5},{1,4},{2,7},{3,6},{4,1},{5,0},{6,3},{7,2},{8,13},{9,12},{10,... | collective-permute-start | bytes 49160 | tf_op jit(solution)/shard_map/ppermute | solution.py:318
  74.8 10.6 %collective-permute-start.25 = (f32[64,64]{1,0:T(8,128)S(1)}, f32[64,64]{1,0:T(8,128)S(1)}, u32[]{:S(2)}, u32[]{:S(2)}) collective-permute-start(f32[64,64]{1,0:T(8,128)S(1)} %local_sum.1), channel_id=1, source_target_pairs={{0,4},{1,5},{2,6},{3,7},{4,0},{5,1},{6,2},{7,3},{8,12},{9,13},{10,... | collective-permute-start | bytes 49160 | tf_op jit(solution)/shard_map/ppermute | solution.py:318
  76.3 9.8 %collective-permute-start.24 = (f32[64,64]{1,0:T(8,128)S(1)}, f32[64,64]{1,0:T(8,128)S(1)}, u32[]{:S(2)}, u32[]{:S(2)}) collective-permute-start(f32[64,64]{1,0:T(8,128)S(1)} %local_sum.1), channel_id=1, source_target_pairs={{0,3},{1,2},{2,1},{3,0},{4,7},{5,6},{6,5},{7,4},{8,11},{9,10},{10,... | collective-permute-start | bytes 49160 | tf_op jit(solution)/shard_map/ppermute | solution.py:318
  76.7 10.8 %collective-permute-start.23 = (f32[64,64]{1,0:T(8,128)S(1)}, f32[64,64]{1,0:T(8,128)S(1)}, u32[]{:S(2)}, u32[]{:S(2)}) collective-permute-start(f32[64,64]{1,0:T(8,128)S(1)} %local_sum.1), channel_id=1, source_target_pairs={{0,2},{1,3},{2,0},{3,1},{4,6},{5,7},{6,4},{7,5},{8,10},{9,11},{10,... | collective-permute-start | bytes 49160 | tf_op jit(solution)/shard_map/ppermute | solution.py:318
  77.8 9.7 %collective-permute-start.22 = (f32[64,64]{1,0:T(8,128)S(1)}, f32[64,64]{1,0:T(8,128)S(1)}, u32[]{:S(2)}, u32[]{:S(2)}) collective-permute-start(f32[64,64]{1,0:T(8,128)S(1)} %local_sum.1), channel_id=1, source_target_pairs={{0,1},{1,0},{2,3},{3,2},{4,5},{5,4},{6,7},{7,6},{8,9},{9,8},{10,11... | collective-permute-start | bytes 49160 | tf_op jit(solution)/shard_map/ppermute | solution.py:318
  84.0 12.0 %collective-permute-start.17 = (bf16[256,256]{1,0:T(8,128)(2,1)S(1)}, bf16[256,256]{1,0:T(8,128)(2,1)S(1)}, u32[]{:S(2)}, u32[]{:S(2)}) collective-permute-start(bf16[256,256]{1,0:T(8,128)(2,1)S(1)} %get-tuple-element.36.refs_0_), channel_id=1, source_target_pairs={{0,6},{1,7},{2,4},{3,5},{4,2},{5,3},{6,0},{7,1},{8,14},{9,15},{10,... | collective-permute-start | bytes 393224 | tf_op jit(solution)/shard_map/ppermute | solution.py:386
  85.4 11.1 %collective-permute-start.16 = (bf16[256,256]{1,0:T(8,128)(2,1)S(1)}, bf16[256,256]{1,0:T(8,128)(2,1)S(1)}, u32[]{:S(2)}, u32[]{:S(2)}) collective-permute-start(bf16[256,256]{1,0:T(8,128)(2,1)S(1)} %get-tuple-element.36.refs_0_), channel_id=1, source_target_pairs={{0,4},{1,5},{2,6},{3,7},{4,0},{5,1},{6,2},{7,3},{8,12},{9,13},{10,... | collective-permute-start | bytes 393224 | tf_op jit(solution)/shard_map/ppermute | solution.py:386
  86.1 10.5 %collective-permute-start.15 = (bf16[256,256]{1,0:T(8,128)(2,1)S(1)}, bf16[256,256]{1,0:T(8,128)(2,1)S(1)}, u32[]{:S(2)}, u32[]{:S(2)}) collective-permute-start(bf16[256,256]{1,0:T(8,128)(2,1)S(1)} %get-tuple-element.36.refs_0_), channel_id=1, source_target_pairs={{0,2},{1,3},{2,0},{3,1},{4,6},{5,7},{6,4},{7,5},{8,10},{9,11},{10,... | collective-permute-start | bytes 393224 | tf_op jit(solution)/shard_map/ppermute | solution.py:386
  87.5 5.8 %collective-permute-start.31 = (f32[64,64]{1,0:T(8,128)S(1)}, f32[64,64]{1,0:T(8,128)S(1)}, u32[]{:S(2)}, u32[]{:S(2)}) collective-permute-start(f32[64,64]{1,0:T(8,128)S(1)} %add_add_fusion), channel_id=1, source_target_pairs={{0,24},{8,16},{16,8},{24,0},{1,25},{9,17},{17,9},{25,1},{2,26},{10... | collective-permute-start | bytes 49160 | tf_op jit(solution)/shard_map/ppermute | solution.py:318
  91.2 4.8 %collective-permute-start.30 = (f32[64,64]{1,0:T(8,128)S(1)}, f32[64,64]{1,0:T(8,128)S(1)}, u32[]{:S(2)}, u32[]{:S(2)}) collective-permute-start(f32[64,64]{1,0:T(8,128)S(1)} %add_add_fusion), channel_id=1, source_target_pairs={{0,16},{8,24},{16,0},{24,8},{1,17},{9,25},{17,1},{25,9},{2,18},{10... | collective-permute-start | bytes 49160 | tf_op jit(solution)/shard_map/ppermute | solution.py:318
  93.4 3.9 %collective-permute-start.29 = (f32[64,64]{1,0:T(8,128)S(1)}, f32[64,64]{1,0:T(8,128)S(1)}, u32[]{:S(2)}, u32[]{:S(2)}) collective-permute-start(f32[64,64]{1,0:T(8,128)S(1)} %add_add_fusion), channel_id=1, source_target_pairs={{0,8},{8,0},{16,24},{24,16},{1,9},{9,1},{17,25},{25,17},{2,10},{10... | collective-permute-start | bytes 49160 | tf_op jit(solution)/shard_map/ppermute | solution.py:318
  96.0 13.8 %collective-permute-start.18 = (bf16[256,256]{1,0:T(8,128)(2,1)S(1)}, bf16[256,256]{1,0:T(8,128)(2,1)S(1)}, u32[]{:S(2)}, u32[]{:S(2)}) collective-permute-start(bf16[256,256]{1,0:T(8,128)(2,1)S(1)} %get-tuple-element.36.refs_0_), channel_id=1, source_target_pairs={{0,1},{1,0},{2,3},{3,2},{4,5},{5,4},{6,7},{7,6},{8,9},{9,8},{10,11... | collective-permute-start | bytes 393224 | tf_op jit(solution)/shard_map/ppermute | solution.py:387
  96.0 13.8 %collective-permute-start.21 = (bf16[256,256]{1,0:T(8,128)(2,1)S(1)}, bf16[256,256]{1,0:T(8,128)(2,1)S(1)}, u32[]{:S(2)}, u32[]{:S(2)}) collective-permute-start(bf16[256,256]{1,0:T(8,128)(2,1)S(1)} %collective-permute-done.17.refs_3_), channel_id=1, source_target_pairs={{0,1},{1,0},{2,3},{3,2},{4,5},{5,4},{6,7},{7,6},{8,9},{9,8},{10,11... | collective-permute-start | bytes 393224 | tf_op jit(solution)/shard_map/ppermute | solution.py:387
  96.5 13.3 %collective-permute-start.20 = (bf16[256,256]{1,0:T(8,128)(2,1)S(1)}, bf16[256,256]{1,0:T(8,128)(2,1)S(1)}, u32[]{:S(2)}, u32[]{:S(2)}) collective-permute-start(bf16[256,256]{1,0:T(8,128)(2,1)S(1)} %collective-permute-done.16.refs_2_), channel_id=1, source_target_pairs={{0,1},{1,0},{2,3},{3,2},{4,5},{5,4},{6,7},{7,6},{8,9},{9,8},{10,11... | collective-permute-start | bytes 393224 | tf_op jit(solution)/shard_map/ppermute | solution.py:387
  96.6 13.2 %collective-permute-start.19 = (bf16[256,256]{1,0:T(8,128)(2,1)S(1)}, bf16[256,256]{1,0:T(8,128)(2,1)S(1)}, u32[]{:S(2)}, u32[]{:S(2)}) collective-permute-start(bf16[256,256]{1,0:T(8,128)(2,1)S(1)} %collective-permute-done.15.refs_1_), channel_id=1, source_target_pairs={{0,1},{1,0},{2,3},{3,2},{4,5},{5,4},{6,7},{7,6},{8,9},{9,8},{10,11... | collective-permute-start | bytes 393224 | tf_op jit(solution)/shard_map/ppermute | solution.py:387
  98.9 10.9 %copy-start.6 = (bf16[32,256,256]{2,1,0:T(8,128)(2,1)S(1)}, bf16[32,256,256]{2,1,0:T(8,128)(2,1)}, u32[]{:S(2)}) copy-start(bf16[32,256,256]{2,1,0:T(8,128)(2,1)} %copy-done.4) | copy-start | bytes 12582916
  98.9 10.9 %copy-start.10 = (bf16[8,256,256]{2,1,0:T(8,128)(2,1)S(1)}, bf16[8,256,256]{2,1,0:T(8,128)(2,1)}, u32[]{:S(2)}) copy-start(bf16[8,256,256]{2,1,0:T(8,128)(2,1)} %constant.16.clone.refs_8_) | copy-start | bytes 3145732
  98.9 10.9 %copy-start.14 = (bf16[64,256]{1,0:T(8,128)(2,1)S(1)}, bf16[64,256]{1,0:T(8,128)(2,1)}, u32[]{:S(2)}) copy-start(bf16[64,256]{1,0:T(8,128)(2,1)} %constant.14.clone.table_ref.refs_9_) | copy-start | bytes 98308
  (3 other events, 2.6 us)

commit v2 on v1

--- a/solution.py
+++ b/solution.py
@@ -18,6 +18,7 @@
 BF16 = jnp.bfloat16
 ROOT = math.sqrt(2.0 / math.pi)
 CUBE = 0.044715
+VMEM = 52 << 20
 
 
 def to_bf16(values):
@@ -62,12 +63,27 @@
     return lax.dot_general(left, right, (((1,), (1,)), ((), ())), preferred_element_type=F32)
 
 
+def streamed(ref, buffer, sem, at, steps, axis, size):
+    def copy(step):
+        where = [slice(None)] * axis + [pl.ds(step % (KX // size) * size, size)]
+        where[1] = pl.ds(step // (KX // size), 1)
+        return pltpu.make_async_copy(ref.at[tuple(where)], buffer.at[step], sem.at[step])
+
+    @pl.when(at == 0)
+    def _():
+        for step in range(steps):
+            copy(step).start()
+
+    copy(at).wait()
+    return buffer.at[at]
+
+
 def whole(shape):
     zeros = (0,) * len(shape)
     return pl.BlockSpec(shape, lambda *_: zeros)
 
 
-def call(kernel, here, operands, grid, in_specs, out_specs, out_shape, scratch=(), flops=0, moved=0, name=None):
+def call(kernel, here, operands, grid, in_specs, out_specs, out_shape, scratch=(), flops=0, moved=0, name=None, aliases=None):
     return pl.pallas_call(
         kernel,
         out_shape=out_shape,
@@ -79,10 +95,11 @@
             scratch_shapes=list(scratch),
         ),
         compiler_params=pltpu.CompilerParams(
-            dimension_semantics=("arbitrary",) * len(grid), vmem_limit_bytes=40 << 20
+            dimension_semantics=("arbitrary",) * len(grid), vmem_limit_bytes=VMEM
         ),
         cost_estimate=pl.CostEstimate(flops=flops, bytes_accessed=moved, transcendentals=0),
         name=name,
+        input_output_aliases=aliases or {},
     )(here, *operands)
 
 
@@ -129,11 +146,12 @@
 
 
 def mix_forward(count, zs, here, *refs):
-    terms, (w_ref, out_ref, spread_ref, coeff, prod) = refs[:count], refs[count:]
-    i, jc = pl.program_id(0), pl.program_id(1)
-    per = w_ref.shape[2]
+    terms, (w_hbm, out_ref, spread_ref, coeff, prod, buffer, sem) = refs[:count], refs[count:]
+    step = pl.program_id(0)
+    per = buffer.shape[3]
     modes = coeff.shape[0] // 2
-    first = (i * pl.num_programs(1) + jc) * per
+    first = step * per
+    w_ref = streamed(w_hbm, buffer, sem, step, buffer.shape[0], 2, per)
 
     @pl.when(first == 0)
     def _():
@@ -174,14 +192,24 @@
 
 
 def mix_backward(count, zs, here, *refs):
-    terms, (w_ref, out_ref, pair_ref, prod) = refs[:count], refs[count:]
-    i, jc = pl.program_id(0), pl.program_id(1)
-    per = w_ref.shape[2]
+    terms, locals_ = refs[:count], refs[count:-6]
+    w_hbm, out_ref, pair_ref, prod, buffer, sem = refs[-6:]
+    step = pl.program_id(0)
+    per = buffer.shape[3]
     modes = prod.shape[1] // (2 * zs)
-    first = (i * pl.num_programs(1) + jc) * per
+    first = step * per
+    w_ref = streamed(w_hbm, buffer, sem, step, buffer.shape[0], 2, per)
 
     @pl.when(first == 0)
     def _():
+        parts = [ref[...] for ref in locals_]
+        while len(parts) > 1:
+            parts = [a + b for a, b in zip(parts[::2], parts[1::2])]
+        extra = 64 // zs
+        value = jnp.concatenate([parts[0][at * extra : (at + 1) * extra] for at in range(zs)], 1)
+        coarse = value.astype(BF16)
+        out_ref[2 * modes : 2 * modes + extra] = coarse
+        out_ref[2 * modes + extra :] = (value - coarse.astype(F32)).astype(BF16)
         grad = total(terms)
         sign = half_sign((modes, 128))
         low = low_half((modes, 128))
@@ -214,12 +242,12 @@
                 ).astype(BF16)
 
 
-def gram(zs, here, spread_ref, pair_ref, out_ref):
-    i, jc = pl.program_id(0), pl.program_id(1)
+def gram(zs, start, here, spread_ref, pair_ref, *refs):
+    out_ref = refs[-1]
     per = out_ref.shape[2]
     group = 4
     unit = 2 * zs
-    first = (i * pl.num_programs(1) + jc) * per
+    first = (start + pl.program_id(0)) * per
     shape = (group * unit, 128)
     owner = lax.broadcasted_iota(jnp.int32, shape, 0) // unit
     for at in range(0, per, group):
@@ -249,76 +277,100 @@
     return jnp.transpose(joined).astype(BF16)
 
 
+def block_mixing(weight, zs):
+    rows = jnp.concatenate([weight] * zs, 1)
+    full = jnp.concatenate([rows] * zs, 0)
+    row = lax.broadcasted_iota(jnp.int32, full.shape, 0) // 64
+    lane = lax.broadcasted_iota(jnp.int32, full.shape, 1) // 64
+    return jnp.where(row == lane, full, 0.0).astype(BF16)
+
+
 def middle(count, here, *refs):
     blocks, rest = refs[:count], refs[count:]
-    x_ref, y_ref, mixing_ref, field_ref, cot_ref = rest[:5]
-    out_ref, grad_ref, keep_ref, send_ref, rows = rest[5:]
-
-    @pl.when(pl.program_id(0) == 0)
+    x_ref, y_ref, weight_ref, field_ref, cot_ref = rest[:5]
+    out_ref, grad_ref, keep_ref, send_ref, term_ref, rows, mixing, acc = rest[5:]
+    step = pl.program_id(0)
+    size = field_ref.shape[0]
+    columns = field_ref.shape[1]
+    zs = columns // 64
+
+    @pl.when(step == 0)
     def _():
         grid_rows(here, blocks, x_ref, rows)
+        mixing[...] = block_mixing(jnp.transpose(weight_ref[...].astype(F32)), zs)
+        acc[...] = jnp.zeros_like(acc)
 
     table = y_ref[...]
-    mixing = mixing_ref[...]
-    parts = []
-    for x in range(field_ref.shape[0]):
-        p = dot(row_at(rows, field_ref.shape[0], x), table) + dot(mixing, field_ref[x])
-        square = p * p
-        t = jnp.tanh(p * (ROOT + ROOT * CUBE * square))
-        half = 0.5 + 0.5 * t
-        out_ref[x] = (p * half).astype(BF16)
-        slope = half + p * (1.0 - t * t) * (0.5 * ROOT + 1.5 * ROOT * CUBE * square)
-        grad = (cot_ref[x].astype(F32) * slope).astype(BF16)
-        grad_ref[x] = grad
-        parts.append(dot_nt(table, grad))
+    lefts = [row_at(rows, size, x) for x in range(size)]
+    low = low_half((64, 128))
+    parts, sums = [], []
+
+    def reduce(x):
+        got = dot_nt(jnp.concatenate([table, field_ref[x]], 0), grad_ref[x])
+        parts.append(got[: 2 * KY])
+        for tile in range(zs // 2):
+            lanes = slice(tile * 128, (tile + 1) * 128)
+            at = 2 * KY + tile * 128
+            sums.append((lanes, jnp.where(low, got[at : at + 64, lanes], got[at + 64 : at + 128, lanes])))
+
+    for x in range(size):
+        for at in range(0, columns, 64):
+            part = slice(at, at + 64)
+            p = dot(lefts[x][part], table) + dot(mixing[part, :], field_ref[x])
+            square = p * p
+            t = jnp.tanh(p * (ROOT + ROOT * CUBE * square))
+            half = 0.5 + 0.5 * t
+            out_ref[x, part] = (p * half).astype(BF16)
+            slope = half + p * (1.0 - t * t) * (0.5 * ROOT + 1.5 * ROOT * CUBE * square)
+            grad_ref[x, part] = (cot_ref[x, part].astype(F32) * slope).astype(BF16)
+        if x:
+            reduce(x - 1)
+    reduce(size - 1)
     store_spectrum(here, parts, keep_ref, send_ref)
-
-
-def local_sum(here, field_ref, grad_ref, out_ref, acc):
-    step = pl.program_id(0)
-
-    @pl.when(step == 0)
-    def _():
-        acc[...] = jnp.zeros_like(acc)
-
-    got = dot_nt(field_ref[0], grad_ref[0])
-    for x in range(1, field_ref.shape[0]):
-        got += dot_nt(field_ref[x], grad_ref[x])
-    acc[...] += got
+    for lanes, value in sums:
+        acc[:, lanes] += value
 
     @pl.when(step == pl.num_programs(0) - 1)
     def _():
         value = acc[...]
-        parts = [value[at : at + 64, at : at + 64] for at in range(0, value.shape[0], 64)]
+        parts = [value[:, at : at + 64] for at in range(0, columns, 64)]
         while len(parts) > 1:
             parts = [a + b for a, b in zip(parts[::2], parts[1::2])]
-        out_ref[...] = parts[0]
-
-
-def last(count, here, *refs):
+        term_ref[...] = parts[0]
+
+
+def last(count, scale, here, *refs):
     blocks, rest = refs[:count], refs[count:]
-    x_ref, y_ref, mixing_ref, grad_ref, out_ref, rows = rest
+    x_ref, y_ref, weight_ref, grad_ref, out_ref, local_ref, rows, mixing = rest
+    columns = grad_ref.shape[1]
+    size = grad_ref.shape[0]
 
     @pl.when(pl.program_id(0) == 0)
     def _():
-        grid_rows(here, blocks, x_ref, rows)
+        height = x_ref.shape[2]
+        extra = 64 * 64 // columns
+        grid_rows(here, [block.at[pl.ds(0, height)] for block in blocks], x_ref, rows)
+        mixing[...] = block_mixing(weight_ref[...].astype(F32), columns // 64)
+        parts = [
+            block[pl.ds(height, extra), :].astype(F32) + block[pl.ds(height + extra, extra), :].astype(F32)
+            for block in blocks
+        ]
+        while len(parts) > 1:
+            parts = [a + b for a, b in zip(parts[::2], parts[1::2])]
+        for at in range(columns // 64):
+            local_ref[at * extra : (at + 1) * extra, :] = parts[0][:, at * 64 : (at + 1) * 64] * scale
 
     table = y_ref[...]
-    mixing = mixing_ref[...]
-    for x in range(grad_ref.shape[0]):
-        value = dot(row_at(rows, grad_ref.shape[0], x), table) + dot(mixing, grad_ref[x])
-        out_ref[x] = value.astype(BF16)
+    lefts = [row_at(rows, size, x) for x in range(size)]
+    for x in range(size):
+        for at in range(0, columns, 64):
+            part = slice(at, at + 64)
+            value = dot(lefts[x][part], table) + dot(mixing[part, :], grad_ref[x])
+            out_ref[x, part] = value.astype(BF16)
 
 
 def flip(axis, size, bit):
     return functools.partial(lax.ppermute, axis_name=axis, perm=[(at, at ^ bit) for at in range(size)])
-
-
-def exchange_sum(value, axis, size):
-    parts = [value] + [flip(axis, size, bit)(value) for bit in range(1, size)]
-    while len(parts) > 1:
-        parts = [a + b for a, b in zip(parts[::2], parts[1::2])]
-    return parts[0]
 
 
 def body(features, out_grad, spectral_weight, local_weight):
@@ -343,20 +395,25 @@
         return jnp.transpose(shaped, (0, 4, 1, 2, 3))
 
     field, cot = inner(features), inner(out_grad)
-    eye = jnp.eye(snaps * zs, dtype=BF16)
-    mixing = jnp.kron(eye, local_weight)
-    mixing_t = jnp.kron(eye, local_weight.T)
-
-    chunk = 4
-    steps = rows_here // chunk
-    field_spec = pl.BlockSpec((chunk, columns, grid_y), lambda g, _: (g, 0, 0))
+    wide, chunk = min(16, rows_here), min(8, rows_here)
+
+    def field_spec(size):
+        return pl.BlockSpec((size, columns, grid_y), lambda g, _: (g, 0, 0))
+
+    def half_spec(size):
+        return pl.BlockSpec((chips, size * unit, columns), lambda g, _: (0, g, 0))
+
     field_shape = jax.ShapeDtypeStruct((rows_here, columns, grid_y), BF16)
-    half_spec = pl.BlockSpec((chips, chunk * unit, columns), lambda g, _: (0, g, 0))
     half_shape = jax.ShapeDtypeStruct((chips, rows_here * unit, columns), BF16)
     y_spec = whole((2 * KY, grid_y))
     mode_shape = jax.ShapeDtypeStruct((2 * modes, columns), BF16)
     mode_spec = whole((2 * modes, columns))
-    mixing_spec = whole((columns, columns))
+    weight_small = whole((channels, channels))
+    small_shape = jax.ShapeDtypeStruct((channels, channels), F32)
+    mixing_scratch = pltpu.VMEM((columns, columns), BF16)
+    extra = 2 * channels * channels // columns
+    back_spec = whole((2 * modes + extra, columns))
+    back_shape = jax.ShapeDtypeStruct((2 * modes + extra, columns), BF16)
     field_bytes = rows_here * columns * grid_y * 2
     mode_bytes = 4 * modes * columns
 
@@ -386,9 +443,13 @@
         mine = [block] + [flip("mp", count, 2 * bit)(block) for bit in range(1, chips)]
         return mine + [flip("mp", count, 1)(value) for value in mine]
 
-    per = 8
-    mode_grid = (mode_rows, KX // per)
-    weight_spec = pl.BlockSpec((zs, 1, per, channels, 2 * channels), lambda i, j, _: (0, i, j, 0, 0))
+    per = 16
+    mode_steps = modes // per
+    weight_spec = pl.BlockSpec(memory_space=pl.ANY)
+    weight_scratch = [
+        pltpu.VMEM((mode_steps, zs, 1, per, channels, 2 * channels), BF16),
+        pltpu.SemaphoreType.DMA((mode_steps,)),
+    ]
     spread_shape = (modes * 2 * zs, columns)
     pair_shape = (modes * 2 * zs, 2 * channels)
     weight_bytes = zs * modes * channels * 2 * channels * 2
@@ -397,9 +458,9 @@
         forward_y,
         here,
         (field, y_plain),
-        (steps,),
-        [field_spec, y_spec],
-        [half_spec] * 2,
+        (rows_here // wide,),
+        [field_spec(wide), y_spec],
+        [half_spec(wide)] * 2,
         [half_shape] * 2,
         flops=field_bytes * 2 * KY,
         moved=field_bytes + mode_bytes * count,
@@ -410,11 +471,11 @@
         functools.partial(mix_forward, chips, zs),
         here,
         (*terms, spectral_weight),
-        mode_grid,
+        (mode_steps,),
         [mode_spec] * chips + [weight_spec],
         [mode_spec, whole(spread_shape)],
         [mode_shape, jax.ShapeDtypeStruct(spread_shape, BF16)],
-        [pltpu.VMEM((2 * modes, columns), F32), pltpu.VMEM(pair_shape, F32)],
+        [pltpu.VMEM((2 * modes, columns), F32), pltpu.VMEM(pair_shape, F32)] + weight_scratch,
         flops=weight_bytes * 8,
         moved=weight_bytes + mode_bytes * chips,
         name="mix_forward",
@@ -422,70 +483,65 @@
     blocks = to_all(mixed)
     x_back_spec = pl.BlockSpec((1, rows_here * unit, 2 * modes), lambda g, m: (m[0], 0, 0))
     rows_scratch = pltpu.VMEM((2, chips, rows_here * unit, columns), F32)
-    output, preact_grad, keep, send = call(
+    output, preact_grad, keep, send, local_term = call(
         functools.partial(middle, count),
         here,
-        (*blocks, x_back, y_weighted, mixing_t, field, cot),
-        (steps,),
-        [mode_spec] * count + [x_back_spec, y_spec, mixing_spec, field_spec, field_spec],
-        [field_spec, field_spec, half_spec, half_spec],
-        [field_shape, field_shape, half_shape, half_shape],
-        [rows_scratch],
-        flops=field_bytes * (4 * KY + columns),
+        (*blocks, x_back, y_weighted, local_weight, field, cot),
+        (rows_here // chunk,),
+        [mode_spec] * count + [x_back_spec, y_spec, weight_small] + [field_spec(chunk)] * 2,
+        [field_spec(chunk)] * 2 + [half_spec(chunk)] * 2 + [weight_small],
+        [field_shape, field_shape, half_shape, half_shape, small_shape],
+        [rows_scratch, mixing_scratch, pltpu.VMEM((channels, columns), F32)],
+        flops=field_bytes * (4 * KY + 2 * columns),
         moved=field_bytes * 4 + mode_bytes * count * 2,
         name="middle",
     )
     terms = to_chips(keep, send)
-    local_term = call(
-        local_sum,
-        here,
-        (field, preact_grad),
-        (steps,),
-        [field_spec] * 2,
-        whole((channels, channels)),
-        jax.ShapeDtypeStruct((channels, channels), F32),
-        [pltpu.VMEM((columns, columns), F32)],
-        flops=field_bytes * columns,
-        moved=field_bytes * 2,
-        name="local_sum",
-    )
+    locals_ = [local_term] + [flip("dp", dp_count, bit)(local_term) for bit in range(1, dp_count)]
     back, pairs = call(
         functools.partial(mix_backward, chips, zs),
         here,
-        (*terms, spectral_weight),
-        mode_grid,
-        [mode_spec] * chips + [weight_spec],
-        [mode_spec, whole(pair_shape)],
-        [mode_shape, jax.ShapeDtypeStruct(pair_shape, F32)],
-        [pltpu.VMEM((zs // 2, modes * 2 * zs, 128), F32)],
+        (*terms, *locals_, spectral_weight),
+        (mode_steps,),
+        [mode_spec] * chips + [weight_small] * dp_count + [weight_spec],
+        [back_spec, whole(pair_shape)],
+        [back_shape, jax.ShapeDtypeStruct(pair_shape, F32)],
+        [pltpu.VMEM((zs // 2, modes * 2 * zs, 128), F32)] + weight_scratch,
         flops=weight_bytes * 8,
         moved=weight_bytes + mode_bytes * chips,
         name="mix_backward",
     )
-    blocks = to_all(back)
-    spectral_grad = call(
-        functools.partial(gram, zs),
+    def gram_part(start, size, before):
+        spec = pl.BlockSpec((zs, 1, KX, channels, 2 * channels), lambda g, _: (0, g + start, 0, 0, 0))
+        return call(
+            functools.partial(gram, zs, start),
+            here,
+            (spread, pairs, *before),
+            (size,),
+            [whole(spread_shape), whole(pair_shape)] + [pl.BlockSpec(memory_space=pl.ANY)] * len(before),
+            spec,
+            jax.ShapeDtypeStruct(spectral_weight.shape, F32),
+            flops=weight_bytes * 4,
+            moved=weight_bytes,
+            name="gram",
+            aliases={3: 0} if before else {},
+        )
+
+    mine = [back] + [flip("mp", count, 2 * bit)(back) for bit in range(1, chips)]
+    spectral_grad = gram_part(0, mode_rows // 2, ())
+    *others, spectral_grad = lax.optimization_barrier((*mine[1:], spectral_grad))
+    blocks = [back, *others] + [flip("mp", count, 1)(value) for value in (back, *others)]
+    spectral_grad = gram_part(mode_rows // 2, mode_rows - mode_rows // 2, (spectral_grad,))
+    scale = 1.0 / math.sqrt(NX * NY * snaps * dp_count * zs)
+    back_field, local_grad = call(
+        functools.partial(last, count, scale),
         here,
-        (spread, pairs),
-        mode_grid,
-        [whole(spread_shape), whole(pair_shape)],
-        weight_spec,
-        jax.ShapeDtypeStruct(spectral_weight.shape, F32),
-        flops=weight_bytes * 8,
-        moved=weight_bytes * 2,
-        name="gram",
-    )
-    grad_scale = 1.0 / math.sqrt(NX * NY * snaps * dp_count * zs)
-    local_grad = exchange_sum(exchange_sum(local_term, "mp", count), "dp", dp_count) * grad_scale
-    back_field = call(
-        functools.partial(last, count),
-        here,
-        (*blocks, x_back, y_plain, mixing, preact_grad),
-        (steps,),
-        [mode_spec] * count + [x_back_spec, y_spec, mixing_spec, field_spec],
-        field_spec,
-        field_shape,
-        [rows_scratch],
+        (*blocks, x_back, y_plain, local_weight, preact_grad),
+        (rows_here // wide,),
+        [back_spec] * count + [x_back_spec, y_spec, weight_small, field_spec(wide)],
+        [field_spec(wide), weight_small],
+        [field_shape, small_shape],
+        [rows_scratch, mixing_scratch],
         flops=field_bytes * (2 * KY + columns),
         moved=field_bytes * 2 + mode_bytes * count,
         name="last",

time: 116 us -> 87.5 us (0.75)
  local copies, waits for them, and re-layouts: 17.3 us -> 0.76 us
  Pallas kernels: 48.1 us -> 42.4 us
  waiting for transfers between devices: 21.2 us -> 18.8 us
  starting transfers between devices: 26.7 us -> 24.5 us
  other arithmetic: 1.61 us -> 0 us
    unnamed x38 -> x8, local copies, waits for them, and re-layouts: 15.8 us -> 0.76 us
    pallas_call x9, Pallas kernels: 48.1 us -> 42.4 us  [call(): pl.pallas_call(kernel, out_shape=out_shape, grid_spec=pltpu.PrefetchScala...]
    ppermute x10, waiting for transfers between devices: 6.86 us -> 2.92 us  [the longest x3 2.37 us: body(): flip('dp', dp_count, bit)(local_term)]
    ppermute x6 -> x3, starting transfers between devices: 7.04 us -> 3.55 us  [to_all(): flip('mp', count, 2 * bit)(block)]
    ppermute x10, starting transfers between devices: 9.56 us -> 11.6 us  [the longest x3 7.48 us: body(): flip('dp', dp_count, bit)(local_term)]
    mul x2 -> x0, other arithmetic: 1.58 us -> none  [the longest x1 0.96 us: body(): mixing = jnp.kron(eye, local_weight)]
    mul x2 -> x0, local copies, waits for them, and re-layouts: 1.4 us -> none  [the longest x1 1.18 us: body(): mixing = jnp.kron(eye, local_weight)]
    ppermute x6 -> x3, waiting for transfers between devices: 4.58 us -> 4.98 us  [to_all(): flip('mp', count, 2 * bit)(block)]
  transfers between devices with their start and end apart: 32 -> 25, of which waited for: 12 -> 10; matrix products, arithmetic and copies ran while one was open for 3% -> 0% of each run, Pallas kernels for 16% -> 10%
where the time goes in v2:
time: 87.5 us; the launch traced here: 87.2 us
  Pallas kernels  42.4 us (48%)
  starting transfers between devices  24.5 us (28%)
  waiting for transfers between devices  18.8 us (21%)
    pallas_call x9, Pallas kernels, call(): pl.pallas_call(kernel, out_shape=out_shape, grid_spec=pltpu.PrefetchScala...  42.4 us
    ppermute x6, starting transfers between devices, to_chips(): flip('mp', count, 2 * bit)(outs[bit])  8.01 us
    ppermute x3, starting transfers between devices, body(): flip('dp', dp_count, bit)(local_term)  7.48 us
    ppermute x6, waiting for transfers between devices, to_chips(): flip('mp', count, 2 * bit)(outs[bit])  6.53 us
    ppermute x3, waiting for transfers between devices, to_all(): flip('mp', count, 2 * bit)(block)  4.98 us
    ppermute x3, starting transfers between devices, to_all(): flip('mp', count, 2 * bit)(block)  3.55 us
    ppermute x3, starting transfers between devices, body(): flip('mp', count, 2 * bit)(back)  3.55 us
    ppermute x2, waiting for transfers between devices, to_chips(): got = flip('mp', count, 1)(send)  3.33 us
  transfers between devices with their start and end apart: 25, of which 10 were waited for; matrix products, arithmetic and copies ran while one was open for 0% of the time, Pallas kernels for 10%

profile of v2, /device:TPU:0, one launch (start us, length us, event | category | flops | bytes accessed | tf_op | source)
XLA Modules:
  0.0 87.2 jit_solution(17724216991455750788)
XLA Ops:
  0.6 0.0 copy-start
  0.6 0.7 copy-done
  1.4 3.2 %forward_y.1 = (bf16[4,256,256]{2,1,0:T(8,128)(2,1)S(1)}, bf16[4,256,256]{2,1,0:T(8,128)(2,1)S(1)}) custom-call(s32[1]{0:T(128)} %bitcast.here, bf16[32,256,256]{2,1,0:T(8,128)(2,1)} %bitcast.17, bf16[64,256]{1,0:T(8,128)(2,1)S(1)} %copy-done), custom_call_target="tpu_custom_call" | custom-call | flops 268435456 | bytes 5242880 | tf_op jit(solution)/shard_map/forward_y/pallas_call | solution.py:87
  4.6 0.5 collective-permute-start
  5.1 1.5 %collective-permute-done.got_ref = bf16[4,256,256]{2,1,0:T(8,128)(2,1)S(1)} collective-permute-done((bf16[4,256,256]{2,1,0:T(8,128)(2,1)S(1)}, bf16[4,256,256]{2,1,0:T(8,128)(2,1)S(1)}, u32[]{:S(2)}, u32[]{:S(2)}) %collective-permute-start) | collective-permute-done | bytes 524320 | tf_op jit(solution)/shard_map/ppermute | solution.py:421
  6.7 1.4 %forward_x.2 = (bf16[256,256]{1,0:T(8,128)(2,1)S(1)}, bf16[256,256]{1,0:T(8,128)(2,1)S(1)}, bf16[256,256]{1,0:T(8,128)(2,1)S(1)}, bf16[256,256]{1,0:T(8,128)(2,1)S(1)}) custom-call(s32[1]{0:T(128)} %bitcast.here, bf16[4,256,256]{2,1,0:T(8,128)(2,1)S(1)} %get-tuple-element.29.keep_ref, bf16[4,256,256]{2,1,0:T(8,128)(2,1)S(1)} %collective-permute-done.got_ref, ...), custom_call_target="tpu_custom_call" | custom-call | flops 268435456 | bytes 1572864 | tf_op jit(solution)/shard_map/forward_x/pallas_call | solution.py:87
  8.1 2.9 %collective-permute-start.1 = (bf16[256,256]{1,0:T(8,128)(2,1)S(1)}, bf16[256,256]{1,0:T(8,128)(2,1)S(1)}, u32[]{:S(2)}, u32[]{:S(2)}) collective-permute-start(bf16[256,256]{1,0:T(8,128)(2,1)S(1)} %get-tuple-element.32), channel_id=1, source_target_pairs={{0,2},{1,3},{2,0},{3,1},{4,6},{5,7},{6,4},{7,5},{8,10},{9,11},{10,... | collective-permute-start | bytes 393224 | tf_op jit(solution)/shard_map/ppermute | solution.py:440
  11.0 1.5 %collective-permute-start.2 = (bf16[256,256]{1,0:T(8,128)(2,1)S(1)}, bf16[256,256]{1,0:T(8,128)(2,1)S(1)}, u32[]{:S(2)}, u32[]{:S(2)}) collective-permute-start(bf16[256,256]{1,0:T(8,128)(2,1)S(1)} %get-tuple-element.33), channel_id=1, source_target_pairs={{0,4},{1,5},{2,6},{3,7},{4,0},{5,1},{6,2},{7,3},{8,12},{9,13},{10,... | collective-permute-start | bytes 393224 | tf_op jit(solution)/shard_map/ppermute | solution.py:440
  12.5 0.0 collective-permute-start.3
  12.6 2.3 %collective-permute-done.1.refs_1_ = bf16[256,256]{1,0:T(8,128)(2,1)S(1)} collective-permute-done((bf16[256,256]{1,0:T(8,128)(2,1)S(1)}, bf16[256,256]{1,0:T(8,128)(2,1)S(1)}, u32[]{:S(2)}, u32[]{:S(2)}) %collective-permute-start.1) | collective-permute-done | bytes 131104 | tf_op jit(solution)/shard_map/ppermute | solution.py:440
  14.9 4.2 %collective-permute-done.2.refs_2_ = bf16[256,256]{1,0:T(8,128)(2,1)S(1)} collective-permute-done((bf16[256,256]{1,0:T(8,128)(2,1)S(1)}, bf16[256,256]{1,0:T(8,128)(2,1)S(1)}, u32[]{:S(2)}, u32[]{:S(2)}) %collective-permute-start.2) | collective-permute-done | bytes 131104 | tf_op jit(solution)/shard_map/ppermute | solution.py:440
  19.1 4.0 %mix_forward.1 = (bf16[256,256]{1,0:T(8,128)(2,1)S(1)}, bf16[1024,256]{1,0:T(8,128)(2,1)S(1)}) custom-call(s32[1]{0:T(128)} %bitcast.here, bf16[256,256]{1,0:T(8,128)(2,1)S(1)} %get-tuple-element.31.refs_0_, bf16[256,256]{1,0:T(8,128)(2,1)S(1)} %collective-permute-done.1.refs_1_, bf16[256,256]{1,0:T(8,128)(2,1)S(1)} %collective-permute-done.2.refs_2_, ...), custom_call_target="tpu_custom_call" | custom-call | flops 67108864 | bytes 8912896 | tf_op jit(solution)/shard_map/mix_forward/pallas_call | solution.py:87
  23.1 1.3 %collective-permute-start.4 = (bf16[256,256]{1,0:T(8,128)(2,1)S(1)}, bf16[256,256]{1,0:T(8,128)(2,1)S(1)}, u32[]{:S(2)}, u32[]{:S(2)}) collective-permute-start(bf16[256,256]{1,0:T(8,128)(2,1)S(1)} %get-tuple-element.35.refs_0_), channel_id=1, source_target_pairs={{0,2},{1,3},{2,0},{3,1},{4,6},{5,7},{6,4},{7,5},{8,10},{9,11},{10,... | collective-permute-start | bytes 393224 | tf_op jit(solution)/shard_map/ppermute | solution.py:443
  24.4 0.8 collective-permute-start.5
  25.2 1.4 %collective-permute-start.6 = (bf16[256,256]{1,0:T(8,128)(2,1)S(1)}, bf16[256,256]{1,0:T(8,128)(2,1)S(1)}, u32[]{:S(2)}, u32[]{:S(2)}) collective-permute-start(bf16[256,256]{1,0:T(8,128)(2,1)S(1)} %get-tuple-element.35.refs_0_), channel_id=1, source_target_pairs={{0,6},{1,7},{2,4},{3,5},{4,2},{5,3},{6,0},{7,1},{8,14},{9,15},{10,... | collective-permute-start | bytes 393224 | tf_op jit(solution)/shard_map/ppermute | solution.py:443
  26.7 2.5 %collective-permute-done.4.refs_1_ = bf16[256,256]{1,0:T(8,128)(2,1)S(1)} collective-permute-done((bf16[256,256]{1,0:T(8,128)(2,1)S(1)}, bf16[256,256]{1,0:T(8,128)(2,1)S(1)}, u32[]{:S(2)}, u32[]{:S(2)}) %collective-permute-start.4) | collective-permute-done | bytes 131104 | tf_op jit(solution)/shard_map/ppermute | solution.py:443
  29.2 0.0 collective-permute-start.8
  29.2 2.5 %collective-permute-done.5.refs_2_ = bf16[256,256]{1,0:T(8,128)(2,1)S(1)} collective-permute-done((bf16[256,256]{1,0:T(8,128)(2,1)S(1)}, bf16[256,256]{1,0:T(8,128)(2,1)S(1)}, u32[]{:S(2)}, u32[]{:S(2)}) %collective-permute-start.5) | collective-permute-done | bytes 131104 | tf_op jit(solution)/shard_map/ppermute | solution.py:443
  31.7 0.0 collective-permute-start.9
  31.7 0.5 collective-permute-start.10
  32.2 0.8 collective-permute-done.9.refs_6_
  33.0 0.2 collective-permute-done.10.refs_7_
  33.2 11.9 %middle.1 = (bf16[32,256,256]{2,1,0:T(8,128)(2,1)}, bf16[32,256,256]{2,1,0:T(8,128)(2,1)}, bf16[4,256,256]{2,1,0:T(8,128)(2,1)S(1)}, bf16[4,256,256]{2,1,0:T(8,128)(2,1)}, f32[64,64]{1,0:T(8,128)S(1)}) custom-call(s32[1]{0:T(128)} %bitcast.here, bf16[256,256]{1,0:T(8,128)(2,1)S(1)} %get-tuple-element.35.refs_0_, ...), custom_call_target="tpu_custom_call" | custom-call | flops 2684354560 | bytes 18874368 | tf_op jit(solution)/shard_map/middle/pallas_call | solution.py:87
  45.1 0.3 collective-permute-start.11
  45.5 1.8 %collective-permute-done.11.got_ref = bf16[4,256,256]{2,1,0:T(8,128)(2,1)S(1)} collective-permute-done((bf16[4,256,256]{2,1,0:T(8,128)(2,1)}, bf16[4,256,256]{2,1,0:T(8,128)(2,1)S(1)}, u32[]{:S(2)}, u32[]{:S(2)}) %collective-permute-start.11) | collective-permute-done | bytes 524320 | tf_op jit(solution)/shard_map/ppermute | solution.py:421
  47.3 1.4 %forward_x.3 = (bf16[256,256]{1,0:T(8,128)(2,1)S(1)}, bf16[256,256]{1,0:T(8,128)(2,1)S(1)}, bf16[256,256]{1,0:T(8,128)(2,1)S(1)}, bf16[256,256]{1,0:T(8,128)(2,1)S(1)}) custom-call(s32[1]{0:T(128)} %bitcast.here, bf16[4,256,256]{2,1,0:T(8,128)(2,1)S(1)} %get-tuple-element.37.keep_ref, bf16[4,256,256]{2,1,0:T(8,128)(2,1)S(1)} %collective-permute-done.11.got_ref, ...), custom_call_target="tpu_custom_call" | custom-call | flops 268435456 | bytes 1572864 | tf_op jit(solution)/shard_map/forward_x/pallas_call | solution.py:87
  48.7 1.3 %collective-permute-start.12 = (bf16[256,256]{1,0:T(8,128)(2,1)S(1)}, bf16[256,256]{1,0:T(8,128)(2,1)S(1)}, u32[]{:S(2)}, u32[]{:S(2)}) collective-permute-start(bf16[256,256]{1,0:T(8,128)(2,1)S(1)} %get-tuple-element.40), channel_id=1, source_target_pairs={{0,2},{1,3},{2,0},{3,1},{4,6},{5,7},{6,4},{7,5},{8,10},{9,11},{10,... | collective-permute-start | bytes 393224 | tf_op jit(solution)/shard_map/ppermute | solution.py:440
  50.0 0.9 %collective-permute-start.13 = (bf16[256,256]{1,0:T(8,128)(2,1)S(1)}, bf16[256,256]{1,0:T(8,128)(2,1)S(1)}, u32[]{:S(2)}, u32[]{:S(2)}) collective-permute-start(bf16[256,256]{1,0:T(8,128)(2,1)S(1)} %get-tuple-element.41), channel_id=1, source_target_pairs={{0,4},{1,5},{2,6},{3,7},{4,0},{5,1},{6,2},{7,3},{8,12},{9,13},{10,... | collective-permute-start | bytes 393224 | tf_op jit(solution)/shard_map/ppermute | solution.py:440
  50.9 1.3 %collective-permute-start.14 = (bf16[256,256]{1,0:T(8,128)(2,1)S(1)}, bf16[256,256]{1,0:T(8,128)(2,1)S(1)}, u32[]{:S(2)}, u32[]{:S(2)}) collective-permute-start(bf16[256,256]{1,0:T(8,128)(2,1)S(1)} %get-tuple-element.42), channel_id=1, source_target_pairs={{0,6},{1,7},{2,4},{3,5},{4,2},{5,3},{6,0},{7,1},{8,14},{9,15},{10,... | collective-permute-start | bytes 393224 | tf_op jit(solution)/shard_map/ppermute | solution.py:440
  52.2 1.5 %collective-permute-start.15 = (f32[64,64]{1,0:T(8,128)S(1)}, f32[64,64]{1,0:T(8,128)S(1)}, u32[]{:S(2)}, u32[]{:S(2)}) collective-permute-start(f32[64,64]{1,0:T(8,128)S(1)} %get-tuple-element.43.refs_4_), channel_id=1, source_target_pairs={{0,8},{8,0},{16,24},{24,16},{1,9},{9,1},{17,25},{25,17},{2,10},{10... | collective-permute-start | bytes 49160 | tf_op jit(solution)/shard_map/ppermute | solution.py:500
  53.8 2.6 %collective-permute-start.16 = (f32[64,64]{1,0:T(8,128)S(1)}, f32[64,64]{1,0:T(8,128)S(1)}, u32[]{:S(2)}, u32[]{:S(2)}) collective-permute-start(f32[64,64]{1,0:T(8,128)S(1)} %get-tuple-element.43.refs_4_), channel_id=1, source_target_pairs={{0,16},{8,24},{16,0},{24,8},{1,17},{9,25},{17,1},{25,9},{2,18},{10... | collective-permute-start | bytes 49160 | tf_op jit(solution)/shard_map/ppermute | solution.py:500
  56.4 3.3 %collective-permute-start.17 = (f32[64,64]{1,0:T(8,128)S(1)}, f32[64,64]{1,0:T(8,128)S(1)}, u32[]{:S(2)}, u32[]{:S(2)}) collective-permute-start(f32[64,64]{1,0:T(8,128)S(1)} %get-tuple-element.43.refs_4_), channel_id=1, source_target_pairs={{0,24},{8,16},{16,8},{24,0},{1,25},{9,17},{17,9},{25,1},{2,26},{10... | collective-permute-start | bytes 49160 | tf_op jit(solution)/shard_map/ppermute | solution.py:500
  59.7 0.0 collective-permute-done.16.refs_6_
  59.7 2.4 %collective-permute-done.17.refs_7_ = f32[64,64]{1,0:T(8,128)S(1)} collective-permute-done((f32[64,64]{1,0:T(8,128)S(1)}, f32[64,64]{1,0:T(8,128)S(1)}, u32[]{:S(2)}, u32[]{:S(2)}) %collective-permute-start.17) | collective-permute-done | bytes 16416 | tf_op jit(solution)/shard_map/ppermute | solution.py:500
  62.1 0.0 collective-permute-done.14.refs_3_
  62.1 4.8 %mix_backward.1 = (bf16[288,256]{1,0:T(8,128)(2,1)S(1)}, f32[1024,128]{1,0:T(8,128)S(1)}) custom-call(s32[1]{0:T(128)} %bitcast.here, bf16[256,256]{1,0:T(8,128)(2,1)S(1)} %get-tuple-element.39.refs_0_, bf16[256,256]{1,0:T(8,128)(2,1)S(1)} %collective-permute-done.12.refs_1_, bf16[256,256]{1,0:T(8,128)(2,1)S(1)} %collective-permute-done.13.refs_2_, ...), custom_call_target="tpu_custom_call" | custom-call | flops 67108864 | bytes 8912896 | tf_op jit(solution)/shard_map/mix_backward/pallas_call | solution.py:87
  66.9 1.3 %collective-permute-start.18 = (bf16[288,256]{1,0:T(8,128)(2,1)S(1)}, bf16[288,256]{1,0:T(8,128)(2,1)S(1)}, u32[]{:S(2)}, u32[]{:S(2)}) collective-permute-start(bf16[288,256]{1,0:T(8,128)(2,1)S(1)} %get-tuple-element.44.refs_0_), channel_id=1, source_target_pairs={{0,2},{1,3},{2,0},{3,1},{4,6},{5,7},{6,4},{7,5},{8,10},{9,11},{10,... | collective-permute-start | bytes 442376 | tf_op jit(solution)/shard_map/ppermute | solution.py:530
  68.2 0.9 %collective-permute-start.19 = (bf16[288,256]{1,0:T(8,128)(2,1)S(1)}, bf16[288,256]{1,0:T(8,128)(2,1)S(1)}, u32[]{:S(2)}, u32[]{:S(2)}) collective-permute-start(bf16[288,256]{1,0:T(8,128)(2,1)S(1)} %get-tuple-element.44.refs_0_), channel_id=1, source_target_pairs={{0,4},{1,5},{2,6},{3,7},{4,0},{5,1},{6,2},{7,3},{8,12},{9,13},{10,... | collective-permute-start | bytes 442376 | tf_op jit(solution)/shard_map/ppermute | solution.py:530
  69.1 1.3 %collective-permute-start.20 = (bf16[288,256]{1,0:T(8,128)(2,1)S(1)}, bf16[288,256]{1,0:T(8,128)(2,1)S(1)}, u32[]{:S(2)}, u32[]{:S(2)}) collective-permute-start(bf16[288,256]{1,0:T(8,128)(2,1)S(1)} %get-tuple-element.44.refs_0_), channel_id=1, source_target_pairs={{0,6},{1,7},{2,4},{3,5},{4,2},{5,3},{6,0},{7,1},{8,14},{9,15},{10,... | collective-permute-start | bytes 442376 | tf_op jit(solution)/shard_map/ppermute | solution.py:530
  70.4 4.1 %gram.2.refs_0_ = f32[4,4,32,64,128]{4,3,2,1,0:T(8,128)} custom-call(s32[1]{0:T(128)} %bitcast.here, bf16[1024,256]{1,0:T(8,128)(2,1)S(1)} %get-tuple-element.45.spread_ref, f32[1024,128]{1,0:T(8,128)S(1)} %get-tuple-element.46.pair_ref), custom_call_target="tpu_custom_call" | custom-call | flops 33554432 | bytes 8388608 | tf_op jit(solution)/shard_map/gram/pallas_call | solution.py:87
  74.6 0.5 collective-permute-done.20.refs_3_
  75.1 0.0 collective-permute-start.22
  75.2 0.5 collective-permute-start.23
  75.6 0.0 collective-permute-start.24
  75.7 4.1 %gram.3 = f32[4,4,32,64,128]{4,3,2,1,0:T(8,128)} custom-call(s32[1]{0:T(128)} %bitcast.here, bf16[1024,256]{1,0:T(8,128)(2,1)S(1)} %get-tuple-element.45.spread_ref, f32[1024,128]{1,0:T(8,128)S(1)} %get-tuple-element.46.pair_ref, f32[4,4,32,64,128]{4,3,2,1,0:T(8,128)} %gram.2.refs_0_), custom_call_target="tpu_custom_call", output_to_operand_aliasing={{}: (3, {})} | custom-call | flops 33554432 | bytes 8388608 | tf_op jit(solution)/shard_map/gram/pallas_call | solution.py:87
  79.8 0.0 collective-permute-done.21.refs_4_
  79.8 0.0 collective-permute-done.22.refs_5_
  79.9 7.3 %last.1 = (bf16[32,256,256]{2,1,0:T(8,128)(2,1)}, f32[64,64]{1,0:T(8,128)}) custom-call(s32[1]{0:T(128)} %bitcast.here, bf16[288,256]{1,0:T(8,128)(2,1)S(1)} %get-tuple-element.44.refs_0_, bf16[288,256]{1,0:T(8,128)(2,1)S(1)} %collective-permute-done.18.refs_1_, bf16[288,256]{1,0:T(8,128)(2,1)S(1)} %collective-permute-done.19.refs_2_, ...), custom_call_target="tpu_custom_call" | custom-call | flops 1342177280 | bytes 9437184 | tf_op jit(solution)/shard_map/last/pallas_call | solution.py:87
  (19 shorter events, 0.0 us)
Async XLA Ops:
  0.6 0.8 copy-start
  4.6 2.1 %collective-permute-start = (bf16[4,256,256]{2,1,0:T(8,128)(2,1)S(1)}, bf16[4,256,256]{2,1,0:T(8,128)(2,1)S(1)}, u32[]{:S(2)}, u32[]{:S(2)}) collective-permute-start(bf16[4,256,256]{2,1,0:T(8,128)(2,1)S(1)} %get-tuple-element.30), channel_id=1, source_target_pairs={{0,1},{1,0},{2,3},{3,2},{4,5},{5,4},{6,7},{7,6},{8,9},{9,8},{10,11... | collective-permute-start | bytes 1572872 | tf_op jit(solution)/shard_map/ppermute | solution.py:421
  8.1 6.8 %collective-permute-start.1 = (bf16[256,256]{1,0:T(8,128)(2,1)S(1)}, bf16[256,256]{1,0:T(8,128)(2,1)S(1)}, u32[]{:S(2)}, u32[]{:S(2)}) collective-permute-start(bf16[256,256]{1,0:T(8,128)(2,1)S(1)} %get-tuple-element.32), channel_id=1, source_target_pairs={{0,2},{1,3},{2,0},{3,1},{4,6},{5,7},{6,4},{7,5},{8,10},{9,11},{10,... | collective-permute-start | bytes 393224 | tf_op jit(solution)/shard_map/ppermute | solution.py:440
  11.0 8.1 %collective-permute-start.2 = (bf16[256,256]{1,0:T(8,128)(2,1)S(1)}, bf16[256,256]{1,0:T(8,128)(2,1)S(1)}, u32[]{:S(2)}, u32[]{:S(2)}) collective-permute-start(bf16[256,256]{1,0:T(8,128)(2,1)S(1)} %get-tuple-element.33), channel_id=1, source_target_pairs={{0,4},{1,5},{2,6},{3,7},{4,0},{5,1},{6,2},{7,3},{8,12},{9,13},{10,... | collective-permute-start | bytes 393224 | tf_op jit(solution)/shard_map/ppermute | solution.py:440
  12.5 6.5 %collective-permute-start.3 = (bf16[256,256]{1,0:T(8,128)(2,1)S(1)}, bf16[256,256]{1,0:T(8,128)(2,1)S(1)}, u32[]{:S(2)}, u32[]{:S(2)}) collective-permute-start(bf16[256,256]{1,0:T(8,128)(2,1)S(1)} %get-tuple-element.34), channel_id=1, source_target_pairs={{0,6},{1,7},{2,4},{3,5},{4,2},{5,3},{6,0},{7,1},{8,14},{9,15},{10,... | collective-permute-start | bytes 393224 | tf_op jit(solution)/shard_map/ppermute | solution.py:440
  19.1 14.1 %copy-start.2 = (bf16[64,64]{1,0:T(8,128)(2,1)S(1)}, bf16[64,64]{1,0:T(8,128)(2,1)}, u32[]{:S(2)}) copy-start(bf16[64,64]{1,0:T(8,128)(2,1)} %refs_10_.3) | copy-start | bytes 24580
  19.1 14.1 %copy-start.3 = (bf16[64,256]{1,0:T(8,128)(2,1)S(1)}, bf16[64,256]{1,0:T(8,128)(2,1)}, u32[]{:S(2)}) copy-start(bf16[64,256]{1,0:T(8,128)(2,1)} %constant.15.clone.refs_9_) | copy-start | bytes 98308
  23.1 6.0 %collective-permute-start.4 = (bf16[256,256]{1,0:T(8,128)(2,1)S(1)}, bf16[256,256]{1,0:T(8,128)(2,1)S(1)}, u32[]{:S(2)}, u32[]{:S(2)}) collective-permute-start(bf16[256,256]{1,0:T(8,128)(2,1)S(1)} %get-tuple-element.35.refs_0_), channel_id=1, source_target_pairs={{0,2},{1,3},{2,0},{3,1},{4,6},{5,7},{6,4},{7,5},{8,10},{9,11},{10,... | collective-permute-start | bytes 393224 | tf_op jit(solution)/shard_map/ppermute | solution.py:443
  24.4 7.2 %collective-permute-start.5 = (bf16[256,256]{1,0:T(8,128)(2,1)S(1)}, bf16[256,256]{1,0:T(8,128)(2,1)S(1)}, u32[]{:S(2)}, u32[]{:S(2)}) collective-permute-start(bf16[256,256]{1,0:T(8,128)(2,1)S(1)} %get-tuple-element.35.refs_0_), channel_id=1, source_target_pairs={{0,4},{1,5},{2,6},{3,7},{4,0},{5,1},{6,2},{7,3},{8,12},{9,13},{10,... | collective-permute-start | bytes 393224 | tf_op jit(solution)/shard_map/ppermute | solution.py:443
  25.2 6.4 %collective-permute-start.6 = (bf16[256,256]{1,0:T(8,128)(2,1)S(1)}, bf16[256,256]{1,0:T(8,128)(2,1)S(1)}, u32[]{:S(2)}, u32[]{:S(2)}) collective-permute-start(bf16[256,256]{1,0:T(8,128)(2,1)S(1)} %get-tuple-element.35.refs_0_), channel_id=1, source_target_pairs={{0,6},{1,7},{2,4},{3,5},{4,2},{5,3},{6,0},{7,1},{8,14},{9,15},{10,... | collective-permute-start | bytes 393224 | tf_op jit(solution)/shard_map/ppermute | solution.py:443
  26.7 5.5 %collective-permute-start.7 = (bf16[256,256]{1,0:T(8,128)(2,1)S(1)}, bf16[256,256]{1,0:T(8,128)(2,1)S(1)}, u32[]{:S(2)}, u32[]{:S(2)}) collective-permute-start(bf16[256,256]{1,0:T(8,128)(2,1)S(1)} %get-tuple-element.35.refs_0_), channel_id=1, source_target_pairs={{0,1},{1,0},{2,3},{3,2},{4,5},{5,4},{6,7},{7,6},{8,9},{9,8},{10,11... | collective-permute-start | bytes 393224 | tf_op jit(solution)/shard_map/ppermute | solution.py:444
  29.2 3.0 %collective-permute-start.8 = (bf16[256,256]{1,0:T(8,128)(2,1)S(1)}, bf16[256,256]{1,0:T(8,128)(2,1)S(1)}, u32[]{:S(2)}, u32[]{:S(2)}) collective-permute-start(bf16[256,256]{1,0:T(8,128)(2,1)S(1)} %collective-permute-done.4.refs_1_), channel_id=1, source_target_pairs={{0,1},{1,0},{2,3},{3,2},{4,5},{5,4},{6,7},{7,6},{8,9},{9,8},{10,11... | collective-permute-start | bytes 393224 | tf_op jit(solution)/shard_map/ppermute | solution.py:444
  31.7 1.3 %collective-permute-start.9 = (bf16[256,256]{1,0:T(8,128)(2,1)S(1)}, bf16[256,256]{1,0:T(8,128)(2,1)S(1)}, u32[]{:S(2)}, u32[]{:S(2)}) collective-permute-start(bf16[256,256]{1,0:T(8,128)(2,1)S(1)} %collective-permute-done.5.refs_2_), channel_id=1, source_target_pairs={{0,1},{1,0},{2,3},{3,2},{4,5},{5,4},{6,7},{7,6},{8,9},{9,8},{10,11... | collective-permute-start | bytes 393224 | tf_op jit(solution)/shard_map/ppermute | solution.py:444
  31.7 1.5 %collective-permute-start.10 = (bf16[256,256]{1,0:T(8,128)(2,1)S(1)}, bf16[256,256]{1,0:T(8,128)(2,1)S(1)}, u32[]{:S(2)}, u32[]{:S(2)}) collective-permute-start(bf16[256,256]{1,0:T(8,128)(2,1)S(1)} %collective-permute-done.6.refs_3_), channel_id=1, source_target_pairs={{0,1},{1,0},{2,3},{3,2},{4,5},{5,4},{6,7},{7,6},{8,9},{9,8},{10,11... | collective-permute-start | bytes 393224 | tf_op jit(solution)/shard_map/ppermute | solution.py:444
  45.1 2.1 %collective-permute-start.11 = (bf16[4,256,256]{2,1,0:T(8,128)(2,1)}, bf16[4,256,256]{2,1,0:T(8,128)(2,1)S(1)}, u32[]{:S(2)}, u32[]{:S(2)}) collective-permute-start(bf16[4,256,256]{2,1,0:T(8,128)(2,1)} %get-tuple-element.38), channel_id=1, source_target_pairs={{0,1},{1,0},{2,3},{3,2},{4,5},{5,4},{6,7},{7,6},{8,9},{9,8},{10,11... | collective-permute-start | bytes 1572872 | tf_op jit(solution)/shard_map/ppermute | solution.py:421
  48.7 13.4 %collective-permute-start.12 = (bf16[256,256]{1,0:T(8,128)(2,1)S(1)}, bf16[256,256]{1,0:T(8,128)(2,1)S(1)}, u32[]{:S(2)}, u32[]{:S(2)}) collective-permute-start(bf16[256,256]{1,0:T(8,128)(2,1)S(1)} %get-tuple-element.40), channel_id=1, source_target_pairs={{0,2},{1,3},{2,0},{3,1},{4,6},{5,7},{6,4},{7,5},{8,10},{9,11},{10,... | collective-permute-start | bytes 393224 | tf_op jit(solution)/shard_map/ppermute | solution.py:440
  50.0 12.1 %collective-permute-start.13 = (bf16[256,256]{1,0:T(8,128)(2,1)S(1)}, bf16[256,256]{1,0:T(8,128)(2,1)S(1)}, u32[]{:S(2)}, u32[]{:S(2)}) collective-permute-start(bf16[256,256]{1,0:T(8,128)(2,1)S(1)} %get-tuple-element.41), channel_id=1, source_target_pairs={{0,4},{1,5},{2,6},{3,7},{4,0},{5,1},{6,2},{7,3},{8,12},{9,13},{10,... | collective-permute-start | bytes 393224 | tf_op jit(solution)/shard_map/ppermute | solution.py:440
  50.9 11.2 %collective-permute-start.14 = (bf16[256,256]{1,0:T(8,128)(2,1)S(1)}, bf16[256,256]{1,0:T(8,128)(2,1)S(1)}, u32[]{:S(2)}, u32[]{:S(2)}) collective-permute-start(bf16[256,256]{1,0:T(8,128)(2,1)S(1)} %get-tuple-element.42), channel_id=1, source_target_pairs={{0,6},{1,7},{2,4},{3,5},{4,2},{5,3},{6,0},{7,1},{8,14},{9,15},{10,... | collective-permute-start | bytes 393224 | tf_op jit(solution)/shard_map/ppermute | solution.py:440
  52.2 4.1 %collective-permute-start.15 = (f32[64,64]{1,0:T(8,128)S(1)}, f32[64,64]{1,0:T(8,128)S(1)}, u32[]{:S(2)}, u32[]{:S(2)}) collective-permute-start(f32[64,64]{1,0:T(8,128)S(1)} %get-tuple-element.43.refs_4_), channel_id=1, source_target_pairs={{0,8},{8,0},{16,24},{24,16},{1,9},{9,1},{17,25},{25,17},{2,10},{10... | collective-permute-start | bytes 49160 | tf_op jit(solution)/shard_map/ppermute | solution.py:500
  53.8 5.9 %collective-permute-start.16 = (f32[64,64]{1,0:T(8,128)S(1)}, f32[64,64]{1,0:T(8,128)S(1)}, u32[]{:S(2)}, u32[]{:S(2)}) collective-permute-start(f32[64,64]{1,0:T(8,128)S(1)} %get-tuple-element.43.refs_4_), channel_id=1, source_target_pairs={{0,16},{8,24},{16,0},{24,8},{1,17},{9,25},{17,1},{25,9},{2,18},{10... | collective-permute-start | bytes 49160 | tf_op jit(solution)/shard_map/ppermute | solution.py:500
  56.4 5.7 %collective-permute-start.17 = (f32[64,64]{1,0:T(8,128)S(1)}, f32[64,64]{1,0:T(8,128)S(1)}, u32[]{:S(2)}, u32[]{:S(2)}) collective-permute-start(f32[64,64]{1,0:T(8,128)S(1)} %get-tuple-element.43.refs_4_), channel_id=1, source_target_pairs={{0,24},{8,16},{16,8},{24,0},{1,25},{9,17},{17,9},{25,1},{2,26},{10... | collective-permute-start | bytes 49160 | tf_op jit(solution)/shard_map/ppermute | solution.py:500
  66.9 7.7 %collective-permute-start.18 = (bf16[288,256]{1,0:T(8,128)(2,1)S(1)}, bf16[288,256]{1,0:T(8,128)(2,1)S(1)}, u32[]{:S(2)}, u32[]{:S(2)}) collective-permute-start(bf16[288,256]{1,0:T(8,128)(2,1)S(1)} %get-tuple-element.44.refs_0_), channel_id=1, source_target_pairs={{0,2},{1,3},{2,0},{3,1},{4,6},{5,7},{6,4},{7,5},{8,10},{9,11},{10,... | collective-permute-start | bytes 442376 | tf_op jit(solution)/shard_map/ppermute | solution.py:530
  68.2 6.4 %collective-permute-start.19 = (bf16[288,256]{1,0:T(8,128)(2,1)S(1)}, bf16[288,256]{1,0:T(8,128)(2,1)S(1)}, u32[]{:S(2)}, u32[]{:S(2)}) collective-permute-start(bf16[288,256]{1,0:T(8,128)(2,1)S(1)} %get-tuple-element.44.refs_0_), channel_id=1, source_target_pairs={{0,4},{1,5},{2,6},{3,7},{4,0},{5,1},{6,2},{7,3},{8,12},{9,13},{10,... | collective-permute-start | bytes 442376 | tf_op jit(solution)/shard_map/ppermute | solution.py:530
  69.1 6.0 %collective-permute-start.20 = (bf16[288,256]{1,0:T(8,128)(2,1)S(1)}, bf16[288,256]{1,0:T(8,128)(2,1)S(1)}, u32[]{:S(2)}, u32[]{:S(2)}) collective-permute-start(bf16[288,256]{1,0:T(8,128)(2,1)S(1)} %get-tuple-element.44.refs_0_), channel_id=1, source_target_pairs={{0,6},{1,7},{2,4},{3,5},{4,2},{5,3},{6,0},{7,1},{8,14},{9,15},{10,... | collective-permute-start | bytes 442376 | tf_op jit(solution)/shard_map/ppermute | solution.py:530
  70.4 9.4 %collective-permute-start.21 = (bf16[288,256]{1,0:T(8,128)(2,1)S(1)}, bf16[288,256]{1,0:T(8,128)(2,1)S(1)}, u32[]{:S(2)}, u32[]{:S(2)}) collective-permute-start(bf16[288,256]{1,0:T(8,128)(2,1)S(1)} %get-tuple-element.44.refs_0_), channel_id=1, source_target_pairs={{0,1},{1,0},{2,3},{3,2},{4,5},{5,4},{6,7},{7,6},{8,9},{9,8},{10,11... | collective-permute-start | bytes 442376 | tf_op jit(solution)/shard_map/ppermute | solution.py:533
  74.6 5.3 %copy-start.1 = (bf16[64,256]{1,0:T(8,128)(2,1)S(1)}, bf16[64,256]{1,0:T(8,128)(2,1)}, u32[]{:S(2)}) copy-start(bf16[64,256]{1,0:T(8,128)(2,1)} %constant.12.clone.table_ref.refs_9_) | copy-start | bytes 98308
  75.1 4.7 %collective-permute-start.22 = (bf16[288,256]{1,0:T(8,128)(2,1)S(1)}, bf16[288,256]{1,0:T(8,128)(2,1)S(1)}, u32[]{:S(2)}, u32[]{:S(2)}) collective-permute-start(bf16[288,256]{1,0:T(8,128)(2,1)S(1)} %collective-permute-done.18.refs_1_), channel_id=1, source_target_pairs={{0,1},{1,0},{2,3},{3,2},{4,5},{5,4},{6,7},{7,6},{8,9},{9,8},{10,11... | collective-permute-start | bytes 442376 | tf_op jit(solution)/shard_map/ppermute | solution.py:533
  75.2 4.7 %collective-permute-start.23 = (bf16[288,256]{1,0:T(8,128)(2,1)S(1)}, bf16[288,256]{1,0:T(8,128)(2,1)S(1)}, u32[]{:S(2)}, u32[]{:S(2)}) collective-permute-start(bf16[288,256]{1,0:T(8,128)(2,1)S(1)} %collective-permute-done.19.refs_2_), channel_id=1, source_target_pairs={{0,1},{1,0},{2,3},{3,2},{4,5},{5,4},{6,7},{7,6},{8,9},{9,8},{10,11... | collective-permute-start | bytes 442376 | tf_op jit(solution)/shard_map/ppermute | solution.py:533
  75.6 4.2 %collective-permute-start.24 = (bf16[288,256]{1,0:T(8,128)(2,1)S(1)}, bf16[288,256]{1,0:T(8,128)(2,1)S(1)}, u32[]{:S(2)}, u32[]{:S(2)}) collective-permute-start(bf16[288,256]{1,0:T(8,128)(2,1)S(1)} %collective-permute-done.20.refs_3_), channel_id=1, source_target_pairs={{0,1},{1,0},{2,3},{3,2},{4,5},{5,4},{6,7},{7,6},{8,9},{9,8},{10,11... | collective-permute-start | bytes 442376 | tf_op jit(solution)/shard_map/ppermute | solution.py:533

commit v3 on v2

--- a/solution.py
+++ b/solution.py
@@ -83,7 +83,7 @@
     return pl.BlockSpec(shape, lambda *_: zeros)
 
 
-def call(kernel, here, operands, grid, in_specs, out_specs, out_shape, scratch=(), flops=0, moved=0, name=None, aliases=None):
+def call(kernel, here, operands, grid, in_specs, out_specs, out_shape, scratch=(), flops=0, moved=0, name=None, aliases=None, limit=VMEM):
     return pl.pallas_call(
         kernel,
         out_shape=out_shape,
@@ -95,7 +95,7 @@
             scratch_shapes=list(scratch),
         ),
         compiler_params=pltpu.CompilerParams(
-            dimension_semantics=("arbitrary",) * len(grid), vmem_limit_bytes=VMEM
+            dimension_semantics=("arbitrary",) * len(grid), vmem_limit_bytes=limit
         ),
         cost_estimate=pl.CostEstimate(flops=flops, bytes_accessed=moved, transcendentals=0),
         name=name,
@@ -277,14 +277,6 @@
     return jnp.transpose(joined).astype(BF16)
 
 
-def block_mixing(weight, zs):
-    rows = jnp.concatenate([weight] * zs, 1)
-    full = jnp.concatenate([rows] * zs, 0)
-    row = lax.broadcasted_iota(jnp.int32, full.shape, 0) // 64
-    lane = lax.broadcasted_iota(jnp.int32, full.shape, 1) // 64
-    return jnp.where(row == lane, full, 0.0).astype(BF16)
-
-
 def middle(count, here, *refs):
     blocks, rest = refs[:count], refs[count:]
     x_ref, y_ref, weight_ref, field_ref, cot_ref = rest[:5]
@@ -297,7 +289,7 @@
     @pl.when(step == 0)
     def _():
         grid_rows(here, blocks, x_ref, rows)
-        mixing[...] = block_mixing(jnp.transpose(weight_ref[...].astype(F32)), zs)
+        mixing[...] = jnp.transpose(weight_ref[...].astype(F32)).astype(BF16)
         acc[...] = jnp.zeros_like(acc)
 
     table = y_ref[...]
@@ -316,7 +308,7 @@
     for x in range(size):
         for at in range(0, columns, 64):
             part = slice(at, at + 64)
-            p = dot(lefts[x][part], table) + dot(mixing[part, :], field_ref[x])
+            p = dot(lefts[x][part], table) + dot(mixing[...], field_ref[x, part])
             square = p * p
             t = jnp.tanh(p * (ROOT + ROOT * CUBE * square))
             half = 0.5 + 0.5 * t
@@ -341,7 +333,7 @@
 
 def last(count, scale, here, *refs):
     blocks, rest = refs[:count], refs[count:]
-    x_ref, y_ref, weight_ref, grad_ref, out_ref, local_ref, rows, mixing = rest
+    x_ref, y_ref, weight_ref, grad_ref, out_ref, local_ref, rows = rest
     columns = grad_ref.shape[1]
     size = grad_ref.shape[0]
 
@@ -350,7 +342,6 @@
         height = x_ref.shape[2]
         extra = 64 * 64 // columns
         grid_rows(here, [block.at[pl.ds(0, height)] for block in blocks], x_ref, rows)
-        mixing[...] = block_mixing(weight_ref[...].astype(F32), columns // 64)
         parts = [
             block[pl.ds(height, extra), :].astype(F32) + block[pl.ds(height + extra, extra), :].astype(F32)
             for block in blocks
@@ -361,11 +352,12 @@
             local_ref[at * extra : (at + 1) * extra, :] = parts[0][:, at * 64 : (at + 1) * 64] * scale
 
     table = y_ref[...]
+    weight = weight_ref[...]
     lefts = [row_at(rows, size, x) for x in range(size)]
     for x in range(size):
         for at in range(0, columns, 64):
             part = slice(at, at + 64)
-            value = dot(lefts[x][part], table) + dot(mixing[part, :], grad_ref[x])
+            value = dot(lefts[x][part], table) + dot(weight, grad_ref[x, part])
             out_ref[x, part] = value.astype(BF16)
 
 
@@ -410,7 +402,7 @@
     mode_spec = whole((2 * modes, columns))
     weight_small = whole((channels, channels))
     small_shape = jax.ShapeDtypeStruct((channels, channels), F32)
-    mixing_scratch = pltpu.VMEM((columns, columns), BF16)
+    mixing_scratch = pltpu.VMEM((channels, channels), BF16)
     extra = 2 * channels * channels // columns
     back_spec = whole((2 * modes + extra, columns))
     back_shape = jax.ShapeDtypeStruct((2 * modes + extra, columns), BF16)
@@ -436,6 +428,7 @@
             flops=8 * chips * modes * rows_here * unit * columns,
             moved=mode_bytes * 3 * chips,
             name="forward_x",
+            limit=8 << 20,
         )
         return [outs[0]] + [flip("mp", count, 2 * bit)(outs[bit]) for bit in range(1, chips)]
 
@@ -497,13 +490,17 @@
         name="middle",
     )
     terms = to_chips(keep, send)
-    locals_ = [local_term] + [flip("dp", dp_count, bit)(local_term) for bit in range(1, dp_count)]
+    bit = 1
+    while 2 * bit < dp_count:
+        local_term = local_term + flip("dp", dp_count, bit)(local_term)
+        bit *= 2
+    locals_ = [local_term] + ([flip("dp", dp_count, bit)(local_term)] if bit < dp_count else [])
     back, pairs = call(
         functools.partial(mix_backward, chips, zs),
         here,
         (*terms, *locals_, spectral_weight),
         (mode_steps,),
-        [mode_spec] * chips + [weight_small] * dp_count + [weight_spec],
+        [mode_spec] * chips + [weight_small] * len(locals_) + [weight_spec],
         [back_spec, whole(pair_shape)],
         [back_shape, jax.ShapeDtypeStruct(pair_shape, F32)],
         [pltpu.VMEM((zs // 2, modes * 2 * zs, 128), F32)] + weight_scratch,
@@ -541,7 +538,7 @@
         [back_spec] * count + [x_back_spec, y_spec, weight_small, field_spec(wide)],
         [field_spec(wide), weight_small],
         [field_shape, small_shape],
-        [rows_scratch, mixing_scratch],
+        [rows_scratch],
         flops=field_bytes * (2 * KY + columns),
         moved=field_bytes * 2 + mode_bytes * count,
         name="last",

time: 87.5 us -> 82.7 us (0.945)
  Pallas kernels: 42.4 us -> 38.7 us
  starting transfers between devices: 24.5 us -> 21.2 us
  waiting for transfers between devices: 18.8 us -> 20.9 us
    ppermute x3 -> x1, starting transfers between devices: 7.48 us -> 2.59 us  [body(): flip('dp', dp_count, bit)(local_term)]
    pallas_call x9, Pallas kernels: 42.4 us -> 38.7 us  [call(): pl.pallas_call(kernel, out_shape=out_shape, grid_spec=pltpu.PrefetchScala...]
    ppermute x0 -> x1, waiting for transfers between devices: none -> 2.34 us  [body(): local_term = local_term + flip('dp', dp_count, bit)(local_term)]
    ppermute x0 -> x1, starting transfers between devices: none -> 1.58 us  [body(): local_term = local_term + flip('dp', dp_count, bit)(local_term)]
    ppermute x3 -> x1, waiting for transfers between devices: 2.37 us -> 2.22 us  [body(): flip('dp', dp_count, bit)(local_term)]
  transfers between devices with their start and end apart: 25 -> 24, of which waited for: 10 -> 11; matrix products, arithmetic and copies ran while one was open for 0% -> 0% of each run, Pallas kernels for 10% -> 10%
where the time goes in v3:
time: 82.7 us; the launch traced here: 82.5 us
  Pallas kernels  38.7 us (47%)
  starting transfers between devices  21.2 us (26%)
  waiting for transfers between devices  20.9 us (25%)
  local copies, waits for them, and re-layouts  0.86 us (1%)
    pallas_call x9, Pallas kernels, call(): pl.pallas_call(kernel, out_shape=out_shape, grid_spec=pltpu.PrefetchScala...  38.7 us
    ppermute x6, starting transfers between devices, to_chips(): flip('mp', count, 2 * bit)(outs[bit])  8.01 us
    ppermute x6, waiting for transfers between devices, to_chips(): flip('mp', count, 2 * bit)(outs[bit])  6.53 us
    ppermute x3, waiting for transfers between devices, to_all(): flip('mp', count, 2 * bit)(block)  4.95 us
    ppermute x3, starting transfers between devices, to_all(): flip('mp', count, 2 * bit)(block)  3.55 us
    ppermute x3, starting transfers between devices, body(): flip('mp', count, 2 * bit)(back)  3.55 us
    ppermute x2, waiting for transfers between devices, to_chips(): got = flip('mp', count, 1)(send)  3.32 us
    ppermute x1, starting transfers between devices, body(): flip('dp', dp_count, bit)(local_term)  2.59 us
  transfers between devices with their start and end apart: 24, of which 11 were waited for; matrix products, arithmetic and copies ran while one was open for 0% of the time, Pallas kernels for 10%

profile of v3, /device:TPU:0, one launch (start us, length us, event | category | flops | bytes accessed | tf_op | source)
XLA Modules:
  0.0 82.5 jit_solution(15944700239517483427)
XLA Ops:
  0.6 0.0 copy-start
  0.6 0.0 copy-start.1
  0.7 0.8 %copy-done.1 = bf16[64,256]{1,0:T(8,128)(2,1)S(1)} copy-done((bf16[64,256]{1,0:T(8,128)(2,1)S(1)}, bf16[64,256]{1,0:T(8,128)(2,1)}, u32[]{:S(2)}) %copy-start.1) | copy-done | bytes 32792
  1.5 3.2 %forward_y.1 = (bf16[4,256,256]{2,1,0:T(8,128)(2,1)S(1)}, bf16[4,256,256]{2,1,0:T(8,128)(2,1)S(1)}) custom-call(s32[1]{0:T(128)} %bitcast.here, bf16[32,256,256]{2,1,0:T(8,128)(2,1)} %bitcast.17, bf16[64,256]{1,0:T(8,128)(2,1)S(1)} %copy-done.1), custom_call_target="tpu_custom_call" | custom-call | flops 268435456 | bytes 5242880 | tf_op jit(solution)/shard_map/forward_y/pallas_call | solution.py:87
  4.7 0.5 collective-permute-start
  5.2 1.5 %collective-permute-done.got_ref = bf16[4,256,256]{2,1,0:T(8,128)(2,1)S(1)} collective-permute-done((bf16[4,256,256]{2,1,0:T(8,128)(2,1)S(1)}, bf16[4,256,256]{2,1,0:T(8,128)(2,1)S(1)}, u32[]{:S(2)}, u32[]{:S(2)}) %collective-permute-start) | collective-permute-done | bytes 524320 | tf_op jit(solution)/shard_map/ppermute | solution.py:413
  6.8 0.5 forward_x.2
  7.2 2.9 %collective-permute-start.1 = (bf16[256,256]{1,0:T(8,128)(2,1)S(1)}, bf16[256,256]{1,0:T(8,128)(2,1)S(1)}, u32[]{:S(2)}, u32[]{:S(2)}) collective-permute-start(bf16[256,256]{1,0:T(8,128)(2,1)S(1)} %get-tuple-element.32), channel_id=1, source_target_pairs={{0,2},{1,3},{2,0},{3,1},{4,6},{5,7},{6,4},{7,5},{8,10},{9,11},{10,... | collective-permute-start | bytes 393224 | tf_op jit(solution)/shard_map/ppermute | solution.py:433
  10.2 1.5 %collective-permute-start.2 = (bf16[256,256]{1,0:T(8,128)(2,1)S(1)}, bf16[256,256]{1,0:T(8,128)(2,1)S(1)}, u32[]{:S(2)}, u32[]{:S(2)}) collective-permute-start(bf16[256,256]{1,0:T(8,128)(2,1)S(1)} %get-tuple-element.33), channel_id=1, source_target_pairs={{0,4},{1,5},{2,6},{3,7},{4,0},{5,1},{6,2},{7,3},{8,12},{9,13},{10,... | collective-permute-start | bytes 393224 | tf_op jit(solution)/shard_map/ppermute | solution.py:433
  11.7 0.0 collective-permute-start.3
  11.7 2.4 %collective-permute-done.1.refs_1_ = bf16[256,256]{1,0:T(8,128)(2,1)S(1)} collective-permute-done((bf16[256,256]{1,0:T(8,128)(2,1)S(1)}, bf16[256,256]{1,0:T(8,128)(2,1)S(1)}, u32[]{:S(2)}, u32[]{:S(2)}) %collective-permute-start.1) | collective-permute-done | bytes 131104 | tf_op jit(solution)/shard_map/ppermute | solution.py:433
  14.1 4.2 %collective-permute-done.2.refs_2_ = bf16[256,256]{1,0:T(8,128)(2,1)S(1)} collective-permute-done((bf16[256,256]{1,0:T(8,128)(2,1)S(1)}, bf16[256,256]{1,0:T(8,128)(2,1)S(1)}, u32[]{:S(2)}, u32[]{:S(2)}) %collective-permute-start.2) | collective-permute-done | bytes 131104 | tf_op jit(solution)/shard_map/ppermute | solution.py:433
  18.2 0.0 collective-permute-done.3.refs_3_
  18.2 4.0 %mix_forward.1 = (bf16[256,256]{1,0:T(8,128)(2,1)S(1)}, bf16[1024,256]{1,0:T(8,128)(2,1)S(1)}) custom-call(s32[1]{0:T(128)} %bitcast.here, bf16[256,256]{1,0:T(8,128)(2,1)S(1)} %get-tuple-element.31.refs_0_, bf16[256,256]{1,0:T(8,128)(2,1)S(1)} %collective-permute-done.1.refs_1_, bf16[256,256]{1,0:T(8,128)(2,1)S(1)} %collective-permute-done.2.refs_2_, ...), custom_call_target="tpu_custom_call" | custom-call | flops 67108864 | bytes 8912896 | tf_op jit(solution)/shard_map/mix_forward/pallas_call | solution.py:87
  22.3 1.3 %collective-permute-start.4 = (bf16[256,256]{1,0:T(8,128)(2,1)S(1)}, bf16[256,256]{1,0:T(8,128)(2,1)S(1)}, u32[]{:S(2)}, u32[]{:S(2)}) collective-permute-start(bf16[256,256]{1,0:T(8,128)(2,1)S(1)} %get-tuple-element.35.refs_0_), channel_id=1, source_target_pairs={{0,2},{1,3},{2,0},{3,1},{4,6},{5,7},{6,4},{7,5},{8,10},{9,11},{10,... | collective-permute-start | bytes 393224 | tf_op jit(solution)/shard_map/ppermute | solution.py:436
  23.6 0.8 %collective-permute-start.5 = (bf16[256,256]{1,0:T(8,128)(2,1)S(1)}, bf16[256,256]{1,0:T(8,128)(2,1)S(1)}, u32[]{:S(2)}, u32[]{:S(2)}) collective-permute-start(bf16[256,256]{1,0:T(8,128)(2,1)S(1)} %get-tuple-element.35.refs_0_), channel_id=1, source_target_pairs={{0,4},{1,5},{2,6},{3,7},{4,0},{5,1},{6,2},{7,3},{8,12},{9,13},{10,... | collective-permute-start | bytes 393224 | tf_op jit(solution)/shard_map/ppermute | solution.py:436
  24.4 1.4 %collective-permute-start.6 = (bf16[256,256]{1,0:T(8,128)(2,1)S(1)}, bf16[256,256]{1,0:T(8,128)(2,1)S(1)}, u32[]{:S(2)}, u32[]{:S(2)}) collective-permute-start(bf16[256,256]{1,0:T(8,128)(2,1)S(1)} %get-tuple-element.35.refs_0_), channel_id=1, source_target_pairs={{0,6},{1,7},{2,4},{3,5},{4,2},{5,3},{6,0},{7,1},{8,14},{9,15},{10,... | collective-permute-start | bytes 393224 | tf_op jit(solution)/shard_map/ppermute | solution.py:436
  25.8 0.0 collective-permute-start.7
  25.8 2.5 %collective-permute-done.4.refs_1_ = bf16[256,256]{1,0:T(8,128)(2,1)S(1)} collective-permute-done((bf16[256,256]{1,0:T(8,128)(2,1)S(1)}, bf16[256,256]{1,0:T(8,128)(2,1)S(1)}, u32[]{:S(2)}, u32[]{:S(2)}) %collective-permute-start.4) | collective-permute-done | bytes 131104 | tf_op jit(solution)/shard_map/ppermute | solution.py:436
  28.3 0.0 collective-permute-start.8
  28.3 2.5 %collective-permute-done.5.refs_2_ = bf16[256,256]{1,0:T(8,128)(2,1)S(1)} collective-permute-done((bf16[256,256]{1,0:T(8,128)(2,1)S(1)}, bf16[256,256]{1,0:T(8,128)(2,1)S(1)}, u32[]{:S(2)}, u32[]{:S(2)}) %collective-permute-start.5) | collective-permute-done | bytes 131104 | tf_op jit(solution)/shard_map/ppermute | solution.py:436
  30.8 0.0 collective-permute-start.9
  30.8 0.5 collective-permute-start.10
  31.3 0.8 %collective-permute-done.9.refs_6_ = bf16[256,256]{1,0:T(8,128)(2,1)S(1)} collective-permute-done((bf16[256,256]{1,0:T(8,128)(2,1)S(1)}, bf16[256,256]{1,0:T(8,128)(2,1)S(1)}, u32[]{:S(2)}, u32[]{:S(2)}) %collective-permute-start.9) | collective-permute-done | bytes 131104 | tf_op jit(solution)/shard_map/ppermute | solution.py:437
  32.1 0.2 collective-permute-done.10.refs_7_
  32.3 11.5 %middle.1 = (bf16[32,256,256]{2,1,0:T(8,128)(2,1)}, bf16[32,256,256]{2,1,0:T(8,128)(2,1)}, bf16[4,256,256]{2,1,0:T(8,128)(2,1)S(1)}, bf16[4,256,256]{2,1,0:T(8,128)(2,1)}, f32[64,64]{1,0:T(8,128)S(1)}) custom-call(s32[1]{0:T(128)} %bitcast.here, bf16[256,256]{1,0:T(8,128)(2,1)S(1)} %get-tuple-element.35.refs_0_, ...), custom_call_target="tpu_custom_call" | custom-call | flops 2684354560 | bytes 18874368 | tf_op jit(solution)/shard_map/middle/pallas_call | solution.py:87
  43.8 0.3 collective-permute-start.11
  44.1 1.8 %collective-permute-done.11.got_ref = bf16[4,256,256]{2,1,0:T(8,128)(2,1)S(1)} collective-permute-done((bf16[4,256,256]{2,1,0:T(8,128)(2,1)}, bf16[4,256,256]{2,1,0:T(8,128)(2,1)S(1)}, u32[]{:S(2)}, u32[]{:S(2)}) %collective-permute-start.11) | collective-permute-done | bytes 524320 | tf_op jit(solution)/shard_map/ppermute | solution.py:413
  45.9 0.4 forward_x.3
  46.4 1.3 %collective-permute-start.12 = (bf16[256,256]{1,0:T(8,128)(2,1)S(1)}, bf16[256,256]{1,0:T(8,128)(2,1)S(1)}, u32[]{:S(2)}, u32[]{:S(2)}) collective-permute-start(bf16[256,256]{1,0:T(8,128)(2,1)S(1)} %get-tuple-element.40), channel_id=1, source_target_pairs={{0,2},{1,3},{2,0},{3,1},{4,6},{5,7},{6,4},{7,5},{8,10},{9,11},{10,... | collective-permute-start | bytes 393224 | tf_op jit(solution)/shard_map/ppermute | solution.py:433
  47.7 0.9 %collective-permute-start.13 = (bf16[256,256]{1,0:T(8,128)(2,1)S(1)}, bf16[256,256]{1,0:T(8,128)(2,1)S(1)}, u32[]{:S(2)}, u32[]{:S(2)}) collective-permute-start(bf16[256,256]{1,0:T(8,128)(2,1)S(1)} %get-tuple-element.41), channel_id=1, source_target_pairs={{0,4},{1,5},{2,6},{3,7},{4,0},{5,1},{6,2},{7,3},{8,12},{9,13},{10,... | collective-permute-start | bytes 393224 | tf_op jit(solution)/shard_map/ppermute | solution.py:433
  48.6 1.3 %collective-permute-start.14 = (bf16[256,256]{1,0:T(8,128)(2,1)S(1)}, bf16[256,256]{1,0:T(8,128)(2,1)S(1)}, u32[]{:S(2)}, u32[]{:S(2)}) collective-permute-start(bf16[256,256]{1,0:T(8,128)(2,1)S(1)} %get-tuple-element.42), channel_id=1, source_target_pairs={{0,6},{1,7},{2,4},{3,5},{4,2},{5,3},{6,0},{7,1},{8,14},{9,15},{10,... | collective-permute-start | bytes 393224 | tf_op jit(solution)/shard_map/ppermute | solution.py:433
  49.9 1.6 %collective-permute-start.15 = (f32[64,64]{1,0:T(8,128)S(1)}, f32[64,64]{1,0:T(8,128)S(1)}, u32[]{:S(2)}, u32[]{:S(2)}) collective-permute-start(f32[64,64]{1,0:T(8,128)S(1)} %get-tuple-element.43), channel_id=1, source_target_pairs={{0,8},{8,0},{16,24},{24,16},{1,9},{9,1},{17,25},{25,17},{2,10},{10... | collective-permute-start | bytes 49160 | tf_op jit(solution)/shard_map/ppermute | solution.py:495
  51.5 2.3 %collective-permute-done.15 = f32[64,64]{1,0:T(8,128)S(1)} collective-permute-done((f32[64,64]{1,0:T(8,128)S(1)}, f32[64,64]{1,0:T(8,128)S(1)}, u32[]{:S(2)}, u32[]{:S(2)}) %collective-permute-start.15) | collective-permute-done | bytes 16416 | tf_op jit(solution)/shard_map/ppermute | solution.py:495
  53.8 2.6 %collective-permute-start.16 = (f32[64,64]{1,0:T(8,128)S(1)}, f32[64,64]{1,0:T(8,128)S(1)}, u32[]{:S(2)}, u32[]{:S(2)}) collective-permute-start(f32[64,64]{1,0:T(8,128)S(1)} %add.3.refs_4_), channel_id=1, source_target_pairs={{0,16},{8,24},{16,0},{24,8},{1,17},{9,25},{17,1},{25,9},{2,18},{10... | collective-permute-start | bytes 49160 | tf_op jit(solution)/shard_map/ppermute | solution.py:497
  56.4 2.2 %collective-permute-done.16.refs_5_ = f32[64,64]{1,0:T(8,128)S(1)} collective-permute-done((f32[64,64]{1,0:T(8,128)S(1)}, f32[64,64]{1,0:T(8,128)S(1)}, u32[]{:S(2)}, u32[]{:S(2)}) %collective-permute-start.16) | collective-permute-done | bytes 16416 | tf_op jit(solution)/shard_map/ppermute | solution.py:497
  58.7 0.0 collective-permute-done.12.refs_1_
  58.7 4.8 %mix_backward.1 = (bf16[288,256]{1,0:T(8,128)(2,1)S(1)}, f32[1024,128]{1,0:T(8,128)S(1)}) custom-call(s32[1]{0:T(128)} %bitcast.here, bf16[256,256]{1,0:T(8,128)(2,1)S(1)} %get-tuple-element.39.refs_0_, bf16[256,256]{1,0:T(8,128)(2,1)S(1)} %collective-permute-done.12.refs_1_, bf16[256,256]{1,0:T(8,128)(2,1)S(1)} %collective-permute-done.13.refs_2_, ...), custom_call_target="tpu_custom_call" | custom-call | flops 67108864 | bytes 8912896 | tf_op jit(solution)/shard_map/mix_backward/pallas_call | solution.py:87
  63.5 1.3 %collective-permute-start.17 = (bf16[288,256]{1,0:T(8,128)(2,1)S(1)}, bf16[288,256]{1,0:T(8,128)(2,1)S(1)}, u32[]{:S(2)}, u32[]{:S(2)}) collective-permute-start(bf16[288,256]{1,0:T(8,128)(2,1)S(1)} %get-tuple-element.44.refs_0_), channel_id=1, source_target_pairs={{0,2},{1,3},{2,0},{3,1},{4,6},{5,7},{6,4},{7,5},{8,10},{9,11},{10,... | collective-permute-start | bytes 442376 | tf_op jit(solution)/shard_map/ppermute | solution.py:527
  64.8 0.9 %collective-permute-start.18 = (bf16[288,256]{1,0:T(8,128)(2,1)S(1)}, bf16[288,256]{1,0:T(8,128)(2,1)S(1)}, u32[]{:S(2)}, u32[]{:S(2)}) collective-permute-start(bf16[288,256]{1,0:T(8,128)(2,1)S(1)} %get-tuple-element.44.refs_0_), channel_id=1, source_target_pairs={{0,4},{1,5},{2,6},{3,7},{4,0},{5,1},{6,2},{7,3},{8,12},{9,13},{10,... | collective-permute-start | bytes 442376 | tf_op jit(solution)/shard_map/ppermute | solution.py:527
  65.7 1.3 %collective-permute-start.19 = (bf16[288,256]{1,0:T(8,128)(2,1)S(1)}, bf16[288,256]{1,0:T(8,128)(2,1)S(1)}, u32[]{:S(2)}, u32[]{:S(2)}) collective-permute-start(bf16[288,256]{1,0:T(8,128)(2,1)S(1)} %get-tuple-element.44.refs_0_), channel_id=1, source_target_pairs={{0,6},{1,7},{2,4},{3,5},{4,2},{5,3},{6,0},{7,1},{8,14},{9,15},{10,... | collective-permute-start | bytes 442376 | tf_op jit(solution)/shard_map/ppermute | solution.py:527
  67.0 4.1 %gram.2.refs_0_ = f32[4,4,32,64,128]{4,3,2,1,0:T(8,128)} custom-call(s32[1]{0:T(128)} %bitcast.here, bf16[1024,256]{1,0:T(8,128)(2,1)S(1)} %get-tuple-element.45.spread_ref, f32[1024,128]{1,0:T(8,128)S(1)} %get-tuple-element.46.pair_ref), custom_call_target="tpu_custom_call" | custom-call | flops 33554432 | bytes 8388608 | tf_op jit(solution)/shard_map/gram/pallas_call | solution.py:87
  71.2 0.5 collective-permute-done.19.refs_3_
  71.7 0.0 collective-permute-start.21
  71.8 0.5 collective-permute-start.22
  72.2 0.0 collective-permute-start.23
  72.3 4.1 %gram.3 = f32[4,4,32,64,128]{4,3,2,1,0:T(8,128)} custom-call(s32[1]{0:T(128)} %bitcast.here, bf16[1024,256]{1,0:T(8,128)(2,1)S(1)} %get-tuple-element.45.spread_ref, f32[1024,128]{1,0:T(8,128)S(1)} %get-tuple-element.46.pair_ref, f32[4,4,32,64,128]{4,3,2,1,0:T(8,128)} %gram.2.refs_0_), custom_call_target="tpu_custom_call", output_to_operand_aliasing={{}: (3, {})} | custom-call | flops 33554432 | bytes 8388608 | tf_op jit(solution)/shard_map/gram/pallas_call | solution.py:87
  76.4 6.1 %last.1 = (bf16[32,256,256]{2,1,0:T(8,128)(2,1)}, f32[64,64]{1,0:T(8,128)}) custom-call(s32[1]{0:T(128)} %bitcast.here, bf16[288,256]{1,0:T(8,128)(2,1)S(1)} %get-tuple-element.44.refs_0_, bf16[288,256]{1,0:T(8,128)(2,1)S(1)} %collective-permute-done.17.refs_1_, bf16[288,256]{1,0:T(8,128)(2,1)S(1)} %collective-permute-done.18.refs_2_, ...), custom_call_target="tpu_custom_call" | custom-call | flops 1342177280 | bytes 9437184 | tf_op jit(solution)/shard_map/last/pallas_call | solution.py:87
  (20 shorter events, 0.1 us)
Async XLA Ops:
  0.6 6.1 %copy-start = (bf16[8,256,256]{2,1,0:T(8,128)(2,1)S(1)}, bf16[8,256,256]{2,1,0:T(8,128)(2,1)}, u32[]{:S(2)}) copy-start(bf16[8,256,256]{2,1,0:T(8,128)(2,1)} %constant.13.clone.own_ref.other_ref) | copy-start | bytes 3145732
  0.6 0.8 %copy-start.1 = (bf16[64,256]{1,0:T(8,128)(2,1)S(1)}, bf16[64,256]{1,0:T(8,128)(2,1)}, u32[]{:S(2)}) copy-start(bf16[64,256]{1,0:T(8,128)(2,1)} %constant.12.clone.table_ref.refs_9_) | copy-start | bytes 98308
  4.7 2.1 %collective-permute-start = (bf16[4,256,256]{2,1,0:T(8,128)(2,1)S(1)}, bf16[4,256,256]{2,1,0:T(8,128)(2,1)S(1)}, u32[]{:S(2)}, u32[]{:S(2)}) collective-permute-start(bf16[4,256,256]{2,1,0:T(8,128)(2,1)S(1)} %get-tuple-element.30), channel_id=1, source_target_pairs={{0,1},{1,0},{2,3},{3,2},{4,5},{5,4},{6,7},{7,6},{8,9},{9,8},{10,11... | collective-permute-start | bytes 1572872 | tf_op jit(solution)/shard_map/ppermute | solution.py:413
  7.2 6.8 %collective-permute-start.1 = (bf16[256,256]{1,0:T(8,128)(2,1)S(1)}, bf16[256,256]{1,0:T(8,128)(2,1)S(1)}, u32[]{:S(2)}, u32[]{:S(2)}) collective-permute-start(bf16[256,256]{1,0:T(8,128)(2,1)S(1)} %get-tuple-element.32), channel_id=1, source_target_pairs={{0,2},{1,3},{2,0},{3,1},{4,6},{5,7},{6,4},{7,5},{8,10},{9,11},{10,... | collective-permute-start | bytes 393224 | tf_op jit(solution)/shard_map/ppermute | solution.py:433
  10.2 8.1 %collective-permute-start.2 = (bf16[256,256]{1,0:T(8,128)(2,1)S(1)}, bf16[256,256]{1,0:T(8,128)(2,1)S(1)}, u32[]{:S(2)}, u32[]{:S(2)}) collective-permute-start(bf16[256,256]{1,0:T(8,128)(2,1)S(1)} %get-tuple-element.33), channel_id=1, source_target_pairs={{0,4},{1,5},{2,6},{3,7},{4,0},{5,1},{6,2},{7,3},{8,12},{9,13},{10,... | collective-permute-start | bytes 393224 | tf_op jit(solution)/shard_map/ppermute | solution.py:433
  11.7 6.5 %collective-permute-start.3 = (bf16[256,256]{1,0:T(8,128)(2,1)S(1)}, bf16[256,256]{1,0:T(8,128)(2,1)S(1)}, u32[]{:S(2)}, u32[]{:S(2)}) collective-permute-start(bf16[256,256]{1,0:T(8,128)(2,1)S(1)} %get-tuple-element.34), channel_id=1, source_target_pairs={{0,6},{1,7},{2,4},{3,5},{4,2},{5,3},{6,0},{7,1},{8,14},{9,15},{10,... | collective-permute-start | bytes 393224 | tf_op jit(solution)/shard_map/ppermute | solution.py:433
  18.2 14.1 %copy-start.3 = (bf16[64,64]{1,0:T(8,128)(2,1)S(1)}, bf16[64,64]{1,0:T(8,128)(2,1)}, u32[]{:S(2)}) copy-start(bf16[64,64]{1,0:T(8,128)(2,1)} %refs_10_.3) | copy-start | bytes 24580
  18.2 14.1 %copy-start.4 = (bf16[64,256]{1,0:T(8,128)(2,1)S(1)}, bf16[64,256]{1,0:T(8,128)(2,1)}, u32[]{:S(2)}) copy-start(bf16[64,256]{1,0:T(8,128)(2,1)} %constant.15.clone.refs_9_) | copy-start | bytes 98308
  22.3 6.1 %collective-permute-start.4 = (bf16[256,256]{1,0:T(8,128)(2,1)S(1)}, bf16[256,256]{1,0:T(8,128)(2,1)S(1)}, u32[]{:S(2)}, u32[]{:S(2)}) collective-permute-start(bf16[256,256]{1,0:T(8,128)(2,1)S(1)} %get-tuple-element.35.refs_0_), channel_id=1, source_target_pairs={{0,2},{1,3},{2,0},{3,1},{4,6},{5,7},{6,4},{7,5},{8,10},{9,11},{10,... | collective-permute-start | bytes 393224 | tf_op jit(solution)/shard_map/ppermute | solution.py:436
  23.6 7.2 %collective-permute-start.5 = (bf16[256,256]{1,0:T(8,128)(2,1)S(1)}, bf16[256,256]{1,0:T(8,128)(2,1)S(1)}, u32[]{:S(2)}, u32[]{:S(2)}) collective-permute-start(bf16[256,256]{1,0:T(8,128)(2,1)S(1)} %get-tuple-element.35.refs_0_), channel_id=1, source_target_pairs={{0,4},{1,5},{2,6},{3,7},{4,0},{5,1},{6,2},{7,3},{8,12},{9,13},{10,... | collective-permute-start | bytes 393224 | tf_op jit(solution)/shard_map/ppermute | solution.py:436
  24.4 6.4 %collective-permute-start.6 = (bf16[256,256]{1,0:T(8,128)(2,1)S(1)}, bf16[256,256]{1,0:T(8,128)(2,1)S(1)}, u32[]{:S(2)}, u32[]{:S(2)}) collective-permute-start(bf16[256,256]{1,0:T(8,128)(2,1)S(1)} %get-tuple-element.35.refs_0_), channel_id=1, source_target_pairs={{0,6},{1,7},{2,4},{3,5},{4,2},{5,3},{6,0},{7,1},{8,14},{9,15},{10,... | collective-permute-start | bytes 393224 | tf_op jit(solution)/shard_map/ppermute | solution.py:436
  25.8 5.5 %collective-permute-start.7 = (bf16[256,256]{1,0:T(8,128)(2,1)S(1)}, bf16[256,256]{1,0:T(8,128)(2,1)S(1)}, u32[]{:S(2)}, u32[]{:S(2)}) collective-permute-start(bf16[256,256]{1,0:T(8,128)(2,1)S(1)} %get-tuple-element.35.refs_0_), channel_id=1, source_target_pairs={{0,1},{1,0},{2,3},{3,2},{4,5},{5,4},{6,7},{7,6},{8,9},{9,8},{10,11... | collective-permute-start | bytes 393224 | tf_op jit(solution)/shard_map/ppermute | solution.py:437
  28.3 3.0 %collective-permute-start.8 = (bf16[256,256]{1,0:T(8,128)(2,1)S(1)}, bf16[256,256]{1,0:T(8,128)(2,1)S(1)}, u32[]{:S(2)}, u32[]{:S(2)}) collective-permute-start(bf16[256,256]{1,0:T(8,128)(2,1)S(1)} %collective-permute-done.4.refs_1_), channel_id=1, source_target_pairs={{0,1},{1,0},{2,3},{3,2},{4,5},{5,4},{6,7},{7,6},{8,9},{9,8},{10,11... | collective-permute-start | bytes 393224 | tf_op jit(solution)/shard_map/ppermute | solution.py:437
  30.8 1.3 %collective-permute-start.9 = (bf16[256,256]{1,0:T(8,128)(2,1)S(1)}, bf16[256,256]{1,0:T(8,128)(2,1)S(1)}, u32[]{:S(2)}, u32[]{:S(2)}) collective-permute-start(bf16[256,256]{1,0:T(8,128)(2,1)S(1)} %collective-permute-done.5.refs_2_), channel_id=1, source_target_pairs={{0,1},{1,0},{2,3},{3,2},{4,5},{5,4},{6,7},{7,6},{8,9},{9,8},{10,11... | collective-permute-start | bytes 393224 | tf_op jit(solution)/shard_map/ppermute | solution.py:437
  30.8 1.5 %collective-permute-start.10 = (bf16[256,256]{1,0:T(8,128)(2,1)S(1)}, bf16[256,256]{1,0:T(8,128)(2,1)S(1)}, u32[]{:S(2)}, u32[]{:S(2)}) collective-permute-start(bf16[256,256]{1,0:T(8,128)(2,1)S(1)} %collective-permute-done.6.refs_3_), channel_id=1, source_target_pairs={{0,1},{1,0},{2,3},{3,2},{4,5},{5,4},{6,7},{7,6},{8,9},{9,8},{10,11... | collective-permute-start | bytes 393224 | tf_op jit(solution)/shard_map/ppermute | solution.py:437
  43.8 2.1 %collective-permute-start.11 = (bf16[4,256,256]{2,1,0:T(8,128)(2,1)}, bf16[4,256,256]{2,1,0:T(8,128)(2,1)S(1)}, u32[]{:S(2)}, u32[]{:S(2)}) collective-permute-start(bf16[4,256,256]{2,1,0:T(8,128)(2,1)} %get-tuple-element.38), channel_id=1, source_target_pairs={{0,1},{1,0},{2,3},{3,2},{4,5},{5,4},{6,7},{7,6},{8,9},{9,8},{10,11... | collective-permute-start | bytes 1572872 | tf_op jit(solution)/shard_map/ppermute | solution.py:413
  46.4 12.3 %collective-permute-start.12 = (bf16[256,256]{1,0:T(8,128)(2,1)S(1)}, bf16[256,256]{1,0:T(8,128)(2,1)S(1)}, u32[]{:S(2)}, u32[]{:S(2)}) collective-permute-start(bf16[256,256]{1,0:T(8,128)(2,1)S(1)} %get-tuple-element.40), channel_id=1, source_target_pairs={{0,2},{1,3},{2,0},{3,1},{4,6},{5,7},{6,4},{7,5},{8,10},{9,11},{10,... | collective-permute-start | bytes 393224 | tf_op jit(solution)/shard_map/ppermute | solution.py:433
  47.7 11.0 %collective-permute-start.13 = (bf16[256,256]{1,0:T(8,128)(2,1)S(1)}, bf16[256,256]{1,0:T(8,128)(2,1)S(1)}, u32[]{:S(2)}, u32[]{:S(2)}) collective-permute-start(bf16[256,256]{1,0:T(8,128)(2,1)S(1)} %get-tuple-element.41), channel_id=1, source_target_pairs={{0,4},{1,5},{2,6},{3,7},{4,0},{5,1},{6,2},{7,3},{8,12},{9,13},{10,... | collective-permute-start | bytes 393224 | tf_op jit(solution)/shard_map/ppermute | solution.py:433
  48.6 10.1 %collective-permute-start.14 = (bf16[256,256]{1,0:T(8,128)(2,1)S(1)}, bf16[256,256]{1,0:T(8,128)(2,1)S(1)}, u32[]{:S(2)}, u32[]{:S(2)}) collective-permute-start(bf16[256,256]{1,0:T(8,128)(2,1)S(1)} %get-tuple-element.42), channel_id=1, source_target_pairs={{0,6},{1,7},{2,4},{3,5},{4,2},{5,3},{6,0},{7,1},{8,14},{9,15},{10,... | collective-permute-start | bytes 393224 | tf_op jit(solution)/shard_map/ppermute | solution.py:433
  49.9 3.9 %collective-permute-start.15 = (f32[64,64]{1,0:T(8,128)S(1)}, f32[64,64]{1,0:T(8,128)S(1)}, u32[]{:S(2)}, u32[]{:S(2)}) collective-permute-start(f32[64,64]{1,0:T(8,128)S(1)} %get-tuple-element.43), channel_id=1, source_target_pairs={{0,8},{8,0},{16,24},{24,16},{1,9},{9,1},{17,25},{25,17},{2,10},{10... | collective-permute-start | bytes 49160 | tf_op jit(solution)/shard_map/ppermute | solution.py:495
  53.8 4.8 %collective-permute-start.16 = (f32[64,64]{1,0:T(8,128)S(1)}, f32[64,64]{1,0:T(8,128)S(1)}, u32[]{:S(2)}, u32[]{:S(2)}) collective-permute-start(f32[64,64]{1,0:T(8,128)S(1)} %add.3.refs_4_), channel_id=1, source_target_pairs={{0,16},{8,24},{16,0},{24,8},{1,17},{9,25},{17,1},{25,9},{2,18},{10... | collective-permute-start | bytes 49160 | tf_op jit(solution)/shard_map/ppermute | solution.py:497
  63.5 7.7 %collective-permute-start.17 = (bf16[288,256]{1,0:T(8,128)(2,1)S(1)}, bf16[288,256]{1,0:T(8,128)(2,1)S(1)}, u32[]{:S(2)}, u32[]{:S(2)}) collective-permute-start(bf16[288,256]{1,0:T(8,128)(2,1)S(1)} %get-tuple-element.44.refs_0_), channel_id=1, source_target_pairs={{0,2},{1,3},{2,0},{3,1},{4,6},{5,7},{6,4},{7,5},{8,10},{9,11},{10,... | collective-permute-start | bytes 442376 | tf_op jit(solution)/shard_map/ppermute | solution.py:527
  64.8 6.4 %collective-permute-start.18 = (bf16[288,256]{1,0:T(8,128)(2,1)S(1)}, bf16[288,256]{1,0:T(8,128)(2,1)S(1)}, u32[]{:S(2)}, u32[]{:S(2)}) collective-permute-start(bf16[288,256]{1,0:T(8,128)(2,1)S(1)} %get-tuple-element.44.refs_0_), channel_id=1, source_target_pairs={{0,4},{1,5},{2,6},{3,7},{4,0},{5,1},{6,2},{7,3},{8,12},{9,13},{10,... | collective-permute-start | bytes 442376 | tf_op jit(solution)/shard_map/ppermute | solution.py:527
  65.7 6.0 %collective-permute-start.19 = (bf16[288,256]{1,0:T(8,128)(2,1)S(1)}, bf16[288,256]{1,0:T(8,128)(2,1)S(1)}, u32[]{:S(2)}, u32[]{:S(2)}) collective-permute-start(bf16[288,256]{1,0:T(8,128)(2,1)S(1)} %get-tuple-element.44.refs_0_), channel_id=1, source_target_pairs={{0,6},{1,7},{2,4},{3,5},{4,2},{5,3},{6,0},{7,1},{8,14},{9,15},{10,... | collective-permute-start | bytes 442376 | tf_op jit(solution)/shard_map/ppermute | solution.py:527
  67.0 9.4 %collective-permute-start.20 = (bf16[288,256]{1,0:T(8,128)(2,1)S(1)}, bf16[288,256]{1,0:T(8,128)(2,1)S(1)}, u32[]{:S(2)}, u32[]{:S(2)}) collective-permute-start(bf16[288,256]{1,0:T(8,128)(2,1)S(1)} %get-tuple-element.44.refs_0_), channel_id=1, source_target_pairs={{0,1},{1,0},{2,3},{3,2},{4,5},{5,4},{6,7},{7,6},{8,9},{9,8},{10,11... | collective-permute-start | bytes 442376 | tf_op jit(solution)/shard_map/ppermute | solution.py:530
  71.2 5.3 %copy-start.2 = (bf16[64,256]{1,0:T(8,128)(2,1)S(1)}, bf16[64,256]{1,0:T(8,128)(2,1)}, u32[]{:S(2)}) copy-start(bf16[64,256]{1,0:T(8,128)(2,1)} %constant.12.clone.table_ref.refs_9_) | copy-start | bytes 98308
  71.7 4.7 %collective-permute-start.21 = (bf16[288,256]{1,0:T(8,128)(2,1)S(1)}, bf16[288,256]{1,0:T(8,128)(2,1)S(1)}, u32[]{:S(2)}, u32[]{:S(2)}) collective-permute-start(bf16[288,256]{1,0:T(8,128)(2,1)S(1)} %collective-permute-done.17.refs_1_), channel_id=1, source_target_pairs={{0,1},{1,0},{2,3},{3,2},{4,5},{5,4},{6,7},{7,6},{8,9},{9,8},{10,11... | collective-permute-start | bytes 442376 | tf_op jit(solution)/shard_map/ppermute | solution.py:530
  71.8 4.7 %collective-permute-start.22 = (bf16[288,256]{1,0:T(8,128)(2,1)S(1)}, bf16[288,256]{1,0:T(8,128)(2,1)S(1)}, u32[]{:S(2)}, u32[]{:S(2)}) collective-permute-start(bf16[288,256]{1,0:T(8,128)(2,1)S(1)} %collective-permute-done.18.refs_2_), channel_id=1, source_target_pairs={{0,1},{1,0},{2,3},{3,2},{4,5},{5,4},{6,7},{7,6},{8,9},{9,8},{10,11... | collective-permute-start | bytes 442376 | tf_op jit(solution)/shard_map/ppermute | solution.py:530
  72.2 4.2 %collective-permute-start.23 = (bf16[288,256]{1,0:T(8,128)(2,1)S(1)}, bf16[288,256]{1,0:T(8,128)(2,1)S(1)}, u32[]{:S(2)}, u32[]{:S(2)}) collective-permute-start(bf16[288,256]{1,0:T(8,128)(2,1)S(1)} %collective-permute-done.19.refs_3_), channel_id=1, source_target_pairs={{0,1},{1,0},{2,3},{3,2},{4,5},{5,4},{6,7},{7,6},{8,9},{9,8},{10,11... | collective-permute-start | bytes 442376 | tf_op jit(solution)/shard_map/ppermute | solution.py:530

commit v4 on v3

--- a/solution.py
+++ b/solution.py
@@ -116,9 +116,29 @@
         send_ref[chip] = jnp.concatenate([part[rows] for part in sent], 0).astype(BF16)
 
 
-def forward_y(here, field_ref, table_ref, keep_ref, send_ref):
-    table = table_ref[...]
-    parts = [dot_nt(table, field_ref[x]) for x in range(field_ref.shape[0])]
+def forward_y(count, here, field_hbm, keep_ref, send_ref, buffer, table, sem):
+    step = pl.program_id(0)
+    steps, size = buffer.shape[:2]
+
+    def copy(at):
+        return pltpu.make_async_copy(field_hbm.at[pl.ds(at * size, size)], buffer.at[at], sem.at[at])
+
+    @pl.when(step == 0)
+    def _():
+        for at in range(steps):
+            copy(at).start()
+        block = KY // count
+        row = lax.broadcasted_iota(jnp.int32, table.shape, 0)
+        y = lax.broadcasted_iota(jnp.int32, table.shape, 1)
+        core, chip = row // KY, row % KY // (2 * block)
+        k = (2 * chip + core) * block + row % block
+        turn = (k * y + row // block % 2 * (NY // 4)) % NY
+        angle = (2.0 * math.pi / NY) * turn.astype(F32)
+        table[...] = (jnp.cos(angle) * (1.0 / math.sqrt(NY))).astype(BF16)
+
+    copy(step).wait()
+    value = table[...]
+    parts = [dot_nt(value, buffer[step, x]) for x in range(size)]
     store_spectrum(here, parts, keep_ref, send_ref)
 
 
@@ -243,13 +263,22 @@
 
 
 def gram(zs, start, here, spread_ref, pair_ref, *refs):
-    out_ref = refs[-1]
-    per = out_ref.shape[2]
+    out_hbm, buffer, sem = refs[-3:]
+    step = pl.program_id(0)
+    steps, per = buffer.shape[0], buffer.shape[3]
     group = 4
     unit = 2 * zs
-    first = (start + pl.program_id(0)) * per
+    first = (start + step) * per
+    out_ref = buffer.at[step]
     shape = (group * unit, 128)
     owner = lax.broadcasted_iota(jnp.int32, shape, 0) // unit
+
+    def copy(step):
+        rows = pl.ds((start + step) * per // KX, 1)
+        return pltpu.make_async_copy(
+            buffer.at[step], out_hbm.at[:, rows, pl.ds((start + step) * per % KX, per)], sem.at[step]
+        )
+
     for at in range(0, per, group):
         base = pl.multiple_of((first + at) * unit, group * unit)
         left = jnp.transpose(spread_ref[pl.ds(base, group * unit), :].astype(F32)).astype(BF16)
@@ -258,6 +287,12 @@
         got = dot(left, right.astype(BF16))
         for t in range(group):
             out_ref[:, 0, at + t] = got[:, t * 128 : (t + 1) * 128].reshape(zs, 64, 128)
+    copy(step).start()
+
+    @pl.when(step == steps - 1)
+    def _():
+        for at in range(steps):
+            copy(at).wait()
 
 
 def grid_rows(here, blocks, x_ref, rows):
@@ -448,13 +483,18 @@
     weight_bytes = zs * modes * channels * 2 * channels * 2
 
     keep, send = call(
-        forward_y,
+        functools.partial(forward_y, count),
         here,
-        (field, y_plain),
-        (rows_here // wide,),
-        [field_spec(wide), y_spec],
-        [half_spec(wide)] * 2,
+        (field,),
+        (rows_here // chunk,),
+        [pl.BlockSpec(memory_space=pltpu.HBM)],
+        [half_spec(chunk)] * 2,
         [half_shape] * 2,
+        [
+            pltpu.VMEM((rows_here // chunk, chunk, columns, grid_y), BF16),
+            pltpu.VMEM((2 * KY, grid_y), BF16),
+            pltpu.SemaphoreType.DMA((rows_here // chunk,)),
+        ],
         flops=field_bytes * 2 * KY,
         moved=field_bytes + mode_bytes * count,
         name="forward_y",
@@ -508,16 +548,23 @@
         moved=weight_bytes + mode_bytes * chips,
         name="mix_backward",
     )
-    def gram_part(start, size, before):
-        spec = pl.BlockSpec((zs, 1, KX, channels, 2 * channels), lambda g, _: (0, g + start, 0, 0, 0))
+    gram_steps = modes // 8
+    early = gram_steps * 5 // 8
+
+    def gram_part(start, steps, before):
+        per = 8
         return call(
             functools.partial(gram, zs, start),
             here,
             (spread, pairs, *before),
-            (size,),
+            (steps,),
             [whole(spread_shape), whole(pair_shape)] + [pl.BlockSpec(memory_space=pl.ANY)] * len(before),
-            spec,
+            pl.BlockSpec(memory_space=pl.ANY),
             jax.ShapeDtypeStruct(spectral_weight.shape, F32),
+            [
+                pltpu.VMEM((steps, zs, 1, per, channels, 2 * channels), F32),
+                pltpu.SemaphoreType.DMA((steps,)),
+            ],
             flops=weight_bytes * 4,
             moved=weight_bytes,
             name="gram",
@@ -525,10 +572,10 @@
         )
 
     mine = [back] + [flip("mp", count, 2 * bit)(back) for bit in range(1, chips)]
-    spectral_grad = gram_part(0, mode_rows // 2, ())
+    spectral_grad = gram_part(0, early, ())
     *others, spectral_grad = lax.optimization_barrier((*mine[1:], spectral_grad))
     blocks = [back, *others] + [flip("mp", count, 1)(value) for value in (back, *others)]
-    spectral_grad = gram_part(mode_rows // 2, mode_rows - mode_rows // 2, (spectral_grad,))
+    spectral_grad = gram_part(early, gram_steps - early, (spectral_grad,))
     scale = 1.0 / math.sqrt(NX * NY * snaps * dp_count * zs)
     back_field, local_grad = call(
         functools.partial(last, count, scale),

time: 82.7 us -> 81.3 us (0.983)
  local copies, waits for them, and re-layouts: 0.86 us -> 0.02 us
    unnamed x10 -> x8, local copies, waits for them, and re-layouts: 0.86 us -> 0.02 us
  transfers between devices with their start and end apart: 24 -> 24, of which waited for: 11 -> 11; matrix products, arithmetic and copies ran while one was open for 0% -> 0% of each run, Pallas kernels for 10% -> 9%
where the time goes in v4:
time: 81.3 us; the launch traced here: 81.1 us
  Pallas kernels  38.1 us (47%)
  starting transfers between devices  21.7 us (27%)
  waiting for transfers between devices  20.5 us (25%)
    pallas_call x9, Pallas kernels, call(): pl.pallas_call(kernel, out_shape=out_shape, grid_spec=pltpu.PrefetchScala...  38.1 us
    ppermute x6, starting transfers between devices, to_chips(): flip('mp', count, 2 * bit)(outs[bit])  8.02 us
    ppermute x6, waiting for transfers between devices, to_chips(): flip('mp', count, 2 * bit)(outs[bit])  6.53 us
    ppermute x3, waiting for transfers between devices, to_all(): flip('mp', count, 2 * bit)(block)  4.95 us
    ppermute x3, starting transfers between devices, to_all(): flip('mp', count, 2 * bit)(block)  3.55 us
    ppermute x3, starting transfers between devices, body(): flip('mp', count, 2 * bit)(back)  3.55 us
    ppermute x2, waiting for transfers between devices, to_chips(): got = flip('mp', count, 1)(send)  3.33 us
    ppermute x1, starting transfers between devices, body(): flip('dp', dp_count, bit)(local_term)  2.59 us
  transfers between devices with their start and end apart: 24, of which 11 were waited for; matrix products, arithmetic and copies ran while one was open for 0% of the time, Pallas kernels for 9%

profile of v4, /device:TPU:0, one launch (start us, length us, event | category | flops | bytes accessed | tf_op | source)
XLA Modules:
  0.0 81.1 jit_solution(1139488836230952760)
XLA Ops:
  0.6 0.0 copy-start
  0.6 3.2 %forward_y.1 = (bf16[4,256,256]{2,1,0:T(8,128)(2,1)S(1)}, bf16[4,256,256]{2,1,0:T(8,128)(2,1)S(1)}) custom-call(s32[1]{0:T(128)} %bitcast.here, bf16[32,256,256]{2,1,0:T(8,128)(2,1)} %bitcast.17), custom_call_target="tpu_custom_call" | custom-call | flops 268435456 | bytes 5242880 | tf_op jit(solution)/shard_map/forward_y/pallas_call | solution.py:87
  3.9 0.5 collective-permute-start
  4.4 1.5 %collective-permute-done.got_ref = bf16[4,256,256]{2,1,0:T(8,128)(2,1)S(1)} collective-permute-done((bf16[4,256,256]{2,1,0:T(8,128)(2,1)S(1)}, bf16[4,256,256]{2,1,0:T(8,128)(2,1)S(1)}, u32[]{:S(2)}, u32[]{:S(2)}) %collective-permute-start) | collective-permute-done | bytes 524320 | tf_op jit(solution)/shard_map/ppermute | solution.py:448
  6.0 0.5 forward_x.2
  6.4 2.9 %collective-permute-start.1 = (bf16[256,256]{1,0:T(8,128)(2,1)S(1)}, bf16[256,256]{1,0:T(8,128)(2,1)S(1)}, u32[]{:S(2)}, u32[]{:S(2)}) collective-permute-start(bf16[256,256]{1,0:T(8,128)(2,1)S(1)} %get-tuple-element.32), channel_id=1, source_target_pairs={{0,2},{1,3},{2,0},{3,1},{4,6},{5,7},{6,4},{7,5},{8,10},{9,11},{10,... | collective-permute-start | bytes 393224 | tf_op jit(solution)/shard_map/ppermute | solution.py:468
  9.3 1.5 %collective-permute-start.2 = (bf16[256,256]{1,0:T(8,128)(2,1)S(1)}, bf16[256,256]{1,0:T(8,128)(2,1)S(1)}, u32[]{:S(2)}, u32[]{:S(2)}) collective-permute-start(bf16[256,256]{1,0:T(8,128)(2,1)S(1)} %get-tuple-element.33), channel_id=1, source_target_pairs={{0,4},{1,5},{2,6},{3,7},{4,0},{5,1},{6,2},{7,3},{8,12},{9,13},{10,... | collective-permute-start | bytes 393224 | tf_op jit(solution)/shard_map/ppermute | solution.py:468
  10.9 0.0 collective-permute-start.3
  10.9 2.3 %collective-permute-done.1.refs_1_ = bf16[256,256]{1,0:T(8,128)(2,1)S(1)} collective-permute-done((bf16[256,256]{1,0:T(8,128)(2,1)S(1)}, bf16[256,256]{1,0:T(8,128)(2,1)S(1)}, u32[]{:S(2)}, u32[]{:S(2)}) %collective-permute-start.1) | collective-permute-done | bytes 131104 | tf_op jit(solution)/shard_map/ppermute | solution.py:468
  13.2 4.2 %collective-permute-done.2.refs_2_ = bf16[256,256]{1,0:T(8,128)(2,1)S(1)} collective-permute-done((bf16[256,256]{1,0:T(8,128)(2,1)S(1)}, bf16[256,256]{1,0:T(8,128)(2,1)S(1)}, u32[]{:S(2)}, u32[]{:S(2)}) %collective-permute-start.2) | collective-permute-done | bytes 131104 | tf_op jit(solution)/shard_map/ppermute | solution.py:468
  17.4 4.0 %mix_forward.1 = (bf16[256,256]{1,0:T(8,128)(2,1)S(1)}, bf16[1024,256]{1,0:T(8,128)(2,1)S(1)}) custom-call(s32[1]{0:T(128)} %bitcast.here, bf16[256,256]{1,0:T(8,128)(2,1)S(1)} %get-tuple-element.31.refs_0_, bf16[256,256]{1,0:T(8,128)(2,1)S(1)} %collective-permute-done.1.refs_1_, bf16[256,256]{1,0:T(8,128)(2,1)S(1)} %collective-permute-done.2.refs_2_, ...), custom_call_target="tpu_custom_call" | custom-call | flops 67108864 | bytes 8912896 | tf_op jit(solution)/shard_map/mix_forward/pallas_call | solution.py:87
  21.5 1.3 %collective-permute-start.4 = (bf16[256,256]{1,0:T(8,128)(2,1)S(1)}, bf16[256,256]{1,0:T(8,128)(2,1)S(1)}, u32[]{:S(2)}, u32[]{:S(2)}) collective-permute-start(bf16[256,256]{1,0:T(8,128)(2,1)S(1)} %get-tuple-element.35.refs_0_), channel_id=1, source_target_pairs={{0,2},{1,3},{2,0},{3,1},{4,6},{5,7},{6,4},{7,5},{8,10},{9,11},{10,... | collective-permute-start | bytes 393224 | tf_op jit(solution)/shard_map/ppermute | solution.py:471
  22.7 0.8 %collective-permute-start.5 = (bf16[256,256]{1,0:T(8,128)(2,1)S(1)}, bf16[256,256]{1,0:T(8,128)(2,1)S(1)}, u32[]{:S(2)}, u32[]{:S(2)}) collective-permute-start(bf16[256,256]{1,0:T(8,128)(2,1)S(1)} %get-tuple-element.35.refs_0_), channel_id=1, source_target_pairs={{0,4},{1,5},{2,6},{3,7},{4,0},{5,1},{6,2},{7,3},{8,12},{9,13},{10,... | collective-permute-start | bytes 393224 | tf_op jit(solution)/shard_map/ppermute | solution.py:471
  23.6 1.4 %collective-permute-start.6 = (bf16[256,256]{1,0:T(8,128)(2,1)S(1)}, bf16[256,256]{1,0:T(8,128)(2,1)S(1)}, u32[]{:S(2)}, u32[]{:S(2)}) collective-permute-start(bf16[256,256]{1,0:T(8,128)(2,1)S(1)} %get-tuple-element.35.refs_0_), channel_id=1, source_target_pairs={{0,6},{1,7},{2,4},{3,5},{4,2},{5,3},{6,0},{7,1},{8,14},{9,15},{10,... | collective-permute-start | bytes 393224 | tf_op jit(solution)/shard_map/ppermute | solution.py:471
  25.0 0.0 collective-permute-start.7
  25.0 2.5 %collective-permute-done.4.refs_1_ = bf16[256,256]{1,0:T(8,128)(2,1)S(1)} collective-permute-done((bf16[256,256]{1,0:T(8,128)(2,1)S(1)}, bf16[256,256]{1,0:T(8,128)(2,1)S(1)}, u32[]{:S(2)}, u32[]{:S(2)}) %collective-permute-start.4) | collective-permute-done | bytes 131104 | tf_op jit(solution)/shard_map/ppermute | solution.py:471
  27.5 0.0 collective-permute-start.8
  27.5 2.4 %collective-permute-done.5.refs_2_ = bf16[256,256]{1,0:T(8,128)(2,1)S(1)} collective-permute-done((bf16[256,256]{1,0:T(8,128)(2,1)S(1)}, bf16[256,256]{1,0:T(8,128)(2,1)S(1)}, u32[]{:S(2)}, u32[]{:S(2)}) %collective-permute-start.5) | collective-permute-done | bytes 131104 | tf_op jit(solution)/shard_map/ppermute | solution.py:471
  30.0 0.0 collective-permute-done.6.refs_3_
  30.0 0.5 collective-permute-start.10
  30.5 0.0 collective-permute-done.7.refs_4_
  30.5 0.0 collective-permute-done.8.refs_5_
  30.5 0.8 %collective-permute-done.9.refs_6_ = bf16[256,256]{1,0:T(8,128)(2,1)S(1)} collective-permute-done((bf16[256,256]{1,0:T(8,128)(2,1)S(1)}, bf16[256,256]{1,0:T(8,128)(2,1)S(1)}, u32[]{:S(2)}, u32[]{:S(2)}) %collective-permute-start.9) | collective-permute-done | bytes 131104 | tf_op jit(solution)/shard_map/ppermute | solution.py:472
  31.3 0.2 collective-permute-done.10.refs_7_
  31.5 11.5 %middle.1 = (bf16[32,256,256]{2,1,0:T(8,128)(2,1)}, bf16[32,256,256]{2,1,0:T(8,128)(2,1)}, bf16[4,256,256]{2,1,0:T(8,128)(2,1)S(1)}, bf16[4,256,256]{2,1,0:T(8,128)(2,1)}, f32[64,64]{1,0:T(8,128)S(1)}) custom-call(s32[1]{0:T(128)} %bitcast.here, bf16[256,256]{1,0:T(8,128)(2,1)S(1)} %get-tuple-element.35.refs_0_, ...), custom_call_target="tpu_custom_call" | custom-call | flops 2684354560 | bytes 18874368 | tf_op jit(solution)/shard_map/middle/pallas_call | solution.py:87
  43.0 0.3 collective-permute-start.11
  43.3 1.8 %collective-permute-done.11.got_ref = bf16[4,256,256]{2,1,0:T(8,128)(2,1)S(1)} collective-permute-done((bf16[4,256,256]{2,1,0:T(8,128)(2,1)}, bf16[4,256,256]{2,1,0:T(8,128)(2,1)S(1)}, u32[]{:S(2)}, u32[]{:S(2)}) %collective-permute-start.11) | collective-permute-done | bytes 524320 | tf_op jit(solution)/shard_map/ppermute | solution.py:448
  45.1 0.4 forward_x.3
  45.5 1.3 %collective-permute-start.12 = (bf16[256,256]{1,0:T(8,128)(2,1)S(1)}, bf16[256,256]{1,0:T(8,128)(2,1)S(1)}, u32[]{:S(2)}, u32[]{:S(2)}) collective-permute-start(bf16[256,256]{1,0:T(8,128)(2,1)S(1)} %get-tuple-element.40), channel_id=1, source_target_pairs={{0,2},{1,3},{2,0},{3,1},{4,6},{5,7},{6,4},{7,5},{8,10},{9,11},{10,... | collective-permute-start | bytes 393224 | tf_op jit(solution)/shard_map/ppermute | solution.py:468
  46.9 0.9 %collective-permute-start.13 = (bf16[256,256]{1,0:T(8,128)(2,1)S(1)}, bf16[256,256]{1,0:T(8,128)(2,1)S(1)}, u32[]{:S(2)}, u32[]{:S(2)}) collective-permute-start(bf16[256,256]{1,0:T(8,128)(2,1)S(1)} %get-tuple-element.41), channel_id=1, source_target_pairs={{0,4},{1,5},{2,6},{3,7},{4,0},{5,1},{6,2},{7,3},{8,12},{9,13},{10,... | collective-permute-start | bytes 393224 | tf_op jit(solution)/shard_map/ppermute | solution.py:468
  47.7 1.3 %collective-permute-start.14 = (bf16[256,256]{1,0:T(8,128)(2,1)S(1)}, bf16[256,256]{1,0:T(8,128)(2,1)S(1)}, u32[]{:S(2)}, u32[]{:S(2)}) collective-permute-start(bf16[256,256]{1,0:T(8,128)(2,1)S(1)} %get-tuple-element.42), channel_id=1, source_target_pairs={{0,6},{1,7},{2,4},{3,5},{4,2},{5,3},{6,0},{7,1},{8,14},{9,15},{10,... | collective-permute-start | bytes 393224 | tf_op jit(solution)/shard_map/ppermute | solution.py:468
  49.1 1.6 %collective-permute-start.15 = (f32[64,64]{1,0:T(8,128)S(1)}, f32[64,64]{1,0:T(8,128)S(1)}, u32[]{:S(2)}, u32[]{:S(2)}) collective-permute-start(f32[64,64]{1,0:T(8,128)S(1)} %get-tuple-element.43), channel_id=1, source_target_pairs={{0,8},{8,0},{16,24},{24,16},{1,9},{9,1},{17,25},{25,17},{2,10},{10... | collective-permute-start | bytes 49160 | tf_op jit(solution)/shard_map/ppermute | solution.py:535
  50.7 2.3 %collective-permute-done.15 = f32[64,64]{1,0:T(8,128)S(1)} collective-permute-done((f32[64,64]{1,0:T(8,128)S(1)}, f32[64,64]{1,0:T(8,128)S(1)}, u32[]{:S(2)}, u32[]{:S(2)}) %collective-permute-start.15) | collective-permute-done | bytes 16416 | tf_op jit(solution)/shard_map/ppermute | solution.py:535
  53.0 2.6 %collective-permute-start.16 = (f32[64,64]{1,0:T(8,128)S(1)}, f32[64,64]{1,0:T(8,128)S(1)}, u32[]{:S(2)}, u32[]{:S(2)}) collective-permute-start(f32[64,64]{1,0:T(8,128)S(1)} %add.3.refs_4_), channel_id=1, source_target_pairs={{0,16},{8,24},{16,0},{24,8},{1,17},{9,25},{17,1},{25,9},{2,18},{10... | collective-permute-start | bytes 49160 | tf_op jit(solution)/shard_map/ppermute | solution.py:537
  55.6 2.2 %collective-permute-done.16.refs_5_ = f32[64,64]{1,0:T(8,128)S(1)} collective-permute-done((f32[64,64]{1,0:T(8,128)S(1)}, f32[64,64]{1,0:T(8,128)S(1)}, u32[]{:S(2)}, u32[]{:S(2)}) %collective-permute-start.16) | collective-permute-done | bytes 16416 | tf_op jit(solution)/shard_map/ppermute | solution.py:537
  57.8 0.0 collective-permute-done.12.refs_1_
  57.8 4.8 %mix_backward.1 = (bf16[288,256]{1,0:T(8,128)(2,1)S(1)}, f32[1024,128]{1,0:T(8,128)S(1)}) custom-call(s32[1]{0:T(128)} %bitcast.here, bf16[256,256]{1,0:T(8,128)(2,1)S(1)} %get-tuple-element.39.refs_0_, bf16[256,256]{1,0:T(8,128)(2,1)S(1)} %collective-permute-done.12.refs_1_, bf16[256,256]{1,0:T(8,128)(2,1)S(1)} %collective-permute-done.13.refs_2_, ...), custom_call_target="tpu_custom_call" | custom-call | flops 67108864 | bytes 8912896 | tf_op jit(solution)/shard_map/mix_backward/pallas_call | solution.py:87
  62.6 1.3 %collective-permute-start.17 = (bf16[288,256]{1,0:T(8,128)(2,1)S(1)}, bf16[288,256]{1,0:T(8,128)(2,1)S(1)}, u32[]{:S(2)}, u32[]{:S(2)}) collective-permute-start(bf16[288,256]{1,0:T(8,128)(2,1)S(1)} %get-tuple-element.44.refs_0_), channel_id=1, source_target_pairs={{0,2},{1,3},{2,0},{3,1},{4,6},{5,7},{6,4},{7,5},{8,10},{9,11},{10,... | collective-permute-start | bytes 442376 | tf_op jit(solution)/shard_map/ppermute | solution.py:574
  63.9 0.9 %collective-permute-start.18 = (bf16[288,256]{1,0:T(8,128)(2,1)S(1)}, bf16[288,256]{1,0:T(8,128)(2,1)S(1)}, u32[]{:S(2)}, u32[]{:S(2)}) collective-permute-start(bf16[288,256]{1,0:T(8,128)(2,1)S(1)} %get-tuple-element.44.refs_0_), channel_id=1, source_target_pairs={{0,4},{1,5},{2,6},{3,7},{4,0},{5,1},{6,2},{7,3},{8,12},{9,13},{10,... | collective-permute-start | bytes 442376 | tf_op jit(solution)/shard_map/ppermute | solution.py:574
  64.8 1.3 %collective-permute-start.19 = (bf16[288,256]{1,0:T(8,128)(2,1)S(1)}, bf16[288,256]{1,0:T(8,128)(2,1)S(1)}, u32[]{:S(2)}, u32[]{:S(2)}) collective-permute-start(bf16[288,256]{1,0:T(8,128)(2,1)S(1)} %get-tuple-element.44.refs_0_), channel_id=1, source_target_pairs={{0,6},{1,7},{2,4},{3,5},{4,2},{5,3},{6,0},{7,1},{8,14},{9,15},{10,... | collective-permute-start | bytes 442376 | tf_op jit(solution)/shard_map/ppermute | solution.py:574
  66.2 4.6 %gram.2.refs_0_ = f32[4,4,32,64,128]{4,3,2,1,0:T(8,128)} custom-call(s32[1]{0:T(128)} %bitcast.here, bf16[1024,256]{1,0:T(8,128)(2,1)S(1)} %get-tuple-element.45.spread_ref, f32[1024,128]{1,0:T(8,128)S(1)} %get-tuple-element.46.pair_ref), custom_call_target="tpu_custom_call" | custom-call | flops 33554432 | bytes 8388608 | tf_op jit(solution)/shard_map/gram/pallas_call | solution.py:87
  70.7 0.0 copy-start.2
  70.8 0.1 collective-permute-done.19.refs_3_
  70.9 0.5 collective-permute-start.21
  71.4 0.1 collective-permute-start.22
  71.4 0.4 collective-permute-start.23
  71.9 3.1 %gram.3 = f32[4,4,32,64,128]{4,3,2,1,0:T(8,128)} custom-call(s32[1]{0:T(128)} %bitcast.here, bf16[1024,256]{1,0:T(8,128)(2,1)S(1)} %get-tuple-element.45.spread_ref, f32[1024,128]{1,0:T(8,128)S(1)} %get-tuple-element.46.pair_ref, f32[4,4,32,64,128]{4,3,2,1,0:T(8,128)} %gram.2.refs_0_), custom_call_target="tpu_custom_call", output_to_operand_aliasing={{}: (3, {})} | custom-call | flops 33554432 | bytes 8388608 | tf_op jit(solution)/shard_map/gram/pallas_call | solution.py:87
  75.0 6.1 %last.1 = (bf16[32,256,256]{2,1,0:T(8,128)(2,1)}, f32[64,64]{1,0:T(8,128)}) custom-call(s32[1]{0:T(128)} %bitcast.here, bf16[288,256]{1,0:T(8,128)(2,1)S(1)} %get-tuple-element.44.refs_0_, bf16[288,256]{1,0:T(8,128)(2,1)S(1)} %collective-permute-done.17.refs_1_, bf16[288,256]{1,0:T(8,128)(2,1)S(1)} %collective-permute-done.18.refs_2_, ...), custom_call_target="tpu_custom_call" | custom-call | flops 1342177280 | bytes 9437184 | tf_op jit(solution)/shard_map/last/pallas_call | solution.py:87
  (18 shorter events, 0.0 us)
Async XLA Ops:
  0.6 5.3 %copy-start = (bf16[8,256,256]{2,1,0:T(8,128)(2,1)S(1)}, bf16[8,256,256]{2,1,0:T(8,128)(2,1)}, u32[]{:S(2)}) copy-start(bf16[8,256,256]{2,1,0:T(8,128)(2,1)} %constant.12.clone.own_ref.other_ref) | copy-start | bytes 3145732
  3.9 2.1 %collective-permute-start = (bf16[4,256,256]{2,1,0:T(8,128)(2,1)S(1)}, bf16[4,256,256]{2,1,0:T(8,128)(2,1)S(1)}, u32[]{:S(2)}, u32[]{:S(2)}) collective-permute-start(bf16[4,256,256]{2,1,0:T(8,128)(2,1)S(1)} %get-tuple-element.30), channel_id=1, source_target_pairs={{0,1},{1,0},{2,3},{3,2},{4,5},{5,4},{6,7},{7,6},{8,9},{9,8},{10,11... | collective-permute-start | bytes 1572872 | tf_op jit(solution)/shard_map/ppermute | solution.py:448
  6.4 6.8 %collective-permute-start.1 = (bf16[256,256]{1,0:T(8,128)(2,1)S(1)}, bf16[256,256]{1,0:T(8,128)(2,1)S(1)}, u32[]{:S(2)}, u32[]{:S(2)}) collective-permute-start(bf16[256,256]{1,0:T(8,128)(2,1)S(1)} %get-tuple-element.32), channel_id=1, source_target_pairs={{0,2},{1,3},{2,0},{3,1},{4,6},{5,7},{6,4},{7,5},{8,10},{9,11},{10,... | collective-permute-start | bytes 393224 | tf_op jit(solution)/shard_map/ppermute | solution.py:468
  9.3 8.1 %collective-permute-start.2 = (bf16[256,256]{1,0:T(8,128)(2,1)S(1)}, bf16[256,256]{1,0:T(8,128)(2,1)S(1)}, u32[]{:S(2)}, u32[]{:S(2)}) collective-permute-start(bf16[256,256]{1,0:T(8,128)(2,1)S(1)} %get-tuple-element.33), channel_id=1, source_target_pairs={{0,4},{1,5},{2,6},{3,7},{4,0},{5,1},{6,2},{7,3},{8,12},{9,13},{10,... | collective-permute-start | bytes 393224 | tf_op jit(solution)/shard_map/ppermute | solution.py:468
  10.9 6.5 %collective-permute-start.3 = (bf16[256,256]{1,0:T(8,128)(2,1)S(1)}, bf16[256,256]{1,0:T(8,128)(2,1)S(1)}, u32[]{:S(2)}, u32[]{:S(2)}) collective-permute-start(bf16[256,256]{1,0:T(8,128)(2,1)S(1)} %get-tuple-element.34), channel_id=1, source_target_pairs={{0,6},{1,7},{2,4},{3,5},{4,2},{5,3},{6,0},{7,1},{8,14},{9,15},{10,... | collective-permute-start | bytes 393224 | tf_op jit(solution)/shard_map/ppermute | solution.py:468
  17.4 14.1 %copy-start.1 = (bf16[64,64]{1,0:T(8,128)(2,1)S(1)}, bf16[64,64]{1,0:T(8,128)(2,1)}, u32[]{:S(2)}) copy-start(bf16[64,64]{1,0:T(8,128)(2,1)} %refs_10_.3) | copy-start | bytes 24580
  17.4 14.1 %copy-start.3 = (bf16[64,256]{1,0:T(8,128)(2,1)S(1)}, bf16[64,256]{1,0:T(8,128)(2,1)}, u32[]{:S(2)}) copy-start(bf16[64,256]{1,0:T(8,128)(2,1)} %constant.14.clone.refs_9_) | copy-start | bytes 98308
  21.5 6.1 %collective-permute-start.4 = (bf16[256,256]{1,0:T(8,128)(2,1)S(1)}, bf16[256,256]{1,0:T(8,128)(2,1)S(1)}, u32[]{:S(2)}, u32[]{:S(2)}) collective-permute-start(bf16[256,256]{1,0:T(8,128)(2,1)S(1)} %get-tuple-element.35.refs_0_), channel_id=1, source_target_pairs={{0,2},{1,3},{2,0},{3,1},{4,6},{5,7},{6,4},{7,5},{8,10},{9,11},{10,... | collective-permute-start | bytes 393224 | tf_op jit(solution)/shard_map/ppermute | solution.py:471
  22.7 7.2 %collective-permute-start.5 = (bf16[256,256]{1,0:T(8,128)(2,1)S(1)}, bf16[256,256]{1,0:T(8,128)(2,1)S(1)}, u32[]{:S(2)}, u32[]{:S(2)}) collective-permute-start(bf16[256,256]{1,0:T(8,128)(2,1)S(1)} %get-tuple-element.35.refs_0_), channel_id=1, source_target_pairs={{0,4},{1,5},{2,6},{3,7},{4,0},{5,1},{6,2},{7,3},{8,12},{9,13},{10,... | collective-permute-start | bytes 393224 | tf_op jit(solution)/shard_map/ppermute | solution.py:471
  23.6 6.4 %collective-permute-start.6 = (bf16[256,256]{1,0:T(8,128)(2,1)S(1)}, bf16[256,256]{1,0:T(8,128)(2,1)S(1)}, u32[]{:S(2)}, u32[]{:S(2)}) collective-permute-start(bf16[256,256]{1,0:T(8,128)(2,1)S(1)} %get-tuple-element.35.refs_0_), channel_id=1, source_target_pairs={{0,6},{1,7},{2,4},{3,5},{4,2},{5,3},{6,0},{7,1},{8,14},{9,15},{10,... | collective-permute-start | bytes 393224 | tf_op jit(solution)/shard_map/ppermute | solution.py:471
  25.0 5.5 %collective-permute-start.7 = (bf16[256,256]{1,0:T(8,128)(2,1)S(1)}, bf16[256,256]{1,0:T(8,128)(2,1)S(1)}, u32[]{:S(2)}, u32[]{:S(2)}) collective-permute-start(bf16[256,256]{1,0:T(8,128)(2,1)S(1)} %get-tuple-element.35.refs_0_), channel_id=1, source_target_pairs={{0,1},{1,0},{2,3},{3,2},{4,5},{5,4},{6,7},{7,6},{8,9},{9,8},{10,11... | collective-permute-start | bytes 393224 | tf_op jit(solution)/shard_map/ppermute | solution.py:472
  27.5 3.0 %collective-permute-start.8 = (bf16[256,256]{1,0:T(8,128)(2,1)S(1)}, bf16[256,256]{1,0:T(8,128)(2,1)S(1)}, u32[]{:S(2)}, u32[]{:S(2)}) collective-permute-start(bf16[256,256]{1,0:T(8,128)(2,1)S(1)} %collective-permute-done.4.refs_1_), channel_id=1, source_target_pairs={{0,1},{1,0},{2,3},{3,2},{4,5},{5,4},{6,7},{7,6},{8,9},{9,8},{10,11... | collective-permute-start | bytes 393224 | tf_op jit(solution)/shard_map/ppermute | solution.py:472
  30.0 1.3 %collective-permute-start.9 = (bf16[256,256]{1,0:T(8,128)(2,1)S(1)}, bf16[256,256]{1,0:T(8,128)(2,1)S(1)}, u32[]{:S(2)}, u32[]{:S(2)}) collective-permute-start(bf16[256,256]{1,0:T(8,128)(2,1)S(1)} %collective-permute-done.5.refs_2_), channel_id=1, source_target_pairs={{0,1},{1,0},{2,3},{3,2},{4,5},{5,4},{6,7},{7,6},{8,9},{9,8},{10,11... | collective-permute-start | bytes 393224 | tf_op jit(solution)/shard_map/ppermute | solution.py:472
  30.0 1.5 %collective-permute-start.10 = (bf16[256,256]{1,0:T(8,128)(2,1)S(1)}, bf16[256,256]{1,0:T(8,128)(2,1)S(1)}, u32[]{:S(2)}, u32[]{:S(2)}) collective-permute-start(bf16[256,256]{1,0:T(8,128)(2,1)S(1)} %collective-permute-done.6.refs_3_), channel_id=1, source_target_pairs={{0,1},{1,0},{2,3},{3,2},{4,5},{5,4},{6,7},{7,6},{8,9},{9,8},{10,11... | collective-permute-start | bytes 393224 | tf_op jit(solution)/shard_map/ppermute | solution.py:472
  43.0 2.1 %collective-permute-start.11 = (bf16[4,256,256]{2,1,0:T(8,128)(2,1)}, bf16[4,256,256]{2,1,0:T(8,128)(2,1)S(1)}, u32[]{:S(2)}, u32[]{:S(2)}) collective-permute-start(bf16[4,256,256]{2,1,0:T(8,128)(2,1)} %get-tuple-element.38), channel_id=1, source_target_pairs={{0,1},{1,0},{2,3},{3,2},{4,5},{5,4},{6,7},{7,6},{8,9},{9,8},{10,11... | collective-permute-start | bytes 1572872 | tf_op jit(solution)/shard_map/ppermute | solution.py:448
  45.5 12.3 %collective-permute-start.12 = (bf16[256,256]{1,0:T(8,128)(2,1)S(1)}, bf16[256,256]{1,0:T(8,128)(2,1)S(1)}, u32[]{:S(2)}, u32[]{:S(2)}) collective-permute-start(bf16[256,256]{1,0:T(8,128)(2,1)S(1)} %get-tuple-element.40), channel_id=1, source_target_pairs={{0,2},{1,3},{2,0},{3,1},{4,6},{5,7},{6,4},{7,5},{8,10},{9,11},{10,... | collective-permute-start | bytes 393224 | tf_op jit(solution)/shard_map/ppermute | solution.py:468
  46.9 11.0 %collective-permute-start.13 = (bf16[256,256]{1,0:T(8,128)(2,1)S(1)}, bf16[256,256]{1,0:T(8,128)(2,1)S(1)}, u32[]{:S(2)}, u32[]{:S(2)}) collective-permute-start(bf16[256,256]{1,0:T(8,128)(2,1)S(1)} %get-tuple-element.41), channel_id=1, source_target_pairs={{0,4},{1,5},{2,6},{3,7},{4,0},{5,1},{6,2},{7,3},{8,12},{9,13},{10,... | collective-permute-start | bytes 393224 | tf_op jit(solution)/shard_map/ppermute | solution.py:468
  47.7 10.1 %collective-permute-start.14 = (bf16[256,256]{1,0:T(8,128)(2,1)S(1)}, bf16[256,256]{1,0:T(8,128)(2,1)S(1)}, u32[]{:S(2)}, u32[]{:S(2)}) collective-permute-start(bf16[256,256]{1,0:T(8,128)(2,1)S(1)} %get-tuple-element.42), channel_id=1, source_target_pairs={{0,6},{1,7},{2,4},{3,5},{4,2},{5,3},{6,0},{7,1},{8,14},{9,15},{10,... | collective-permute-start | bytes 393224 | tf_op jit(solution)/shard_map/ppermute | solution.py:468
  49.1 3.9 %collective-permute-start.15 = (f32[64,64]{1,0:T(8,128)S(1)}, f32[64,64]{1,0:T(8,128)S(1)}, u32[]{:S(2)}, u32[]{:S(2)}) collective-permute-start(f32[64,64]{1,0:T(8,128)S(1)} %get-tuple-element.43), channel_id=1, source_target_pairs={{0,8},{8,0},{16,24},{24,16},{1,9},{9,1},{17,25},{25,17},{2,10},{10... | collective-permute-start | bytes 49160 | tf_op jit(solution)/shard_map/ppermute | solution.py:535
  53.0 4.8 %collective-permute-start.16 = (f32[64,64]{1,0:T(8,128)S(1)}, f32[64,64]{1,0:T(8,128)S(1)}, u32[]{:S(2)}, u32[]{:S(2)}) collective-permute-start(f32[64,64]{1,0:T(8,128)S(1)} %add.3.refs_4_), channel_id=1, source_target_pairs={{0,16},{8,24},{16,0},{24,8},{1,17},{9,25},{17,1},{25,9},{2,18},{10... | collective-permute-start | bytes 49160 | tf_op jit(solution)/shard_map/ppermute | solution.py:537
  62.6 8.1 %collective-permute-start.17 = (bf16[288,256]{1,0:T(8,128)(2,1)S(1)}, bf16[288,256]{1,0:T(8,128)(2,1)S(1)}, u32[]{:S(2)}, u32[]{:S(2)}) collective-permute-start(bf16[288,256]{1,0:T(8,128)(2,1)S(1)} %get-tuple-element.44.refs_0_), channel_id=1, source_target_pairs={{0,2},{1,3},{2,0},{3,1},{4,6},{5,7},{6,4},{7,5},{8,10},{9,11},{10,... | collective-permute-start | bytes 442376 | tf_op jit(solution)/shard_map/ppermute | solution.py:574
  63.9 6.8 %collective-permute-start.18 = (bf16[288,256]{1,0:T(8,128)(2,1)S(1)}, bf16[288,256]{1,0:T(8,128)(2,1)S(1)}, u32[]{:S(2)}, u32[]{:S(2)}) collective-permute-start(bf16[288,256]{1,0:T(8,128)(2,1)S(1)} %get-tuple-element.44.refs_0_), channel_id=1, source_target_pairs={{0,4},{1,5},{2,6},{3,7},{4,0},{5,1},{6,2},{7,3},{8,12},{9,13},{10,... | collective-permute-start | bytes 442376 | tf_op jit(solution)/shard_map/ppermute | solution.py:574
  64.8 6.0 %collective-permute-start.19 = (bf16[288,256]{1,0:T(8,128)(2,1)S(1)}, bf16[288,256]{1,0:T(8,128)(2,1)S(1)}, u32[]{:S(2)}, u32[]{:S(2)}) collective-permute-start(bf16[288,256]{1,0:T(8,128)(2,1)S(1)} %get-tuple-element.44.refs_0_), channel_id=1, source_target_pairs={{0,6},{1,7},{2,4},{3,5},{4,2},{5,3},{6,0},{7,1},{8,14},{9,15},{10,... | collective-permute-start | bytes 442376 | tf_op jit(solution)/shard_map/ppermute | solution.py:574
  66.2 8.8 %collective-permute-start.20 = (bf16[288,256]{1,0:T(8,128)(2,1)S(1)}, bf16[288,256]{1,0:T(8,128)(2,1)S(1)}, u32[]{:S(2)}, u32[]{:S(2)}) collective-permute-start(bf16[288,256]{1,0:T(8,128)(2,1)S(1)} %get-tuple-element.44.refs_0_), channel_id=1, source_target_pairs={{0,1},{1,0},{2,3},{3,2},{4,5},{5,4},{6,7},{7,6},{8,9},{9,8},{10,11... | collective-permute-start | bytes 442376 | tf_op jit(solution)/shard_map/ppermute | solution.py:577
  70.7 4.3 %copy-start.2 = (bf16[64,256]{1,0:T(8,128)(2,1)S(1)}, bf16[64,256]{1,0:T(8,128)(2,1)}, u32[]{:S(2)}) copy-start(bf16[64,256]{1,0:T(8,128)(2,1)} %constant.15.clone.refs_9_) | copy-start | bytes 98308
  70.9 4.1 %collective-permute-start.21 = (bf16[288,256]{1,0:T(8,128)(2,1)S(1)}, bf16[288,256]{1,0:T(8,128)(2,1)S(1)}, u32[]{:S(2)}, u32[]{:S(2)}) collective-permute-start(bf16[288,256]{1,0:T(8,128)(2,1)S(1)} %collective-permute-done.17.refs_1_), channel_id=1, source_target_pairs={{0,1},{1,0},{2,3},{3,2},{4,5},{5,4},{6,7},{7,6},{8,9},{9,8},{10,11... | collective-permute-start | bytes 442376 | tf_op jit(solution)/shard_map/ppermute | solution.py:577
  71.4 3.7 %collective-permute-start.22 = (bf16[288,256]{1,0:T(8,128)(2,1)S(1)}, bf16[288,256]{1,0:T(8,128)(2,1)S(1)}, u32[]{:S(2)}, u32[]{:S(2)}) collective-permute-start(bf16[288,256]{1,0:T(8,128)(2,1)S(1)} %collective-permute-done.18.refs_2_), channel_id=1, source_target_pairs={{0,1},{1,0},{2,3},{3,2},{4,5},{5,4},{6,7},{7,6},{8,9},{9,8},{10,11... | collective-permute-start | bytes 442376 | tf_op jit(solution)/shard_map/ppermute | solution.py:577
  71.4 3.6 %collective-permute-start.23 = (bf16[288,256]{1,0:T(8,128)(2,1)S(1)}, bf16[288,256]{1,0:T(8,128)(2,1)S(1)}, u32[]{:S(2)}, u32[]{:S(2)}) collective-permute-start(bf16[288,256]{1,0:T(8,128)(2,1)S(1)} %collective-permute-done.19.refs_3_), channel_id=1, source_target_pairs={{0,1},{1,0},{2,3},{3,2},{4,5},{5,4},{6,7},{7,6},{8,9},{9,8},{10,11... | collective-permute-start | bytes 442376 | tf_op jit(solution)/shard_map/ppermute | solution.py:577

commit v5 on v4

--- a/solution.py
+++ b/solution.py
@@ -444,7 +444,7 @@
     field_bytes = rows_here * columns * grid_y * 2
     mode_bytes = 4 * modes * columns
 
-    def to_chips(keep, send):
+    def to_chips(keep, send, beside=None):
         got = flip("mp", count, 1)(send)
         x_spec = (1, 2 * modes, rows_here * unit)
         outs = call(
@@ -465,7 +465,10 @@
             name="forward_x",
             limit=8 << 20,
         )
-        return [outs[0]] + [flip("mp", count, 2 * bit)(outs[bit]) for bit in range(1, chips)]
+        outs = list(outs)
+        if beside is not None:
+            outs[-1], beside = lax.optimization_barrier((outs[-1], beside))
+        return [outs[0]] + [flip("mp", count, 2 * bit)(outs[bit]) for bit in range(1, chips)], beside
 
     def to_all(block):
         mine = [block] + [flip("mp", count, 2 * bit)(block) for bit in range(1, chips)]
@@ -499,7 +502,7 @@
         moved=field_bytes + mode_bytes * count,
         name="forward_y",
     )
-    terms = to_chips(keep, send)
+    terms, _ = to_chips(keep, send)
     mixed, spread = call(
         functools.partial(mix_forward, chips, zs),
         here,
@@ -529,12 +532,13 @@
         moved=field_bytes * 4 + mode_bytes * count * 2,
         name="middle",
     )
-    terms = to_chips(keep, send)
-    bit = 1
-    while 2 * bit < dp_count:
-        local_term = local_term + flip("dp", dp_count, bit)(local_term)
+    first_got = flip("dp", dp_count, 1)(local_term) if dp_count > 1 else jnp.zeros_like(local_term)
+    terms, first_got = to_chips(keep, send, first_got)
+    locals_, bit = [local_term, first_got], 2
+    while bit < dp_count:
+        local_term = locals_[0] + locals_[1]
+        locals_ = [local_term, flip("dp", dp_count, bit)(local_term)]
         bit *= 2
-    locals_ = [local_term] + ([flip("dp", dp_count, bit)(local_term)] if bit < dp_count else [])
     back, pairs = call(
         functools.partial(mix_backward, chips, zs),
         here,

time: 81.3 us -> 79 us (0.972)
  waiting for transfers between devices: 20.5 us -> 18.6 us
    ppermute x2, waiting for transfers between devices: 4.56 us -> 2.22 us  [the longest x1 2.22 us: body(): locals_ = [local_term, flip('dp', dp_count, bit)(local_term)]]
    ppermute x2, waiting for transfers between devices: 3.33 us -> 1.75 us  [to_chips(): got = flip('mp', count, 1)(send)]
    ppermute x6, waiting for transfers between devices: 6.53 us -> 7.71 us  [to_chips(): flip('mp', count, 2 * bit)(outs[bit])]
    ppermute x3, waiting for transfers between devices: 0.1 us -> 0.96 us  [body(): flip('mp', count, 2 * bit)(back)]
  transfers between devices with their start and end apart: 24 -> 24, of which waited for: 11 -> 11; matrix products, arithmetic and copies ran while one was open for 0% -> 0% of each run, Pallas kernels for 9% -> 10%
where the time goes in v5:
time: 79 us; the launch traced here: 78.7 us
  Pallas kernels  38.1 us (48%)
  starting transfers between devices  21.2 us (27%)
  waiting for transfers between devices  18.6 us (24%)
    pallas_call x9, Pallas kernels, call(): pl.pallas_call(kernel, out_shape=out_shape, grid_spec=pltpu.PrefetchScala...  38.1 us
    ppermute x6, starting transfers between devices, to_chips(): flip('mp', count, 2 * bit)(outs[bit])  8.02 us
    ppermute x6, waiting for transfers between devices, to_chips(): flip('mp', count, 2 * bit)(outs[bit])  7.71 us
    ppermute x3, waiting for transfers between devices, to_all(): flip('mp', count, 2 * bit)(block)  4.95 us
    ppermute x3, starting transfers between devices, to_all(): flip('mp', count, 2 * bit)(block)  3.55 us
    ppermute x3, starting transfers between devices, body(): flip('mp', count, 2 * bit)(back)  3.55 us
    ppermute x1, starting transfers between devices, body(): locals_ = [local_term, flip('dp', dp_count, bit)(local_term)]  2.59 us
    ppermute x1, waiting for transfers between devices, body(): locals_ = [local_term, flip('dp', dp_count, bit)(local_term)]  2.22 us
  transfers between devices with their start and end apart: 24, of which 11 were waited for; matrix products, arithmetic and copies ran while one was open for 0% of the time, Pallas kernels for 10%

profile of v5, /device:TPU:0, one launch (start us, length us, event | category | flops | bytes accessed | tf_op | source)
XLA Modules:
  0.0 78.7 jit_solution(414599773188163894)
XLA Ops:
  0.6 0.0 copy-start
  0.6 3.2 %forward_y.1 = (bf16[4,256,256]{2,1,0:T(8,128)(2,1)S(1)}, bf16[4,256,256]{2,1,0:T(8,128)(2,1)S(1)}) custom-call(s32[1]{0:T(128)} %bitcast.here, bf16[32,256,256]{2,1,0:T(8,128)(2,1)} %bitcast.17), custom_call_target="tpu_custom_call" | custom-call | flops 268435456 | bytes 5242880 | tf_op jit(solution)/shard_map/forward_y/pallas_call | solution.py:87
  3.9 0.5 collective-permute-start
  4.4 1.5 %collective-permute-done.got_ref = bf16[4,256,256]{2,1,0:T(8,128)(2,1)S(1)} collective-permute-done((bf16[4,256,256]{2,1,0:T(8,128)(2,1)S(1)}, bf16[4,256,256]{2,1,0:T(8,128)(2,1)S(1)}, u32[]{:S(2)}, u32[]{:S(2)}) %collective-permute-start) | collective-permute-done | bytes 524320 | tf_op jit(solution)/shard_map/ppermute | solution.py:448
  6.0 0.5 forward_x.2
  6.4 2.9 %collective-permute-start.1 = (bf16[256,256]{1,0:T(8,128)(2,1)S(1)}, bf16[256,256]{1,0:T(8,128)(2,1)S(1)}, u32[]{:S(2)}, u32[]{:S(2)}) collective-permute-start(bf16[256,256]{1,0:T(8,128)(2,1)S(1)} %get-tuple-element.34), channel_id=1, source_target_pairs={{0,2},{1,3},{2,0},{3,1},{4,6},{5,7},{6,4},{7,5},{8,10},{9,11},{10,... | collective-permute-start | bytes 393224 | tf_op jit(solution)/shard_map/ppermute | solution.py:471
  9.3 1.5 %collective-permute-start.2 = (bf16[256,256]{1,0:T(8,128)(2,1)S(1)}, bf16[256,256]{1,0:T(8,128)(2,1)S(1)}, u32[]{:S(2)}, u32[]{:S(2)}) collective-permute-start(bf16[256,256]{1,0:T(8,128)(2,1)S(1)} %get-tuple-element.35), channel_id=1, source_target_pairs={{0,4},{1,5},{2,6},{3,7},{4,0},{5,1},{6,2},{7,3},{8,12},{9,13},{10,... | collective-permute-start | bytes 393224 | tf_op jit(solution)/shard_map/ppermute | solution.py:471
  10.9 0.0 collective-permute-start.3
  10.9 2.3 %collective-permute-done.1.refs_1_ = bf16[256,256]{1,0:T(8,128)(2,1)S(1)} collective-permute-done((bf16[256,256]{1,0:T(8,128)(2,1)S(1)}, bf16[256,256]{1,0:T(8,128)(2,1)S(1)}, u32[]{:S(2)}, u32[]{:S(2)}) %collective-permute-start.1) | collective-permute-done | bytes 131104 | tf_op jit(solution)/shard_map/ppermute | solution.py:471
  13.2 4.2 %collective-permute-done.2.refs_2_ = bf16[256,256]{1,0:T(8,128)(2,1)S(1)} collective-permute-done((bf16[256,256]{1,0:T(8,128)(2,1)S(1)}, bf16[256,256]{1,0:T(8,128)(2,1)S(1)}, u32[]{:S(2)}, u32[]{:S(2)}) %collective-permute-start.2) | collective-permute-done | bytes 131104 | tf_op jit(solution)/shard_map/ppermute | solution.py:471
  17.4 0.0 collective-permute-done.3.refs_3_
  17.4 4.0 %mix_forward.1 = (bf16[256,256]{1,0:T(8,128)(2,1)S(1)}, bf16[1024,256]{1,0:T(8,128)(2,1)S(1)}) custom-call(s32[1]{0:T(128)} %bitcast.here, bf16[256,256]{1,0:T(8,128)(2,1)S(1)} %get-tuple-element.33.refs_0_, bf16[256,256]{1,0:T(8,128)(2,1)S(1)} %collective-permute-done.1.refs_1_, bf16[256,256]{1,0:T(8,128)(2,1)S(1)} %collective-permute-done.2.refs_2_, ...), custom_call_target="tpu_custom_call" | custom-call | flops 67108864 | bytes 8912896 | tf_op jit(solution)/shard_map/mix_forward/pallas_call | solution.py:87
  21.5 1.3 %collective-permute-start.4 = (bf16[256,256]{1,0:T(8,128)(2,1)S(1)}, bf16[256,256]{1,0:T(8,128)(2,1)S(1)}, u32[]{:S(2)}, u32[]{:S(2)}) collective-permute-start(bf16[256,256]{1,0:T(8,128)(2,1)S(1)} %get-tuple-element.37.refs_0_), channel_id=1, source_target_pairs={{0,2},{1,3},{2,0},{3,1},{4,6},{5,7},{6,4},{7,5},{8,10},{9,11},{10,... | collective-permute-start | bytes 393224 | tf_op jit(solution)/shard_map/ppermute | solution.py:474
  22.7 0.8 %collective-permute-start.5 = (bf16[256,256]{1,0:T(8,128)(2,1)S(1)}, bf16[256,256]{1,0:T(8,128)(2,1)S(1)}, u32[]{:S(2)}, u32[]{:S(2)}) collective-permute-start(bf16[256,256]{1,0:T(8,128)(2,1)S(1)} %get-tuple-element.37.refs_0_), channel_id=1, source_target_pairs={{0,4},{1,5},{2,6},{3,7},{4,0},{5,1},{6,2},{7,3},{8,12},{9,13},{10,... | collective-permute-start | bytes 393224 | tf_op jit(solution)/shard_map/ppermute | solution.py:474
  23.6 1.4 %collective-permute-start.6 = (bf16[256,256]{1,0:T(8,128)(2,1)S(1)}, bf16[256,256]{1,0:T(8,128)(2,1)S(1)}, u32[]{:S(2)}, u32[]{:S(2)}) collective-permute-start(bf16[256,256]{1,0:T(8,128)(2,1)S(1)} %get-tuple-element.37.refs_0_), channel_id=1, source_target_pairs={{0,6},{1,7},{2,4},{3,5},{4,2},{5,3},{6,0},{7,1},{8,14},{9,15},{10,... | collective-permute-start | bytes 393224 | tf_op jit(solution)/shard_map/ppermute | solution.py:474
  25.0 0.0 collective-permute-start.7
  25.0 2.5 %collective-permute-done.4.refs_1_ = bf16[256,256]{1,0:T(8,128)(2,1)S(1)} collective-permute-done((bf16[256,256]{1,0:T(8,128)(2,1)S(1)}, bf16[256,256]{1,0:T(8,128)(2,1)S(1)}, u32[]{:S(2)}, u32[]{:S(2)}) %collective-permute-start.4) | collective-permute-done | bytes 131104 | tf_op jit(solution)/shard_map/ppermute | solution.py:474
  27.5 2.4 %collective-permute-done.5.refs_2_ = bf16[256,256]{1,0:T(8,128)(2,1)S(1)} collective-permute-done((bf16[256,256]{1,0:T(8,128)(2,1)S(1)}, bf16[256,256]{1,0:T(8,128)(2,1)S(1)}, u32[]{:S(2)}, u32[]{:S(2)}) %collective-permute-start.5) | collective-permute-done | bytes 131104 | tf_op jit(solution)/shard_map/ppermute | solution.py:474
  30.0 0.5 collective-permute-start.10
  30.5 0.0 collective-permute-done.8.refs_5_
  30.5 0.8 %collective-permute-done.9.refs_6_ = bf16[256,256]{1,0:T(8,128)(2,1)S(1)} collective-permute-done((bf16[256,256]{1,0:T(8,128)(2,1)S(1)}, bf16[256,256]{1,0:T(8,128)(2,1)S(1)}, u32[]{:S(2)}, u32[]{:S(2)}) %collective-permute-start.9) | collective-permute-done | bytes 131104 | tf_op jit(solution)/shard_map/ppermute | solution.py:475
  31.3 0.2 collective-permute-done.10.refs_7_
  31.5 11.5 %middle.1 = (bf16[32,256,256]{2,1,0:T(8,128)(2,1)}, bf16[32,256,256]{2,1,0:T(8,128)(2,1)}, bf16[4,256,256]{2,1,0:T(8,128)(2,1)S(1)}, bf16[4,256,256]{2,1,0:T(8,128)(2,1)}, f32[64,64]{1,0:T(8,128)S(1)}) custom-call(s32[1]{0:T(128)} %bitcast.here, bf16[256,256]{1,0:T(8,128)(2,1)S(1)} %get-tuple-element.37.refs_0_, ...), custom_call_target="tpu_custom_call" | custom-call | flops 2684354560 | bytes 18874368 | tf_op jit(solution)/shard_map/middle/pallas_call | solution.py:87
  43.0 0.3 collective-permute-start.11
  43.3 1.6 %collective-permute-start.14 = (f32[64,64]{1,0:T(8,128)S(1)}, f32[64,64]{1,0:T(8,128)S(1)}, u32[]{:S(2)}, u32[]{:S(2)}) collective-permute-start(f32[64,64]{1,0:T(8,128)S(1)} %get-tuple-element.45), channel_id=1, source_target_pairs={{0,8},{8,0},{16,24},{24,16},{1,9},{9,1},{17,25},{25,17},{2,10},{10... | collective-permute-start | bytes 49160 | tf_op jit(solution)/shard_map/ppermute | solution.py:535
  44.9 0.2 collective-permute-done.11.got_ref
  45.1 0.4 forward_x.3
  45.5 1.3 %collective-permute-start.12 = (bf16[256,256]{1,0:T(8,128)(2,1)S(1)}, bf16[256,256]{1,0:T(8,128)(2,1)S(1)}, u32[]{:S(2)}, u32[]{:S(2)}) collective-permute-start(bf16[256,256]{1,0:T(8,128)(2,1)S(1)} %get-tuple-element.42), channel_id=1, source_target_pairs={{0,2},{1,3},{2,0},{3,1},{4,6},{5,7},{6,4},{7,5},{8,10},{9,11},{10,... | collective-permute-start | bytes 393224 | tf_op jit(solution)/shard_map/ppermute | solution.py:471
  46.9 0.9 %collective-permute-start.13 = (bf16[256,256]{1,0:T(8,128)(2,1)S(1)}, bf16[256,256]{1,0:T(8,128)(2,1)S(1)}, u32[]{:S(2)}, u32[]{:S(2)}) collective-permute-start(bf16[256,256]{1,0:T(8,128)(2,1)S(1)} %get-tuple-element.43), channel_id=1, source_target_pairs={{0,4},{1,5},{2,6},{3,7},{4,0},{5,1},{6,2},{7,3},{8,12},{9,13},{10,... | collective-permute-start | bytes 393224 | tf_op jit(solution)/shard_map/ppermute | solution.py:471
  47.7 0.0 collective-permute-done.14
  47.8 1.3 %collective-permute-start.15 = (bf16[256,256]{1,0:T(8,128)(2,1)S(1)}, bf16[256,256]{1,0:T(8,128)(2,1)S(1)}, u32[]{:S(2)}, u32[]{:S(2)}) collective-permute-start(bf16[256,256]{1,0:T(8,128)(2,1)S(1)} %get-tuple-element.46), channel_id=1, source_target_pairs={{0,6},{1,7},{2,4},{3,5},{4,2},{5,3},{6,0},{7,1},{8,14},{9,15},{10,... | collective-permute-start | bytes 393224 | tf_op jit(solution)/shard_map/ppermute | solution.py:471
  49.1 2.6 %collective-permute-start.16 = (f32[64,64]{1,0:T(8,128)S(1)}, f32[64,64]{1,0:T(8,128)S(1)}, u32[]{:S(2)}, u32[]{:S(2)}) collective-permute-start(f32[64,64]{1,0:T(8,128)S(1)} %add.3.refs_4_), channel_id=1, source_target_pairs={{0,16},{8,24},{16,0},{24,8},{1,17},{9,25},{17,1},{25,9},{2,18},{10... | collective-permute-start | bytes 49160 | tf_op jit(solution)/shard_map/ppermute | solution.py:540
  51.7 2.2 %collective-permute-done.16.refs_5_ = f32[64,64]{1,0:T(8,128)S(1)} collective-permute-done((f32[64,64]{1,0:T(8,128)S(1)}, f32[64,64]{1,0:T(8,128)S(1)}, u32[]{:S(2)}, u32[]{:S(2)}) %collective-permute-start.16) | collective-permute-done | bytes 16416 | tf_op jit(solution)/shard_map/ppermute | solution.py:540
  53.9 1.2 %collective-permute-done.13.refs_2_ = bf16[256,256]{1,0:T(8,128)(2,1)S(1)} collective-permute-done((bf16[256,256]{1,0:T(8,128)(2,1)S(1)}, bf16[256,256]{1,0:T(8,128)(2,1)S(1)}, u32[]{:S(2)}, u32[]{:S(2)}) %collective-permute-start.13) | collective-permute-done | bytes 131104 | tf_op jit(solution)/shard_map/ppermute | solution.py:471
  55.1 0.0 collective-permute-done.15.refs_3_
  55.1 4.8 %mix_backward.1 = (bf16[288,256]{1,0:T(8,128)(2,1)S(1)}, f32[1024,128]{1,0:T(8,128)S(1)}) custom-call(s32[1]{0:T(128)} %bitcast.here, bf16[256,256]{1,0:T(8,128)(2,1)S(1)} %get-tuple-element.41.refs_0_, bf16[256,256]{1,0:T(8,128)(2,1)S(1)} %collective-permute-done.12.refs_1_, bf16[256,256]{1,0:T(8,128)(2,1)S(1)} %collective-permute-done.13.refs_2_, ...), custom_call_target="tpu_custom_call" | custom-call | flops 67108864 | bytes 8912896 | tf_op jit(solution)/shard_map/mix_backward/pallas_call | solution.py:87
  59.9 0.8 %collective-permute-start.17 = (bf16[288,256]{1,0:T(8,128)(2,1)S(1)}, bf16[288,256]{1,0:T(8,128)(2,1)S(1)}, u32[]{:S(2)}, u32[]{:S(2)}) collective-permute-start(bf16[288,256]{1,0:T(8,128)(2,1)S(1)} %get-tuple-element.48.refs_0_), channel_id=1, source_target_pairs={{0,2},{1,3},{2,0},{3,1},{4,6},{5,7},{6,4},{7,5},{8,10},{9,11},{10,... | collective-permute-start | bytes 442376 | tf_op jit(solution)/shard_map/ppermute | solution.py:578
  60.7 1.3 %collective-permute-start.18 = (bf16[288,256]{1,0:T(8,128)(2,1)S(1)}, bf16[288,256]{1,0:T(8,128)(2,1)S(1)}, u32[]{:S(2)}, u32[]{:S(2)}) collective-permute-start(bf16[288,256]{1,0:T(8,128)(2,1)S(1)} %get-tuple-element.48.refs_0_), channel_id=1, source_target_pairs={{0,4},{1,5},{2,6},{3,7},{4,0},{5,1},{6,2},{7,3},{8,12},{9,13},{10,... | collective-permute-start | bytes 442376 | tf_op jit(solution)/shard_map/ppermute | solution.py:578
  62.0 1.4 %collective-permute-start.19 = (bf16[288,256]{1,0:T(8,128)(2,1)S(1)}, bf16[288,256]{1,0:T(8,128)(2,1)S(1)}, u32[]{:S(2)}, u32[]{:S(2)}) collective-permute-start(bf16[288,256]{1,0:T(8,128)(2,1)S(1)} %get-tuple-element.48.refs_0_), channel_id=1, source_target_pairs={{0,6},{1,7},{2,4},{3,5},{4,2},{5,3},{6,0},{7,1},{8,14},{9,15},{10,... | collective-permute-start | bytes 442376 | tf_op jit(solution)/shard_map/ppermute | solution.py:578
  63.4 0.0 collective-permute-start.20
  63.4 4.6 %gram.2.refs_0_ = f32[4,4,32,64,128]{4,3,2,1,0:T(8,128)} custom-call(s32[1]{0:T(128)} %bitcast.here, bf16[1024,256]{1,0:T(8,128)(2,1)S(1)} %get-tuple-element.49.spread_ref, f32[1024,128]{1,0:T(8,128)S(1)} %get-tuple-element.50.pair_ref), custom_call_target="tpu_custom_call" | custom-call | flops 33554432 | bytes 8388608 | tf_op jit(solution)/shard_map/gram/pallas_call | solution.py:87
  68.0 0.0 copy-start.2
  68.0 0.0 collective-permute-done.17.refs_1_
  68.0 1.0 %collective-permute-done.18.refs_2_ = bf16[288,256]{1,0:T(8,128)(2,1)S(1)} collective-permute-done((bf16[288,256]{1,0:T(8,128)(2,1)S(1)}, bf16[288,256]{1,0:T(8,128)(2,1)S(1)}, u32[]{:S(2)}, u32[]{:S(2)}) %collective-permute-start.18) | collective-permute-done | bytes 147488 | tf_op jit(solution)/shard_map/ppermute | solution.py:578
  69.0 0.5 collective-permute-start.22
  69.5 0.0 collective-permute-start.23
  69.5 3.1 %gram.3 = f32[4,4,32,64,128]{4,3,2,1,0:T(8,128)} custom-call(s32[1]{0:T(128)} %bitcast.here, bf16[1024,256]{1,0:T(8,128)(2,1)S(1)} %get-tuple-element.49.spread_ref, f32[1024,128]{1,0:T(8,128)S(1)} %get-tuple-element.50.pair_ref, f32[4,4,32,64,128]{4,3,2,1,0:T(8,128)} %gram.2.refs_0_), custom_call_target="tpu_custom_call", output_to_operand_aliasing={{}: (3, {})} | custom-call | flops 33554432 | bytes 8388608 | tf_op jit(solution)/shard_map/gram/pallas_call | solution.py:87
  72.7 6.1 %last.1 = (bf16[32,256,256]{2,1,0:T(8,128)(2,1)}, f32[64,64]{1,0:T(8,128)}) custom-call(s32[1]{0:T(128)} %bitcast.here, bf16[288,256]{1,0:T(8,128)(2,1)S(1)} %get-tuple-element.48.refs_0_, bf16[288,256]{1,0:T(8,128)(2,1)S(1)} %collective-permute-done.17.refs_1_, bf16[288,256]{1,0:T(8,128)(2,1)S(1)} %collective-permute-done.18.refs_2_, ...), custom_call_target="tpu_custom_call" | custom-call | flops 1342177280 | bytes 9437184 | tf_op jit(solution)/shard_map/last/pallas_call | solution.py:87
  (18 shorter events, 0.0 us)
Async XLA Ops:
  0.6 5.3 %copy-start = (bf16[8,256,256]{2,1,0:T(8,128)(2,1)S(1)}, bf16[8,256,256]{2,1,0:T(8,128)(2,1)}, u32[]{:S(2)}) copy-start(bf16[8,256,256]{2,1,0:T(8,128)(2,1)} %constant.12.clone.own_ref.other_ref) | copy-start | bytes 3145732
  3.9 2.1 %collective-permute-start = (bf16[4,256,256]{2,1,0:T(8,128)(2,1)S(1)}, bf16[4,256,256]{2,1,0:T(8,128)(2,1)S(1)}, u32[]{:S(2)}, u32[]{:S(2)}) collective-permute-start(bf16[4,256,256]{2,1,0:T(8,128)(2,1)S(1)} %get-tuple-element.32), channel_id=1, source_target_pairs={{0,1},{1,0},{2,3},{3,2},{4,5},{5,4},{6,7},{7,6},{8,9},{9,8},{10,11... | collective-permute-start | bytes 1572872 | tf_op jit(solution)/shard_map/ppermute | solution.py:448
  6.4 6.8 %collective-permute-start.1 = (bf16[256,256]{1,0:T(8,128)(2,1)S(1)}, bf16[256,256]{1,0:T(8,128)(2,1)S(1)}, u32[]{:S(2)}, u32[]{:S(2)}) collective-permute-start(bf16[256,256]{1,0:T(8,128)(2,1)S(1)} %get-tuple-element.34), channel_id=1, source_target_pairs={{0,2},{1,3},{2,0},{3,1},{4,6},{5,7},{6,4},{7,5},{8,10},{9,11},{10,... | collective-permute-start | bytes 393224 | tf_op jit(solution)/shard_map/ppermute | solution.py:471
  9.3 8.1 %collective-permute-start.2 = (bf16[256,256]{1,0:T(8,128)(2,1)S(1)}, bf16[256,256]{1,0:T(8,128)(2,1)S(1)}, u32[]{:S(2)}, u32[]{:S(2)}) collective-permute-start(bf16[256,256]{1,0:T(8,128)(2,1)S(1)} %get-tuple-element.35), channel_id=1, source_target_pairs={{0,4},{1,5},{2,6},{3,7},{4,0},{5,1},{6,2},{7,3},{8,12},{9,13},{10,... | collective-permute-start | bytes 393224 | tf_op jit(solution)/shard_map/ppermute | solution.py:471
  10.9 6.5 %collective-permute-start.3 = (bf16[256,256]{1,0:T(8,128)(2,1)S(1)}, bf16[256,256]{1,0:T(8,128)(2,1)S(1)}, u32[]{:S(2)}, u32[]{:S(2)}) collective-permute-start(bf16[256,256]{1,0:T(8,128)(2,1)S(1)} %get-tuple-element.36), channel_id=1, source_target_pairs={{0,6},{1,7},{2,4},{3,5},{4,2},{5,3},{6,0},{7,1},{8,14},{9,15},{10,... | collective-permute-start | bytes 393224 | tf_op jit(solution)/shard_map/ppermute | solution.py:471
  17.4 14.1 %copy-start.1 = (bf16[64,64]{1,0:T(8,128)(2,1)S(1)}, bf16[64,64]{1,0:T(8,128)(2,1)}, u32[]{:S(2)}) copy-start(bf16[64,64]{1,0:T(8,128)(2,1)} %refs_10_.3) | copy-start | bytes 24580
  17.4 14.1 %copy-start.3 = (bf16[64,256]{1,0:T(8,128)(2,1)S(1)}, bf16[64,256]{1,0:T(8,128)(2,1)}, u32[]{:S(2)}) copy-start(bf16[64,256]{1,0:T(8,128)(2,1)} %constant.14.clone.refs_9_) | copy-start | bytes 98308
  21.5 6.1 %collective-permute-start.4 = (bf16[256,256]{1,0:T(8,128)(2,1)S(1)}, bf16[256,256]{1,0:T(8,128)(2,1)S(1)}, u32[]{:S(2)}, u32[]{:S(2)}) collective-permute-start(bf16[256,256]{1,0:T(8,128)(2,1)S(1)} %get-tuple-element.37.refs_0_), channel_id=1, source_target_pairs={{0,2},{1,3},{2,0},{3,1},{4,6},{5,7},{6,4},{7,5},{8,10},{9,11},{10,... | collective-permute-start | bytes 393224 | tf_op jit(solution)/shard_map/ppermute | solution.py:474
  22.7 7.2 %collective-permute-start.5 = (bf16[256,256]{1,0:T(8,128)(2,1)S(1)}, bf16[256,256]{1,0:T(8,128)(2,1)S(1)}, u32[]{:S(2)}, u32[]{:S(2)}) collective-permute-start(bf16[256,256]{1,0:T(8,128)(2,1)S(1)} %get-tuple-element.37.refs_0_), channel_id=1, source_target_pairs={{0,4},{1,5},{2,6},{3,7},{4,0},{5,1},{6,2},{7,3},{8,12},{9,13},{10,... | collective-permute-start | bytes 393224 | tf_op jit(solution)/shard_map/ppermute | solution.py:474
  23.6 6.4 %collective-permute-start.6 = (bf16[256,256]{1,0:T(8,128)(2,1)S(1)}, bf16[256,256]{1,0:T(8,128)(2,1)S(1)}, u32[]{:S(2)}, u32[]{:S(2)}) collective-permute-start(bf16[256,256]{1,0:T(8,128)(2,1)S(1)} %get-tuple-element.37.refs_0_), channel_id=1, source_target_pairs={{0,6},{1,7},{2,4},{3,5},{4,2},{5,3},{6,0},{7,1},{8,14},{9,15},{10,... | collective-permute-start | bytes 393224 | tf_op jit(solution)/shard_map/ppermute | solution.py:474
  25.0 5.5 %collective-permute-start.7 = (bf16[256,256]{1,0:T(8,128)(2,1)S(1)}, bf16[256,256]{1,0:T(8,128)(2,1)S(1)}, u32[]{:S(2)}, u32[]{:S(2)}) collective-permute-start(bf16[256,256]{1,0:T(8,128)(2,1)S(1)} %get-tuple-element.37.refs_0_), channel_id=1, source_target_pairs={{0,1},{1,0},{2,3},{3,2},{4,5},{5,4},{6,7},{7,6},{8,9},{9,8},{10,11... | collective-permute-start | bytes 393224 | tf_op jit(solution)/shard_map/ppermute | solution.py:475
  27.5 3.0 %collective-permute-start.8 = (bf16[256,256]{1,0:T(8,128)(2,1)S(1)}, bf16[256,256]{1,0:T(8,128)(2,1)S(1)}, u32[]{:S(2)}, u32[]{:S(2)}) collective-permute-start(bf16[256,256]{1,0:T(8,128)(2,1)S(1)} %collective-permute-done.4.refs_1_), channel_id=1, source_target_pairs={{0,1},{1,0},{2,3},{3,2},{4,5},{5,4},{6,7},{7,6},{8,9},{9,8},{10,11... | collective-permute-start | bytes 393224 | tf_op jit(solution)/shard_map/ppermute | solution.py:475
  30.0 1.3 %collective-permute-start.9 = (bf16[256,256]{1,0:T(8,128)(2,1)S(1)}, bf16[256,256]{1,0:T(8,128)(2,1)S(1)}, u32[]{:S(2)}, u32[]{:S(2)}) collective-permute-start(bf16[256,256]{1,0:T(8,128)(2,1)S(1)} %collective-permute-done.5.refs_2_), channel_id=1, source_target_pairs={{0,1},{1,0},{2,3},{3,2},{4,5},{5,4},{6,7},{7,6},{8,9},{9,8},{10,11... | collective-permute-start | bytes 393224 | tf_op jit(solution)/shard_map/ppermute | solution.py:475
  30.0 1.5 %collective-permute-start.10 = (bf16[256,256]{1,0:T(8,128)(2,1)S(1)}, bf16[256,256]{1,0:T(8,128)(2,1)S(1)}, u32[]{:S(2)}, u32[]{:S(2)}) collective-permute-start(bf16[256,256]{1,0:T(8,128)(2,1)S(1)} %collective-permute-done.6.refs_3_), channel_id=1, source_target_pairs={{0,1},{1,0},{2,3},{3,2},{4,5},{5,4},{6,7},{7,6},{8,9},{9,8},{10,11... | collective-permute-start | bytes 393224 | tf_op jit(solution)/shard_map/ppermute | solution.py:475
  43.0 2.1 %collective-permute-start.11 = (bf16[4,256,256]{2,1,0:T(8,128)(2,1)}, bf16[4,256,256]{2,1,0:T(8,128)(2,1)S(1)}, u32[]{:S(2)}, u32[]{:S(2)}) collective-permute-start(bf16[4,256,256]{2,1,0:T(8,128)(2,1)} %get-tuple-element.40), channel_id=1, source_target_pairs={{0,1},{1,0},{2,3},{3,2},{4,5},{5,4},{6,7},{7,6},{8,9},{9,8},{10,11... | collective-permute-start | bytes 1572872 | tf_op jit(solution)/shard_map/ppermute | solution.py:448
  43.3 4.5 %collective-permute-start.14 = (f32[64,64]{1,0:T(8,128)S(1)}, f32[64,64]{1,0:T(8,128)S(1)}, u32[]{:S(2)}, u32[]{:S(2)}) collective-permute-start(f32[64,64]{1,0:T(8,128)S(1)} %get-tuple-element.45), channel_id=1, source_target_pairs={{0,8},{8,0},{16,24},{24,16},{1,9},{9,1},{17,25},{25,17},{2,10},{10... | collective-permute-start | bytes 49160 | tf_op jit(solution)/shard_map/ppermute | solution.py:535
  45.5 8.4 %collective-permute-start.12 = (bf16[256,256]{1,0:T(8,128)(2,1)S(1)}, bf16[256,256]{1,0:T(8,128)(2,1)S(1)}, u32[]{:S(2)}, u32[]{:S(2)}) collective-permute-start(bf16[256,256]{1,0:T(8,128)(2,1)S(1)} %get-tuple-element.42), channel_id=1, source_target_pairs={{0,2},{1,3},{2,0},{3,1},{4,6},{5,7},{6,4},{7,5},{8,10},{9,11},{10,... | collective-permute-start | bytes 393224 | tf_op jit(solution)/shard_map/ppermute | solution.py:471
  46.9 8.3 %collective-permute-start.13 = (bf16[256,256]{1,0:T(8,128)(2,1)S(1)}, bf16[256,256]{1,0:T(8,128)(2,1)S(1)}, u32[]{:S(2)}, u32[]{:S(2)}) collective-permute-start(bf16[256,256]{1,0:T(8,128)(2,1)S(1)} %get-tuple-element.43), channel_id=1, source_target_pairs={{0,4},{1,5},{2,6},{3,7},{4,0},{5,1},{6,2},{7,3},{8,12},{9,13},{10,... | collective-permute-start | bytes 393224 | tf_op jit(solution)/shard_map/ppermute | solution.py:471
  47.8 7.4 %collective-permute-start.15 = (bf16[256,256]{1,0:T(8,128)(2,1)S(1)}, bf16[256,256]{1,0:T(8,128)(2,1)S(1)}, u32[]{:S(2)}, u32[]{:S(2)}) collective-permute-start(bf16[256,256]{1,0:T(8,128)(2,1)S(1)} %get-tuple-element.46), channel_id=1, source_target_pairs={{0,6},{1,7},{2,4},{3,5},{4,2},{5,3},{6,0},{7,1},{8,14},{9,15},{10,... | collective-permute-start | bytes 393224 | tf_op jit(solution)/shard_map/ppermute | solution.py:471
  49.1 4.8 %collective-permute-start.16 = (f32[64,64]{1,0:T(8,128)S(1)}, f32[64,64]{1,0:T(8,128)S(1)}, u32[]{:S(2)}, u32[]{:S(2)}) collective-permute-start(f32[64,64]{1,0:T(8,128)S(1)} %add.3.refs_4_), channel_id=1, source_target_pairs={{0,16},{8,24},{16,0},{24,8},{1,17},{9,25},{17,1},{25,9},{2,18},{10... | collective-permute-start | bytes 49160 | tf_op jit(solution)/shard_map/ppermute | solution.py:540
  59.9 8.1 %collective-permute-start.17 = (bf16[288,256]{1,0:T(8,128)(2,1)S(1)}, bf16[288,256]{1,0:T(8,128)(2,1)S(1)}, u32[]{:S(2)}, u32[]{:S(2)}) collective-permute-start(bf16[288,256]{1,0:T(8,128)(2,1)S(1)} %get-tuple-element.48.refs_0_), channel_id=1, source_target_pairs={{0,2},{1,3},{2,0},{3,1},{4,6},{5,7},{6,4},{7,5},{8,10},{9,11},{10,... | collective-permute-start | bytes 442376 | tf_op jit(solution)/shard_map/ppermute | solution.py:578
  60.7 8.2 %collective-permute-start.18 = (bf16[288,256]{1,0:T(8,128)(2,1)S(1)}, bf16[288,256]{1,0:T(8,128)(2,1)S(1)}, u32[]{:S(2)}, u32[]{:S(2)}) collective-permute-start(bf16[288,256]{1,0:T(8,128)(2,1)S(1)} %get-tuple-element.48.refs_0_), channel_id=1, source_target_pairs={{0,4},{1,5},{2,6},{3,7},{4,0},{5,1},{6,2},{7,3},{8,12},{9,13},{10,... | collective-permute-start | bytes 442376 | tf_op jit(solution)/shard_map/ppermute | solution.py:578
  62.0 7.0 %collective-permute-start.19 = (bf16[288,256]{1,0:T(8,128)(2,1)S(1)}, bf16[288,256]{1,0:T(8,128)(2,1)S(1)}, u32[]{:S(2)}, u32[]{:S(2)}) collective-permute-start(bf16[288,256]{1,0:T(8,128)(2,1)S(1)} %get-tuple-element.48.refs_0_), channel_id=1, source_target_pairs={{0,6},{1,7},{2,4},{3,5},{4,2},{5,3},{6,0},{7,1},{8,14},{9,15},{10,... | collective-permute-start | bytes 442376 | tf_op jit(solution)/shard_map/ppermute | solution.py:578
  63.4 9.2 %collective-permute-start.20 = (bf16[288,256]{1,0:T(8,128)(2,1)S(1)}, bf16[288,256]{1,0:T(8,128)(2,1)S(1)}, u32[]{:S(2)}, u32[]{:S(2)}) collective-permute-start(bf16[288,256]{1,0:T(8,128)(2,1)S(1)} %get-tuple-element.48.refs_0_), channel_id=1, source_target_pairs={{0,1},{1,0},{2,3},{3,2},{4,5},{5,4},{6,7},{7,6},{8,9},{9,8},{10,11... | collective-permute-start | bytes 442376 | tf_op jit(solution)/shard_map/ppermute | solution.py:581
  68.0 4.7 %copy-start.2 = (bf16[64,256]{1,0:T(8,128)(2,1)S(1)}, bf16[64,256]{1,0:T(8,128)(2,1)}, u32[]{:S(2)}) copy-start(bf16[64,256]{1,0:T(8,128)(2,1)} %constant.15.clone.refs_9_) | copy-start | bytes 98308
  69.0 3.7 %collective-permute-start.21 = (bf16[288,256]{1,0:T(8,128)(2,1)S(1)}, bf16[288,256]{1,0:T(8,128)(2,1)S(1)}, u32[]{:S(2)}, u32[]{:S(2)}) collective-permute-start(bf16[288,256]{1,0:T(8,128)(2,1)S(1)} %collective-permute-done.17.refs_1_), channel_id=1, source_target_pairs={{0,1},{1,0},{2,3},{3,2},{4,5},{5,4},{6,7},{7,6},{8,9},{9,8},{10,11... | collective-permute-start | bytes 442376 | tf_op jit(solution)/shard_map/ppermute | solution.py:581
  69.0 3.7 %collective-permute-start.22 = (bf16[288,256]{1,0:T(8,128)(2,1)S(1)}, bf16[288,256]{1,0:T(8,128)(2,1)S(1)}, u32[]{:S(2)}, u32[]{:S(2)}) collective-permute-start(bf16[288,256]{1,0:T(8,128)(2,1)S(1)} %collective-permute-done.18.refs_2_), channel_id=1, source_target_pairs={{0,1},{1,0},{2,3},{3,2},{4,5},{5,4},{6,7},{7,6},{8,9},{9,8},{10,11... | collective-permute-start | bytes 442376 | tf_op jit(solution)/shard_map/ppermute | solution.py:581
  69.5 3.2 %collective-permute-start.23 = (bf16[288,256]{1,0:T(8,128)(2,1)S(1)}, bf16[288,256]{1,0:T(8,128)(2,1)S(1)}, u32[]{:S(2)}, u32[]{:S(2)}) collective-permute-start(bf16[288,256]{1,0:T(8,128)(2,1)S(1)} %collective-permute-done.19.refs_3_), channel_id=1, source_target_pairs={{0,1},{1,0},{2,3},{3,2},{4,5},{5,4},{6,7},{7,6},{8,9},{9,8},{10,11... | collective-permute-start | bytes 442376 | tf_op jit(solution)/shard_map/ppermute | solution.py:581

commit v6 on v5

--- a/solution.py
+++ b/solution.py
@@ -553,7 +553,7 @@
         name="mix_backward",
     )
     gram_steps = modes // 8
-    early = gram_steps * 5 // 8
+    early = gram_steps * 3 // 4
 
     def gram_part(start, steps, before):
         per = 8

time: 79 us -> 78.6 us (level)
  no operation moved by 1% of the time
where the time goes in v6:
time: 78.6 us; the launch traced here: 78.4 us
  Pallas kernels  38.1 us (48%)
  starting transfers between devices  21.6 us (27%)
  waiting for transfers between devices  17.9 us (23%)
    pallas_call x9, Pallas kernels, call(): pl.pallas_call(kernel, out_shape=out_shape, grid_spec=pltpu.PrefetchScala...  38.1 us
    ppermute x6, starting transfers between devices, to_chips(): flip('mp', count, 2 * bit)(outs[bit])  8.02 us
    ppermute x6, waiting for transfers between devices, to_chips(): flip('mp', count, 2 * bit)(outs[bit])  7.71 us
    ppermute x3, waiting for transfers between devices, to_all(): flip('mp', count, 2 * bit)(block)  4.95 us
    ppermute x3, starting transfers between devices, body(): flip('mp', count, 2 * bit)(back)  3.55 us
    ppermute x3, starting transfers between devices, to_all(): flip('mp', count, 2 * bit)(block)  3.55 us
    ppermute x1, starting transfers between devices, body(): locals_ = [local_term, flip('dp', dp_count, bit)(local_term)]  2.59 us
    ppermute x1, waiting for transfers between devices, body(): locals_ = [local_term, flip('dp', dp_count, bit)(local_term)]  2.22 us
  transfers between devices with their start and end apart: 24, of which 11 were waited for; matrix products, arithmetic and copies ran while one was open for 0% of the time, Pallas kernels for 10%

profile of v6, /device:TPU:0, one launch (start us, length us, event | category | flops | bytes accessed | tf_op | source)
XLA Modules:
  0.0 78.4 jit_solution(4111684937191147772)
XLA Ops:
  0.6 0.0 copy-start
  0.6 3.2 %forward_y.1 = (bf16[4,256,256]{2,1,0:T(8,128)(2,1)S(1)}, bf16[4,256,256]{2,1,0:T(8,128)(2,1)S(1)}) custom-call(s32[1]{0:T(128)} %bitcast.here, bf16[32,256,256]{2,1,0:T(8,128)(2,1)} %bitcast.17), custom_call_target="tpu_custom_call" | custom-call | flops 268435456 | bytes 5242880 | tf_op jit(solution)/shard_map/forward_y/pallas_call | solution.py:87
  3.9 0.5 collective-permute-start
  4.4 1.5 %collective-permute-done.got_ref = bf16[4,256,256]{2,1,0:T(8,128)(2,1)S(1)} collective-permute-done((bf16[4,256,256]{2,1,0:T(8,128)(2,1)S(1)}, bf16[4,256,256]{2,1,0:T(8,128)(2,1)S(1)}, u32[]{:S(2)}, u32[]{:S(2)}) %collective-permute-start) | collective-permute-done | bytes 524320 | tf_op jit(solution)/shard_map/ppermute | solution.py:448
  6.0 0.5 forward_x.2
  6.4 2.9 %collective-permute-start.1 = (bf16[256,256]{1,0:T(8,128)(2,1)S(1)}, bf16[256,256]{1,0:T(8,128)(2,1)S(1)}, u32[]{:S(2)}, u32[]{:S(2)}) collective-permute-start(bf16[256,256]{1,0:T(8,128)(2,1)S(1)} %get-tuple-element.34), channel_id=1, source_target_pairs={{0,2},{1,3},{2,0},{3,1},{4,6},{5,7},{6,4},{7,5},{8,10},{9,11},{10,... | collective-permute-start | bytes 393224 | tf_op jit(solution)/shard_map/ppermute | solution.py:471
  9.3 1.5 %collective-permute-start.2 = (bf16[256,256]{1,0:T(8,128)(2,1)S(1)}, bf16[256,256]{1,0:T(8,128)(2,1)S(1)}, u32[]{:S(2)}, u32[]{:S(2)}) collective-permute-start(bf16[256,256]{1,0:T(8,128)(2,1)S(1)} %get-tuple-element.35), channel_id=1, source_target_pairs={{0,4},{1,5},{2,6},{3,7},{4,0},{5,1},{6,2},{7,3},{8,12},{9,13},{10,... | collective-permute-start | bytes 393224 | tf_op jit(solution)/shard_map/ppermute | solution.py:471
  10.9 0.0 collective-permute-start.3
  10.9 2.3 %collective-permute-done.1.refs_1_ = bf16[256,256]{1,0:T(8,128)(2,1)S(1)} collective-permute-done((bf16[256,256]{1,0:T(8,128)(2,1)S(1)}, bf16[256,256]{1,0:T(8,128)(2,1)S(1)}, u32[]{:S(2)}, u32[]{:S(2)}) %collective-permute-start.1) | collective-permute-done | bytes 131104 | tf_op jit(solution)/shard_map/ppermute | solution.py:471
  13.2 4.2 %collective-permute-done.2.refs_2_ = bf16[256,256]{1,0:T(8,128)(2,1)S(1)} collective-permute-done((bf16[256,256]{1,0:T(8,128)(2,1)S(1)}, bf16[256,256]{1,0:T(8,128)(2,1)S(1)}, u32[]{:S(2)}, u32[]{:S(2)}) %collective-permute-start.2) | collective-permute-done | bytes 131104 | tf_op jit(solution)/shard_map/ppermute | solution.py:471
  17.4 0.0 collective-permute-done.3.refs_3_
  17.4 4.0 %mix_forward.1 = (bf16[256,256]{1,0:T(8,128)(2,1)S(1)}, bf16[1024,256]{1,0:T(8,128)(2,1)S(1)}) custom-call(s32[1]{0:T(128)} %bitcast.here, bf16[256,256]{1,0:T(8,128)(2,1)S(1)} %get-tuple-element.33.refs_0_, bf16[256,256]{1,0:T(8,128)(2,1)S(1)} %collective-permute-done.1.refs_1_, bf16[256,256]{1,0:T(8,128)(2,1)S(1)} %collective-permute-done.2.refs_2_, ...), custom_call_target="tpu_custom_call" | custom-call | flops 67108864 | bytes 8912896 | tf_op jit(solution)/shard_map/mix_forward/pallas_call | solution.py:87
  21.5 1.3 %collective-permute-start.4 = (bf16[256,256]{1,0:T(8,128)(2,1)S(1)}, bf16[256,256]{1,0:T(8,128)(2,1)S(1)}, u32[]{:S(2)}, u32[]{:S(2)}) collective-permute-start(bf16[256,256]{1,0:T(8,128)(2,1)S(1)} %get-tuple-element.37.refs_0_), channel_id=1, source_target_pairs={{0,2},{1,3},{2,0},{3,1},{4,6},{5,7},{6,4},{7,5},{8,10},{9,11},{10,... | collective-permute-start | bytes 393224 | tf_op jit(solution)/shard_map/ppermute | solution.py:474
  22.7 0.8 %collective-permute-start.5 = (bf16[256,256]{1,0:T(8,128)(2,1)S(1)}, bf16[256,256]{1,0:T(8,128)(2,1)S(1)}, u32[]{:S(2)}, u32[]{:S(2)}) collective-permute-start(bf16[256,256]{1,0:T(8,128)(2,1)S(1)} %get-tuple-element.37.refs_0_), channel_id=1, source_target_pairs={{0,4},{1,5},{2,6},{3,7},{4,0},{5,1},{6,2},{7,3},{8,12},{9,13},{10,... | collective-permute-start | bytes 393224 | tf_op jit(solution)/shard_map/ppermute | solution.py:474
  23.6 1.4 %collective-permute-start.6 = (bf16[256,256]{1,0:T(8,128)(2,1)S(1)}, bf16[256,256]{1,0:T(8,128)(2,1)S(1)}, u32[]{:S(2)}, u32[]{:S(2)}) collective-permute-start(bf16[256,256]{1,0:T(8,128)(2,1)S(1)} %get-tuple-element.37.refs_0_), channel_id=1, source_target_pairs={{0,6},{1,7},{2,4},{3,5},{4,2},{5,3},{6,0},{7,1},{8,14},{9,15},{10,... | collective-permute-start | bytes 393224 | tf_op jit(solution)/shard_map/ppermute | solution.py:474
  25.0 2.5 %collective-permute-done.4.refs_1_ = bf16[256,256]{1,0:T(8,128)(2,1)S(1)} collective-permute-done((bf16[256,256]{1,0:T(8,128)(2,1)S(1)}, bf16[256,256]{1,0:T(8,128)(2,1)S(1)}, u32[]{:S(2)}, u32[]{:S(2)}) %collective-permute-start.4) | collective-permute-done | bytes 131104 | tf_op jit(solution)/shard_map/ppermute | solution.py:474
  27.5 0.0 collective-permute-start.8
  27.5 2.4 %collective-permute-done.5.refs_2_ = bf16[256,256]{1,0:T(8,128)(2,1)S(1)} collective-permute-done((bf16[256,256]{1,0:T(8,128)(2,1)S(1)}, bf16[256,256]{1,0:T(8,128)(2,1)S(1)}, u32[]{:S(2)}, u32[]{:S(2)}) %collective-permute-start.5) | collective-permute-done | bytes 131104 | tf_op jit(solution)/shard_map/ppermute | solution.py:474
  30.0 0.0 collective-permute-start.9
  30.0 0.0 collective-permute-done.6.refs_3_
  30.0 0.5 collective-permute-start.10
  30.5 0.0 collective-permute-done.7.refs_4_
  30.5 0.8 %collective-permute-done.9.refs_6_ = bf16[256,256]{1,0:T(8,128)(2,1)S(1)} collective-permute-done((bf16[256,256]{1,0:T(8,128)(2,1)S(1)}, bf16[256,256]{1,0:T(8,128)(2,1)S(1)}, u32[]{:S(2)}, u32[]{:S(2)}) %collective-permute-start.9) | collective-permute-done | bytes 131104 | tf_op jit(solution)/shard_map/ppermute | solution.py:475
  31.3 0.2 collective-permute-done.10.refs_7_
  31.5 11.5 %middle.1 = (bf16[32,256,256]{2,1,0:T(8,128)(2,1)}, bf16[32,256,256]{2,1,0:T(8,128)(2,1)}, bf16[4,256,256]{2,1,0:T(8,128)(2,1)S(1)}, bf16[4,256,256]{2,1,0:T(8,128)(2,1)}, f32[64,64]{1,0:T(8,128)S(1)}) custom-call(s32[1]{0:T(128)} %bitcast.here, bf16[256,256]{1,0:T(8,128)(2,1)S(1)} %get-tuple-element.37.refs_0_, ...), custom_call_target="tpu_custom_call" | custom-call | flops 2684354560 | bytes 18874368 | tf_op jit(solution)/shard_map/middle/pallas_call | solution.py:87
  43.0 0.3 collective-permute-start.11
  43.3 1.6 %collective-permute-start.14 = (f32[64,64]{1,0:T(8,128)S(1)}, f32[64,64]{1,0:T(8,128)S(1)}, u32[]{:S(2)}, u32[]{:S(2)}) collective-permute-start(f32[64,64]{1,0:T(8,128)S(1)} %get-tuple-element.45), channel_id=1, source_target_pairs={{0,8},{8,0},{16,24},{24,16},{1,9},{9,1},{17,25},{25,17},{2,10},{10... | collective-permute-start | bytes 49160 | tf_op jit(solution)/shard_map/ppermute | solution.py:535
  44.9 0.2 collective-permute-done.11.got_ref
  45.1 0.4 forward_x.3
  45.5 1.3 %collective-permute-start.12 = (bf16[256,256]{1,0:T(8,128)(2,1)S(1)}, bf16[256,256]{1,0:T(8,128)(2,1)S(1)}, u32[]{:S(2)}, u32[]{:S(2)}) collective-permute-start(bf16[256,256]{1,0:T(8,128)(2,1)S(1)} %get-tuple-element.42), channel_id=1, source_target_pairs={{0,2},{1,3},{2,0},{3,1},{4,6},{5,7},{6,4},{7,5},{8,10},{9,11},{10,... | collective-permute-start | bytes 393224 | tf_op jit(solution)/shard_map/ppermute | solution.py:471
  46.9 0.9 %collective-permute-start.13 = (bf16[256,256]{1,0:T(8,128)(2,1)S(1)}, bf16[256,256]{1,0:T(8,128)(2,1)S(1)}, u32[]{:S(2)}, u32[]{:S(2)}) collective-permute-start(bf16[256,256]{1,0:T(8,128)(2,1)S(1)} %get-tuple-element.43), channel_id=1, source_target_pairs={{0,4},{1,5},{2,6},{3,7},{4,0},{5,1},{6,2},{7,3},{8,12},{9,13},{10,... | collective-permute-start | bytes 393224 | tf_op jit(solution)/shard_map/ppermute | solution.py:471
  47.8 1.3 %collective-permute-start.15 = (bf16[256,256]{1,0:T(8,128)(2,1)S(1)}, bf16[256,256]{1,0:T(8,128)(2,1)S(1)}, u32[]{:S(2)}, u32[]{:S(2)}) collective-permute-start(bf16[256,256]{1,0:T(8,128)(2,1)S(1)} %get-tuple-element.46), channel_id=1, source_target_pairs={{0,6},{1,7},{2,4},{3,5},{4,2},{5,3},{6,0},{7,1},{8,14},{9,15},{10,... | collective-permute-start | bytes 393224 | tf_op jit(solution)/shard_map/ppermute | solution.py:471
  49.1 2.6 %collective-permute-start.16 = (f32[64,64]{1,0:T(8,128)S(1)}, f32[64,64]{1,0:T(8,128)S(1)}, u32[]{:S(2)}, u32[]{:S(2)}) collective-permute-start(f32[64,64]{1,0:T(8,128)S(1)} %add.3.refs_4_), channel_id=1, source_target_pairs={{0,16},{8,24},{16,0},{24,8},{1,17},{9,25},{17,1},{25,9},{2,18},{10... | collective-permute-start | bytes 49160 | tf_op jit(solution)/shard_map/ppermute | solution.py:540
  51.7 2.2 %collective-permute-done.16.refs_5_ = f32[64,64]{1,0:T(8,128)S(1)} collective-permute-done((f32[64,64]{1,0:T(8,128)S(1)}, f32[64,64]{1,0:T(8,128)S(1)}, u32[]{:S(2)}, u32[]{:S(2)}) %collective-permute-start.16) | collective-permute-done | bytes 16416 | tf_op jit(solution)/shard_map/ppermute | solution.py:540
  53.9 0.0 collective-permute-done.12.refs_1_
  53.9 1.2 %collective-permute-done.13.refs_2_ = bf16[256,256]{1,0:T(8,128)(2,1)S(1)} collective-permute-done((bf16[256,256]{1,0:T(8,128)(2,1)S(1)}, bf16[256,256]{1,0:T(8,128)(2,1)S(1)}, u32[]{:S(2)}, u32[]{:S(2)}) %collective-permute-start.13) | collective-permute-done | bytes 131104 | tf_op jit(solution)/shard_map/ppermute | solution.py:471
  55.1 4.8 %mix_backward.1 = (bf16[288,256]{1,0:T(8,128)(2,1)S(1)}, f32[1024,128]{1,0:T(8,128)S(1)}) custom-call(s32[1]{0:T(128)} %bitcast.here, bf16[256,256]{1,0:T(8,128)(2,1)S(1)} %get-tuple-element.41.refs_0_, bf16[256,256]{1,0:T(8,128)(2,1)S(1)} %collective-permute-done.12.refs_1_, bf16[256,256]{1,0:T(8,128)(2,1)S(1)} %collective-permute-done.13.refs_2_, ...), custom_call_target="tpu_custom_call" | custom-call | flops 67108864 | bytes 8912896 | tf_op jit(solution)/shard_map/mix_backward/pallas_call | solution.py:87
  59.9 0.8 %collective-permute-start.17 = (bf16[288,256]{1,0:T(8,128)(2,1)S(1)}, bf16[288,256]{1,0:T(8,128)(2,1)S(1)}, u32[]{:S(2)}, u32[]{:S(2)}) collective-permute-start(bf16[288,256]{1,0:T(8,128)(2,1)S(1)} %get-tuple-element.48.refs_0_), channel_id=1, source_target_pairs={{0,2},{1,3},{2,0},{3,1},{4,6},{5,7},{6,4},{7,5},{8,10},{9,11},{10,... | collective-permute-start | bytes 442376 | tf_op jit(solution)/shard_map/ppermute | solution.py:578
  60.7 1.3 %collective-permute-start.18 = (bf16[288,256]{1,0:T(8,128)(2,1)S(1)}, bf16[288,256]{1,0:T(8,128)(2,1)S(1)}, u32[]{:S(2)}, u32[]{:S(2)}) collective-permute-start(bf16[288,256]{1,0:T(8,128)(2,1)S(1)} %get-tuple-element.48.refs_0_), channel_id=1, source_target_pairs={{0,4},{1,5},{2,6},{3,7},{4,0},{5,1},{6,2},{7,3},{8,12},{9,13},{10,... | collective-permute-start | bytes 442376 | tf_op jit(solution)/shard_map/ppermute | solution.py:578
  62.0 1.4 %collective-permute-start.19 = (bf16[288,256]{1,0:T(8,128)(2,1)S(1)}, bf16[288,256]{1,0:T(8,128)(2,1)S(1)}, u32[]{:S(2)}, u32[]{:S(2)}) collective-permute-start(bf16[288,256]{1,0:T(8,128)(2,1)S(1)} %get-tuple-element.48.refs_0_), channel_id=1, source_target_pairs={{0,6},{1,7},{2,4},{3,5},{4,2},{5,3},{6,0},{7,1},{8,14},{9,15},{10,... | collective-permute-start | bytes 442376 | tf_op jit(solution)/shard_map/ppermute | solution.py:578
  63.4 5.3 %gram.2.refs_0_ = f32[4,4,32,64,128]{4,3,2,1,0:T(8,128)} custom-call(s32[1]{0:T(128)} %bitcast.here, bf16[1024,256]{1,0:T(8,128)(2,1)S(1)} %get-tuple-element.49.spread_ref, f32[1024,128]{1,0:T(8,128)S(1)} %get-tuple-element.50.pair_ref), custom_call_target="tpu_custom_call" | custom-call | flops 33554432 | bytes 8388608 | tf_op jit(solution)/shard_map/gram/pallas_call | solution.py:87
  68.7 0.0 copy-start.2
  68.8 0.2 collective-permute-done.18.refs_2_
  69.0 0.4 collective-permute-start.21
  69.4 0.1 collective-permute-start.22
  69.5 0.4 collective-permute-start.23
  69.9 2.4 %gram.3 = f32[4,4,32,64,128]{4,3,2,1,0:T(8,128)} custom-call(s32[1]{0:T(128)} %bitcast.here, bf16[1024,256]{1,0:T(8,128)(2,1)S(1)} %get-tuple-element.49.spread_ref, f32[1024,128]{1,0:T(8,128)S(1)} %get-tuple-element.50.pair_ref, f32[4,4,32,64,128]{4,3,2,1,0:T(8,128)} %gram.2.refs_0_), custom_call_target="tpu_custom_call", output_to_operand_aliasing={{}: (3, {})} | custom-call | flops 33554432 | bytes 8388608 | tf_op jit(solution)/shard_map/gram/pallas_call | solution.py:87
  72.3 6.1 %last.1 = (bf16[32,256,256]{2,1,0:T(8,128)(2,1)}, f32[64,64]{1,0:T(8,128)}) custom-call(s32[1]{0:T(128)} %bitcast.here, bf16[288,256]{1,0:T(8,128)(2,1)S(1)} %get-tuple-element.48.refs_0_, bf16[288,256]{1,0:T(8,128)(2,1)S(1)} %collective-permute-done.17.refs_1_, bf16[288,256]{1,0:T(8,128)(2,1)S(1)} %collective-permute-done.18.refs_2_, ...), custom_call_target="tpu_custom_call" | custom-call | flops 1342177280 | bytes 9437184 | tf_op jit(solution)/shard_map/last/pallas_call | solution.py:87
  (18 shorter events, 0.0 us)
Async XLA Ops:
  0.6 5.3 %copy-start = (bf16[8,256,256]{2,1,0:T(8,128)(2,1)S(1)}, bf16[8,256,256]{2,1,0:T(8,128)(2,1)}, u32[]{:S(2)}) copy-start(bf16[8,256,256]{2,1,0:T(8,128)(2,1)} %constant.12.clone.own_ref.other_ref) | copy-start | bytes 3145732
  3.9 2.1 %collective-permute-start = (bf16[4,256,256]{2,1,0:T(8,128)(2,1)S(1)}, bf16[4,256,256]{2,1,0:T(8,128)(2,1)S(1)}, u32[]{:S(2)}, u32[]{:S(2)}) collective-permute-start(bf16[4,256,256]{2,1,0:T(8,128)(2,1)S(1)} %get-tuple-element.32), channel_id=1, source_target_pairs={{0,1},{1,0},{2,3},{3,2},{4,5},{5,4},{6,7},{7,6},{8,9},{9,8},{10,11... | collective-permute-start | bytes 1572872 | tf_op jit(solution)/shard_map/ppermute | solution.py:448
  6.4 6.8 %collective-permute-start.1 = (bf16[256,256]{1,0:T(8,128)(2,1)S(1)}, bf16[256,256]{1,0:T(8,128)(2,1)S(1)}, u32[]{:S(2)}, u32[]{:S(2)}) collective-permute-start(bf16[256,256]{1,0:T(8,128)(2,1)S(1)} %get-tuple-element.34), channel_id=1, source_target_pairs={{0,2},{1,3},{2,0},{3,1},{4,6},{5,7},{6,4},{7,5},{8,10},{9,11},{10,... | collective-permute-start | bytes 393224 | tf_op jit(solution)/shard_map/ppermute | solution.py:471
  9.3 8.1 %collective-permute-start.2 = (bf16[256,256]{1,0:T(8,128)(2,1)S(1)}, bf16[256,256]{1,0:T(8,128)(2,1)S(1)}, u32[]{:S(2)}, u32[]{:S(2)}) collective-permute-start(bf16[256,256]{1,0:T(8,128)(2,1)S(1)} %get-tuple-element.35), channel_id=1, source_target_pairs={{0,4},{1,5},{2,6},{3,7},{4,0},{5,1},{6,2},{7,3},{8,12},{9,13},{10,... | collective-permute-start | bytes 393224 | tf_op jit(solution)/shard_map/ppermute | solution.py:471
  10.9 6.5 %collective-permute-start.3 = (bf16[256,256]{1,0:T(8,128)(2,1)S(1)}, bf16[256,256]{1,0:T(8,128)(2,1)S(1)}, u32[]{:S(2)}, u32[]{:S(2)}) collective-permute-start(bf16[256,256]{1,0:T(8,128)(2,1)S(1)} %get-tuple-element.36), channel_id=1, source_target_pairs={{0,6},{1,7},{2,4},{3,5},{4,2},{5,3},{6,0},{7,1},{8,14},{9,15},{10,... | collective-permute-start | bytes 393224 | tf_op jit(solution)/shard_map/ppermute | solution.py:471
  17.4 14.1 %copy-start.1 = (bf16[64,64]{1,0:T(8,128)(2,1)S(1)}, bf16[64,64]{1,0:T(8,128)(2,1)}, u32[]{:S(2)}) copy-start(bf16[64,64]{1,0:T(8,128)(2,1)} %refs_10_.3) | copy-start | bytes 24580
  17.4 14.1 %copy-start.3 = (bf16[64,256]{1,0:T(8,128)(2,1)S(1)}, bf16[64,256]{1,0:T(8,128)(2,1)}, u32[]{:S(2)}) copy-start(bf16[64,256]{1,0:T(8,128)(2,1)} %constant.14.clone.refs_9_) | copy-start | bytes 98308
  21.5 6.1 %collective-permute-start.4 = (bf16[256,256]{1,0:T(8,128)(2,1)S(1)}, bf16[256,256]{1,0:T(8,128)(2,1)S(1)}, u32[]{:S(2)}, u32[]{:S(2)}) collective-permute-start(bf16[256,256]{1,0:T(8,128)(2,1)S(1)} %get-tuple-element.37.refs_0_), channel_id=1, source_target_pairs={{0,2},{1,3},{2,0},{3,1},{4,6},{5,7},{6,4},{7,5},{8,10},{9,11},{10,... | collective-permute-start | bytes 393224 | tf_op jit(solution)/shard_map/ppermute | solution.py:474
  22.7 7.2 %collective-permute-start.5 = (bf16[256,256]{1,0:T(8,128)(2,1)S(1)}, bf16[256,256]{1,0:T(8,128)(2,1)S(1)}, u32[]{:S(2)}, u32[]{:S(2)}) collective-permute-start(bf16[256,256]{1,0:T(8,128)(2,1)S(1)} %get-tuple-element.37.refs_0_), channel_id=1, source_target_pairs={{0,4},{1,5},{2,6},{3,7},{4,0},{5,1},{6,2},{7,3},{8,12},{9,13},{10,... | collective-permute-start | bytes 393224 | tf_op jit(solution)/shard_map/ppermute | solution.py:474
  23.6 6.4 %collective-permute-start.6 = (bf16[256,256]{1,0:T(8,128)(2,1)S(1)}, bf16[256,256]{1,0:T(8,128)(2,1)S(1)}, u32[]{:S(2)}, u32[]{:S(2)}) collective-permute-start(bf16[256,256]{1,0:T(8,128)(2,1)S(1)} %get-tuple-element.37.refs_0_), channel_id=1, source_target_pairs={{0,6},{1,7},{2,4},{3,5},{4,2},{5,3},{6,0},{7,1},{8,14},{9,15},{10,... | collective-permute-start | bytes 393224 | tf_op jit(solution)/shard_map/ppermute | solution.py:474
  25.0 5.5 %collective-permute-start.7 = (bf16[256,256]{1,0:T(8,128)(2,1)S(1)}, bf16[256,256]{1,0:T(8,128)(2,1)S(1)}, u32[]{:S(2)}, u32[]{:S(2)}) collective-permute-start(bf16[256,256]{1,0:T(8,128)(2,1)S(1)} %get-tuple-element.37.refs_0_), channel_id=1, source_target_pairs={{0,1},{1,0},{2,3},{3,2},{4,5},{5,4},{6,7},{7,6},{8,9},{9,8},{10,11... | collective-permute-start | bytes 393224 | tf_op jit(solution)/shard_map/ppermute | solution.py:475
  27.5 3.0 %collective-permute-start.8 = (bf16[256,256]{1,0:T(8,128)(2,1)S(1)}, bf16[256,256]{1,0:T(8,128)(2,1)S(1)}, u32[]{:S(2)}, u32[]{:S(2)}) collective-permute-start(bf16[256,256]{1,0:T(8,128)(2,1)S(1)} %collective-permute-done.4.refs_1_), channel_id=1, source_target_pairs={{0,1},{1,0},{2,3},{3,2},{4,5},{5,4},{6,7},{7,6},{8,9},{9,8},{10,11... | collective-permute-start | bytes 393224 | tf_op jit(solution)/shard_map/ppermute | solution.py:475
  30.0 1.3 %collective-permute-start.9 = (bf16[256,256]{1,0:T(8,128)(2,1)S(1)}, bf16[256,256]{1,0:T(8,128)(2,1)S(1)}, u32[]{:S(2)}, u32[]{:S(2)}) collective-permute-start(bf16[256,256]{1,0:T(8,128)(2,1)S(1)} %collective-permute-done.5.refs_2_), channel_id=1, source_target_pairs={{0,1},{1,0},{2,3},{3,2},{4,5},{5,4},{6,7},{7,6},{8,9},{9,8},{10,11... | collective-permute-start | bytes 393224 | tf_op jit(solution)/shard_map/ppermute | solution.py:475
  30.0 1.5 %collective-permute-start.10 = (bf16[256,256]{1,0:T(8,128)(2,1)S(1)}, bf16[256,256]{1,0:T(8,128)(2,1)S(1)}, u32[]{:S(2)}, u32[]{:S(2)}) collective-permute-start(bf16[256,256]{1,0:T(8,128)(2,1)S(1)} %collective-permute-done.6.refs_3_), channel_id=1, source_target_pairs={{0,1},{1,0},{2,3},{3,2},{4,5},{5,4},{6,7},{7,6},{8,9},{9,8},{10,11... | collective-permute-start | bytes 393224 | tf_op jit(solution)/shard_map/ppermute | solution.py:475
  43.0 2.1 %collective-permute-start.11 = (bf16[4,256,256]{2,1,0:T(8,128)(2,1)}, bf16[4,256,256]{2,1,0:T(8,128)(2,1)S(1)}, u32[]{:S(2)}, u32[]{:S(2)}) collective-permute-start(bf16[4,256,256]{2,1,0:T(8,128)(2,1)} %get-tuple-element.40), channel_id=1, source_target_pairs={{0,1},{1,0},{2,3},{3,2},{4,5},{5,4},{6,7},{7,6},{8,9},{9,8},{10,11... | collective-permute-start | bytes 1572872 | tf_op jit(solution)/shard_map/ppermute | solution.py:448
  43.3 4.5 %collective-permute-start.14 = (f32[64,64]{1,0:T(8,128)S(1)}, f32[64,64]{1,0:T(8,128)S(1)}, u32[]{:S(2)}, u32[]{:S(2)}) collective-permute-start(f32[64,64]{1,0:T(8,128)S(1)} %get-tuple-element.45), channel_id=1, source_target_pairs={{0,8},{8,0},{16,24},{24,16},{1,9},{9,1},{17,25},{25,17},{2,10},{10... | collective-permute-start | bytes 49160 | tf_op jit(solution)/shard_map/ppermute | solution.py:535
  45.5 8.4 %collective-permute-start.12 = (bf16[256,256]{1,0:T(8,128)(2,1)S(1)}, bf16[256,256]{1,0:T(8,128)(2,1)S(1)}, u32[]{:S(2)}, u32[]{:S(2)}) collective-permute-start(bf16[256,256]{1,0:T(8,128)(2,1)S(1)} %get-tuple-element.42), channel_id=1, source_target_pairs={{0,2},{1,3},{2,0},{3,1},{4,6},{5,7},{6,4},{7,5},{8,10},{9,11},{10,... | collective-permute-start | bytes 393224 | tf_op jit(solution)/shard_map/ppermute | solution.py:471
  46.9 8.3 %collective-permute-start.13 = (bf16[256,256]{1,0:T(8,128)(2,1)S(1)}, bf16[256,256]{1,0:T(8,128)(2,1)S(1)}, u32[]{:S(2)}, u32[]{:S(2)}) collective-permute-start(bf16[256,256]{1,0:T(8,128)(2,1)S(1)} %get-tuple-element.43), channel_id=1, source_target_pairs={{0,4},{1,5},{2,6},{3,7},{4,0},{5,1},{6,2},{7,3},{8,12},{9,13},{10,... | collective-permute-start | bytes 393224 | tf_op jit(solution)/shard_map/ppermute | solution.py:471
  47.8 7.4 %collective-permute-start.15 = (bf16[256,256]{1,0:T(8,128)(2,1)S(1)}, bf16[256,256]{1,0:T(8,128)(2,1)S(1)}, u32[]{:S(2)}, u32[]{:S(2)}) collective-permute-start(bf16[256,256]{1,0:T(8,128)(2,1)S(1)} %get-tuple-element.46), channel_id=1, source_target_pairs={{0,6},{1,7},{2,4},{3,5},{4,2},{5,3},{6,0},{7,1},{8,14},{9,15},{10,... | collective-permute-start | bytes 393224 | tf_op jit(solution)/shard_map/ppermute | solution.py:471
  49.1 4.8 %collective-permute-start.16 = (f32[64,64]{1,0:T(8,128)S(1)}, f32[64,64]{1,0:T(8,128)S(1)}, u32[]{:S(2)}, u32[]{:S(2)}) collective-permute-start(f32[64,64]{1,0:T(8,128)S(1)} %add.3.refs_4_), channel_id=1, source_target_pairs={{0,16},{8,24},{16,0},{24,8},{1,17},{9,25},{17,1},{25,9},{2,18},{10... | collective-permute-start | bytes 49160 | tf_op jit(solution)/shard_map/ppermute | solution.py:540
  59.9 8.9 %collective-permute-start.17 = (bf16[288,256]{1,0:T(8,128)(2,1)S(1)}, bf16[288,256]{1,0:T(8,128)(2,1)S(1)}, u32[]{:S(2)}, u32[]{:S(2)}) collective-permute-start(bf16[288,256]{1,0:T(8,128)(2,1)S(1)} %get-tuple-element.48.refs_0_), channel_id=1, source_target_pairs={{0,2},{1,3},{2,0},{3,1},{4,6},{5,7},{6,4},{7,5},{8,10},{9,11},{10,... | collective-permute-start | bytes 442376 | tf_op jit(solution)/shard_map/ppermute | solution.py:578
  60.7 8.2 %collective-permute-start.18 = (bf16[288,256]{1,0:T(8,128)(2,1)S(1)}, bf16[288,256]{1,0:T(8,128)(2,1)S(1)}, u32[]{:S(2)}, u32[]{:S(2)}) collective-permute-start(bf16[288,256]{1,0:T(8,128)(2,1)S(1)} %get-tuple-element.48.refs_0_), channel_id=1, source_target_pairs={{0,4},{1,5},{2,6},{3,7},{4,0},{5,1},{6,2},{7,3},{8,12},{9,13},{10,... | collective-permute-start | bytes 442376 | tf_op jit(solution)/shard_map/ppermute | solution.py:578
  62.0 7.0 %collective-permute-start.19 = (bf16[288,256]{1,0:T(8,128)(2,1)S(1)}, bf16[288,256]{1,0:T(8,128)(2,1)S(1)}, u32[]{:S(2)}, u32[]{:S(2)}) collective-permute-start(bf16[288,256]{1,0:T(8,128)(2,1)S(1)} %get-tuple-element.48.refs_0_), channel_id=1, source_target_pairs={{0,6},{1,7},{2,4},{3,5},{4,2},{5,3},{6,0},{7,1},{8,14},{9,15},{10,... | collective-permute-start | bytes 442376 | tf_op jit(solution)/shard_map/ppermute | solution.py:578
  63.4 8.8 %collective-permute-start.20 = (bf16[288,256]{1,0:T(8,128)(2,1)S(1)}, bf16[288,256]{1,0:T(8,128)(2,1)S(1)}, u32[]{:S(2)}, u32[]{:S(2)}) collective-permute-start(bf16[288,256]{1,0:T(8,128)(2,1)S(1)} %get-tuple-element.48.refs_0_), channel_id=1, source_target_pairs={{0,1},{1,0},{2,3},{3,2},{4,5},{5,4},{6,7},{7,6},{8,9},{9,8},{10,11... | collective-permute-start | bytes 442376 | tf_op jit(solution)/shard_map/ppermute | solution.py:581
  68.7 3.6 %copy-start.2 = (bf16[64,256]{1,0:T(8,128)(2,1)S(1)}, bf16[64,256]{1,0:T(8,128)(2,1)}, u32[]{:S(2)}) copy-start(bf16[64,256]{1,0:T(8,128)(2,1)} %constant.15.clone.refs_9_) | copy-start | bytes 98308
  69.0 3.3 %collective-permute-start.21 = (bf16[288,256]{1,0:T(8,128)(2,1)S(1)}, bf16[288,256]{1,0:T(8,128)(2,1)S(1)}, u32[]{:S(2)}, u32[]{:S(2)}) collective-permute-start(bf16[288,256]{1,0:T(8,128)(2,1)S(1)} %collective-permute-done.17.refs_1_), channel_id=1, source_target_pairs={{0,1},{1,0},{2,3},{3,2},{4,5},{5,4},{6,7},{7,6},{8,9},{9,8},{10,11... | collective-permute-start | bytes 442376 | tf_op jit(solution)/shard_map/ppermute | solution.py:581
  69.4 2.9 %collective-permute-start.22 = (bf16[288,256]{1,0:T(8,128)(2,1)S(1)}, bf16[288,256]{1,0:T(8,128)(2,1)S(1)}, u32[]{:S(2)}, u32[]{:S(2)}) collective-permute-start(bf16[288,256]{1,0:T(8,128)(2,1)S(1)} %collective-permute-done.18.refs_2_), channel_id=1, source_target_pairs={{0,1},{1,0},{2,3},{3,2},{4,5},{5,4},{6,7},{7,6},{8,9},{9,8},{10,11... | collective-permute-start | bytes 442376 | tf_op jit(solution)/shard_map/ppermute | solution.py:581
  69.5 2.8 %collective-permute-start.23 = (bf16[288,256]{1,0:T(8,128)(2,1)S(1)}, bf16[288,256]{1,0:T(8,128)(2,1)S(1)}, u32[]{:S(2)}, u32[]{:S(2)}) collective-permute-start(bf16[288,256]{1,0:T(8,128)(2,1)S(1)} %collective-permute-done.19.refs_3_), channel_id=1, source_target_pairs={{0,1},{1,0},{2,3},{3,2},{4,5},{5,4},{6,7},{7,6},{8,9},{9,8},{10,11... | collective-permute-start | bytes 442376 | tf_op jit(solution)/shard_map/ppermute | solution.py:581

commit v7 on v6

--- a/solution.py
+++ b/solution.py
@@ -551,6 +551,7 @@
         flops=weight_bytes * 8,
         moved=weight_bytes + mode_bytes * chips,
         name="mix_backward",
+        limit=24 << 20,
     )
     gram_steps = modes // 8
     early = gram_steps * 3 // 4

time: 78.6 us -> 78.3 us (level)
  no operation moved by 1% of the time
where the time goes in v7:
time: 78.3 us; the launch traced here: 78.1 us
  Pallas kernels  37.8 us (48%)
  starting transfers between devices  21.6 us (28%)
  waiting for transfers between devices  17.9 us (23%)
  between operations  0.8 us (1%)
    pallas_call x9, Pallas kernels, call(): pl.pallas_call(kernel, out_shape=out_shape, grid_spec=pltpu.PrefetchScala...  37.8 us
    ppermute x6, starting transfers between devices, to_chips(): flip('mp', count, 2 * bit)(outs[bit])  8.01 us
    ppermute x6, waiting for transfers between devices, to_chips(): flip('mp', count, 2 * bit)(outs[bit])  7.74 us
    ppermute x3, waiting for transfers between devices, to_all(): flip('mp', count, 2 * bit)(block)  4.95 us
    ppermute x3, starting transfers between devices, to_all(): flip('mp', count, 2 * bit)(block)  3.55 us
    ppermute x3, starting transfers between devices, body(): flip('mp', count, 2 * bit)(back)  3.55 us
    ppermute x1, starting transfers between devices, body(): locals_ = [local_term, flip('dp', dp_count, bit)(local_term)]  2.59 us
    ppermute x1, waiting for transfers between devices, body(): locals_ = [local_term, flip('dp', dp_count, bit)(local_term)]  2.22 us
  transfers between devices with their start and end apart: 24, of which 11 were waited for; matrix products, arithmetic and copies ran while one was open for 0% of the time, Pallas kernels for 10%

profile of v7, /device:TPU:0, one launch (start us, length us, event | category | flops | bytes accessed | tf_op | source)
XLA Modules:
  0.0 78.1 jit_solution(11780251415811467007)
XLA Ops:
  0.6 0.0 copy-start
  0.6 3.2 %forward_y.1 = (bf16[4,256,256]{2,1,0:T(8,128)(2,1)S(1)}, bf16[4,256,256]{2,1,0:T(8,128)(2,1)S(1)}) custom-call(s32[1]{0:T(128)} %bitcast.here, bf16[32,256,256]{2,1,0:T(8,128)(2,1)} %bitcast.19), custom_call_target="tpu_custom_call" | custom-call | flops 268435456 | bytes 5242880 | tf_op jit(solution)/shard_map/forward_y/pallas_call | solution.py:87
  3.9 0.5 collective-permute-start
  4.4 1.5 %collective-permute-done.got_ref = bf16[4,256,256]{2,1,0:T(8,128)(2,1)S(1)} collective-permute-done((bf16[4,256,256]{2,1,0:T(8,128)(2,1)S(1)}, bf16[4,256,256]{2,1,0:T(8,128)(2,1)S(1)}, u32[]{:S(2)}, u32[]{:S(2)}) %collective-permute-start) | collective-permute-done | bytes 524320 | tf_op jit(solution)/shard_map/ppermute | solution.py:448
  6.0 0.4 forward_x.2
  6.4 2.9 %collective-permute-start.1 = (bf16[256,256]{1,0:T(8,128)(2,1)S(1)}, bf16[256,256]{1,0:T(8,128)(2,1)S(1)}, u32[]{:S(2)}, u32[]{:S(2)}) collective-permute-start(bf16[256,256]{1,0:T(8,128)(2,1)S(1)} %get-tuple-element.34), channel_id=1, source_target_pairs={{0,2},{1,3},{2,0},{3,1},{4,6},{5,7},{6,4},{7,5},{8,10},{9,11},{10,... | collective-permute-start | bytes 393224 | tf_op jit(solution)/shard_map/ppermute | solution.py:471
  9.3 1.5 %collective-permute-start.2 = (bf16[256,256]{1,0:T(8,128)(2,1)S(1)}, bf16[256,256]{1,0:T(8,128)(2,1)S(1)}, u32[]{:S(2)}, u32[]{:S(2)}) collective-permute-start(bf16[256,256]{1,0:T(8,128)(2,1)S(1)} %get-tuple-element.35), channel_id=1, source_target_pairs={{0,4},{1,5},{2,6},{3,7},{4,0},{5,1},{6,2},{7,3},{8,12},{9,13},{10,... | collective-permute-start | bytes 393224 | tf_op jit(solution)/shard_map/ppermute | solution.py:471
  10.8 0.0 collective-permute-start.3
  10.9 2.4 %collective-permute-done.1.refs_1_ = bf16[256,256]{1,0:T(8,128)(2,1)S(1)} collective-permute-done((bf16[256,256]{1,0:T(8,128)(2,1)S(1)}, bf16[256,256]{1,0:T(8,128)(2,1)S(1)}, u32[]{:S(2)}, u32[]{:S(2)}) %collective-permute-start.1) | collective-permute-done | bytes 131104 | tf_op jit(solution)/shard_map/ppermute | solution.py:471
  13.2 4.2 %collective-permute-done.2.refs_2_ = bf16[256,256]{1,0:T(8,128)(2,1)S(1)} collective-permute-done((bf16[256,256]{1,0:T(8,128)(2,1)S(1)}, bf16[256,256]{1,0:T(8,128)(2,1)S(1)}, u32[]{:S(2)}, u32[]{:S(2)}) %collective-permute-start.2) | collective-permute-done | bytes 131104 | tf_op jit(solution)/shard_map/ppermute | solution.py:471
  17.4 4.2 %mix_forward.1 = (bf16[256,256]{1,0:T(8,128)(2,1)S(1)}, bf16[1024,256]{1,0:T(8,128)(2,1)S(1)}) custom-call(s32[1]{0:T(128)} %bitcast.here, bf16[256,256]{1,0:T(8,128)(2,1)S(1)} %get-tuple-element.33.refs_0_, bf16[256,256]{1,0:T(8,128)(2,1)S(1)} %collective-permute-done.1.refs_1_, bf16[256,256]{1,0:T(8,128)(2,1)S(1)} %collective-permute-done.2.refs_2_, ...), custom_call_target="tpu_custom_call" | custom-call | flops 67108864 | bytes 8912896 | tf_op jit(solution)/shard_map/mix_forward/pallas_call | solution.py:87
  21.6 1.3 %collective-permute-start.4 = (bf16[256,256]{1,0:T(8,128)(2,1)S(1)}, bf16[256,256]{1,0:T(8,128)(2,1)S(1)}, u32[]{:S(2)}, u32[]{:S(2)}) collective-permute-start(bf16[256,256]{1,0:T(8,128)(2,1)S(1)} %get-tuple-element.37.refs_0_), channel_id=1, source_target_pairs={{0,2},{1,3},{2,0},{3,1},{4,6},{5,7},{6,4},{7,5},{8,10},{9,11},{10,... | collective-permute-start | bytes 393224 | tf_op jit(solution)/shard_map/ppermute | solution.py:474
  22.9 0.9 %collective-permute-start.5 = (bf16[256,256]{1,0:T(8,128)(2,1)S(1)}, bf16[256,256]{1,0:T(8,128)(2,1)S(1)}, u32[]{:S(2)}, u32[]{:S(2)}) collective-permute-start(bf16[256,256]{1,0:T(8,128)(2,1)S(1)} %get-tuple-element.37.refs_0_), channel_id=1, source_target_pairs={{0,4},{1,5},{2,6},{3,7},{4,0},{5,1},{6,2},{7,3},{8,12},{9,13},{10,... | collective-permute-start | bytes 393224 | tf_op jit(solution)/shard_map/ppermute | solution.py:474
  23.7 1.4 %collective-permute-start.6 = (bf16[256,256]{1,0:T(8,128)(2,1)S(1)}, bf16[256,256]{1,0:T(8,128)(2,1)S(1)}, u32[]{:S(2)}, u32[]{:S(2)}) collective-permute-start(bf16[256,256]{1,0:T(8,128)(2,1)S(1)} %get-tuple-element.37.refs_0_), channel_id=1, source_target_pairs={{0,6},{1,7},{2,4},{3,5},{4,2},{5,3},{6,0},{7,1},{8,14},{9,15},{10,... | collective-permute-start | bytes 393224 | tf_op jit(solution)/shard_map/ppermute | solution.py:474
  25.1 0.0 collective-permute-start.7
  25.1 2.5 %collective-permute-done.4.refs_1_ = bf16[256,256]{1,0:T(8,128)(2,1)S(1)} collective-permute-done((bf16[256,256]{1,0:T(8,128)(2,1)S(1)}, bf16[256,256]{1,0:T(8,128)(2,1)S(1)}, u32[]{:S(2)}, u32[]{:S(2)}) %collective-permute-start.4) | collective-permute-done | bytes 131104 | tf_op jit(solution)/shard_map/ppermute | solution.py:474
  27.7 2.4 %collective-permute-done.5.refs_2_ = bf16[256,256]{1,0:T(8,128)(2,1)S(1)} collective-permute-done((bf16[256,256]{1,0:T(8,128)(2,1)S(1)}, bf16[256,256]{1,0:T(8,128)(2,1)S(1)}, u32[]{:S(2)}, u32[]{:S(2)}) %collective-permute-start.5) | collective-permute-done | bytes 131104 | tf_op jit(solution)/shard_map/ppermute | solution.py:474
  30.1 0.0 collective-permute-start.9
  30.1 0.0 collective-permute-done.6.refs_3_
  30.1 0.5 collective-permute-start.10
  30.6 0.0 collective-permute-done.7.refs_4_
  30.6 0.0 collective-permute-done.8.refs_5_
  30.6 0.8 %collective-permute-done.9.refs_6_ = bf16[256,256]{1,0:T(8,128)(2,1)S(1)} collective-permute-done((bf16[256,256]{1,0:T(8,128)(2,1)S(1)}, bf16[256,256]{1,0:T(8,128)(2,1)S(1)}, u32[]{:S(2)}, u32[]{:S(2)}) %collective-permute-start.9) | collective-permute-done | bytes 131104 | tf_op jit(solution)/shard_map/ppermute | solution.py:475
  31.4 0.2 collective-permute-done.10.refs_7_
  31.6 11.6 %middle.1 = (bf16[32,256,256]{2,1,0:T(8,128)(2,1)}, bf16[32,256,256]{2,1,0:T(8,128)(2,1)}, bf16[4,256,256]{2,1,0:T(8,128)(2,1)S(1)}, bf16[4,256,256]{2,1,0:T(8,128)(2,1)}, f32[64,64]{1,0:T(8,128)S(1)}) custom-call(s32[1]{0:T(128)} %bitcast.here, bf16[256,256]{1,0:T(8,128)(2,1)S(1)} %get-tuple-element.37.refs_0_, ...), custom_call_target="tpu_custom_call" | custom-call | flops 2684354560 | bytes 18874368 | tf_op jit(solution)/shard_map/middle/pallas_call | solution.py:87
  43.3 0.3 collective-permute-start.11
  43.6 1.6 %collective-permute-start.14 = (f32[64,64]{1,0:T(8,128)S(1)}, f32[64,64]{1,0:T(8,128)S(1)}, u32[]{:S(2)}, u32[]{:S(2)}) collective-permute-start(f32[64,64]{1,0:T(8,128)S(1)} %get-tuple-element.45), channel_id=1, source_target_pairs={{0,8},{8,0},{16,24},{24,16},{1,9},{9,1},{17,25},{25,17},{2,10},{10... | collective-permute-start | bytes 49160 | tf_op jit(solution)/shard_map/ppermute | solution.py:535
  45.2 0.2 collective-permute-done.11.got_ref
  45.4 0.4 forward_x.3
  45.8 1.3 %collective-permute-start.12 = (bf16[256,256]{1,0:T(8,128)(2,1)S(1)}, bf16[256,256]{1,0:T(8,128)(2,1)S(1)}, u32[]{:S(2)}, u32[]{:S(2)}) collective-permute-start(bf16[256,256]{1,0:T(8,128)(2,1)S(1)} %get-tuple-element.42), channel_id=1, source_target_pairs={{0,2},{1,3},{2,0},{3,1},{4,6},{5,7},{6,4},{7,5},{8,10},{9,11},{10,... | collective-permute-start | bytes 393224 | tf_op jit(solution)/shard_map/ppermute | solution.py:471
  47.2 0.9 %collective-permute-start.13 = (bf16[256,256]{1,0:T(8,128)(2,1)S(1)}, bf16[256,256]{1,0:T(8,128)(2,1)S(1)}, u32[]{:S(2)}, u32[]{:S(2)}) collective-permute-start(bf16[256,256]{1,0:T(8,128)(2,1)S(1)} %get-tuple-element.43), channel_id=1, source_target_pairs={{0,4},{1,5},{2,6},{3,7},{4,0},{5,1},{6,2},{7,3},{8,12},{9,13},{10,... | collective-permute-start | bytes 393224 | tf_op jit(solution)/shard_map/ppermute | solution.py:471
  48.1 1.3 %collective-permute-start.15 = (bf16[256,256]{1,0:T(8,128)(2,1)S(1)}, bf16[256,256]{1,0:T(8,128)(2,1)S(1)}, u32[]{:S(2)}, u32[]{:S(2)}) collective-permute-start(bf16[256,256]{1,0:T(8,128)(2,1)S(1)} %get-tuple-element.46), channel_id=1, source_target_pairs={{0,6},{1,7},{2,4},{3,5},{4,2},{5,3},{6,0},{7,1},{8,14},{9,15},{10,... | collective-permute-start | bytes 393224 | tf_op jit(solution)/shard_map/ppermute | solution.py:471
  49.4 2.6 %collective-permute-start.16 = (f32[64,64]{1,0:T(8,128)S(1)}, f32[64,64]{1,0:T(8,128)S(1)}, u32[]{:S(2)}, u32[]{:S(2)}) collective-permute-start(f32[64,64]{1,0:T(8,128)S(1)} %add.3.refs_4_), channel_id=1, source_target_pairs={{0,16},{8,24},{16,0},{24,8},{1,17},{9,25},{17,1},{25,9},{2,18},{10... | collective-permute-start | bytes 49160 | tf_op jit(solution)/shard_map/ppermute | solution.py:540
  52.0 2.2 %collective-permute-done.16.refs_5_ = f32[64,64]{1,0:T(8,128)S(1)} collective-permute-done((f32[64,64]{1,0:T(8,128)S(1)}, f32[64,64]{1,0:T(8,128)S(1)}, u32[]{:S(2)}, u32[]{:S(2)}) %collective-permute-start.16) | collective-permute-done | bytes 16416 | tf_op jit(solution)/shard_map/ppermute | solution.py:540
  54.2 1.2 %collective-permute-done.13.refs_2_ = bf16[256,256]{1,0:T(8,128)(2,1)S(1)} collective-permute-done((bf16[256,256]{1,0:T(8,128)(2,1)S(1)}, bf16[256,256]{1,0:T(8,128)(2,1)S(1)}, u32[]{:S(2)}, u32[]{:S(2)}) %collective-permute-start.13) | collective-permute-done | bytes 131104 | tf_op jit(solution)/shard_map/ppermute | solution.py:471
  55.4 0.0 collective-permute-done.15.refs_3_
  55.4 4.1 %mix_backward.1 = (bf16[288,256]{1,0:T(8,128)(2,1)S(1)}, f32[1024,128]{1,0:T(8,128)S(1)}) custom-call(s32[1]{0:T(128)} %bitcast.here, bf16[256,256]{1,0:T(8,128)(2,1)S(1)} %get-tuple-element.41.refs_0_, bf16[256,256]{1,0:T(8,128)(2,1)S(1)} %collective-permute-done.12.refs_1_, bf16[256,256]{1,0:T(8,128)(2,1)S(1)} %collective-permute-done.13.refs_2_, ...), custom_call_target="tpu_custom_call" | custom-call | flops 67108864 | bytes 8912896 | tf_op jit(solution)/shard_map/mix_backward/pallas_call | solution.py:87
  59.6 0.8 %collective-permute-start.17 = (bf16[288,256]{1,0:T(8,128)(2,1)S(1)}, bf16[288,256]{1,0:T(8,128)(2,1)S(1)}, u32[]{:S(2)}, u32[]{:S(2)}) collective-permute-start(bf16[288,256]{1,0:T(8,128)(2,1)S(1)} %get-tuple-element.48.refs_0_), channel_id=1, source_target_pairs={{0,2},{1,3},{2,0},{3,1},{4,6},{5,7},{6,4},{7,5},{8,10},{9,11},{10,... | collective-permute-start | bytes 442376 | tf_op jit(solution)/shard_map/ppermute | solution.py:579
  60.4 1.3 %collective-permute-start.18 = (bf16[288,256]{1,0:T(8,128)(2,1)S(1)}, bf16[288,256]{1,0:T(8,128)(2,1)S(1)}, u32[]{:S(2)}, u32[]{:S(2)}) collective-permute-start(bf16[288,256]{1,0:T(8,128)(2,1)S(1)} %get-tuple-element.48.refs_0_), channel_id=1, source_target_pairs={{0,4},{1,5},{2,6},{3,7},{4,0},{5,1},{6,2},{7,3},{8,12},{9,13},{10,... | collective-permute-start | bytes 442376 | tf_op jit(solution)/shard_map/ppermute | solution.py:579
  61.7 1.4 %collective-permute-start.19 = (bf16[288,256]{1,0:T(8,128)(2,1)S(1)}, bf16[288,256]{1,0:T(8,128)(2,1)S(1)}, u32[]{:S(2)}, u32[]{:S(2)}) collective-permute-start(bf16[288,256]{1,0:T(8,128)(2,1)S(1)} %get-tuple-element.48.refs_0_), channel_id=1, source_target_pairs={{0,6},{1,7},{2,4},{3,5},{4,2},{5,3},{6,0},{7,1},{8,14},{9,15},{10,... | collective-permute-start | bytes 442376 | tf_op jit(solution)/shard_map/ppermute | solution.py:579
  63.1 5.3 %gram.2.refs_0_ = f32[4,4,32,64,128]{4,3,2,1,0:T(8,128)} custom-call(s32[1]{0:T(128)} %bitcast.here, bf16[1024,256]{1,0:T(8,128)(2,1)S(1)} %get-tuple-element.49.spread_ref, f32[1024,128]{1,0:T(8,128)S(1)} %get-tuple-element.50.pair_ref), custom_call_target="tpu_custom_call" | custom-call | flops 33554432 | bytes 8388608 | tf_op jit(solution)/shard_map/gram/pallas_call | solution.py:87
  68.4 0.0 copy-start.2
  68.5 0.2 collective-permute-done.18.refs_2_
  68.6 0.4 collective-permute-start.21
  69.1 0.1 collective-permute-start.22
  69.1 0.4 collective-permute-start.23
  69.6 2.4 %gram.3 = f32[4,4,32,64,128]{4,3,2,1,0:T(8,128)} custom-call(s32[1]{0:T(128)} %bitcast.here, bf16[1024,256]{1,0:T(8,128)(2,1)S(1)} %get-tuple-element.49.spread_ref, f32[1024,128]{1,0:T(8,128)S(1)} %get-tuple-element.50.pair_ref, f32[4,4,32,64,128]{4,3,2,1,0:T(8,128)} %gram.2.refs_0_), custom_call_target="tpu_custom_call", output_to_operand_aliasing={{}: (3, {})} | custom-call | flops 33554432 | bytes 8388608 | tf_op jit(solution)/shard_map/gram/pallas_call | solution.py:87
  72.0 6.1 %last.1 = (bf16[32,256,256]{2,1,0:T(8,128)(2,1)}, f32[64,64]{1,0:T(8,128)}) custom-call(s32[1]{0:T(128)} %bitcast.here, bf16[288,256]{1,0:T(8,128)(2,1)S(1)} %get-tuple-element.48.refs_0_, bf16[288,256]{1,0:T(8,128)(2,1)S(1)} %collective-permute-done.17.refs_1_, bf16[288,256]{1,0:T(8,128)(2,1)S(1)} %collective-permute-done.18.refs_2_, ...), custom_call_target="tpu_custom_call" | custom-call | flops 1342177280 | bytes 9437184 | tf_op jit(solution)/shard_map/last/pallas_call | solution.py:87
  (23 shorter events, 0.1 us)
Async XLA Ops:
  0.6 5.3 %copy-start = (bf16[8,256,256]{2,1,0:T(8,128)(2,1)S(1)}, bf16[8,256,256]{2,1,0:T(8,128)(2,1)}, u32[]{:S(2)}) copy-start(bf16[8,256,256]{2,1,0:T(8,128)(2,1)} %constant.12.clone.own_ref.other_ref) | copy-start | bytes 3145732
  3.9 2.1 %collective-permute-start = (bf16[4,256,256]{2,1,0:T(8,128)(2,1)S(1)}, bf16[4,256,256]{2,1,0:T(8,128)(2,1)S(1)}, u32[]{:S(2)}, u32[]{:S(2)}) collective-permute-start(bf16[4,256,256]{2,1,0:T(8,128)(2,1)S(1)} %get-tuple-element.32), channel_id=1, source_target_pairs={{0,1},{1,0},{2,3},{3,2},{4,5},{5,4},{6,7},{7,6},{8,9},{9,8},{10,11... | collective-permute-start | bytes 1572872 | tf_op jit(solution)/shard_map/ppermute | solution.py:448
  6.4 6.8 %collective-permute-start.1 = (bf16[256,256]{1,0:T(8,128)(2,1)S(1)}, bf16[256,256]{1,0:T(8,128)(2,1)S(1)}, u32[]{:S(2)}, u32[]{:S(2)}) collective-permute-start(bf16[256,256]{1,0:T(8,128)(2,1)S(1)} %get-tuple-element.34), channel_id=1, source_target_pairs={{0,2},{1,3},{2,0},{3,1},{4,6},{5,7},{6,4},{7,5},{8,10},{9,11},{10,... | collective-permute-start | bytes 393224 | tf_op jit(solution)/shard_map/ppermute | solution.py:471
  9.3 8.1 %collective-permute-start.2 = (bf16[256,256]{1,0:T(8,128)(2,1)S(1)}, bf16[256,256]{1,0:T(8,128)(2,1)S(1)}, u32[]{:S(2)}, u32[]{:S(2)}) collective-permute-start(bf16[256,256]{1,0:T(8,128)(2,1)S(1)} %get-tuple-element.35), channel_id=1, source_target_pairs={{0,4},{1,5},{2,6},{3,7},{4,0},{5,1},{6,2},{7,3},{8,12},{9,13},{10,... | collective-permute-start | bytes 393224 | tf_op jit(solution)/shard_map/ppermute | solution.py:471
  10.8 6.6 %collective-permute-start.3 = (bf16[256,256]{1,0:T(8,128)(2,1)S(1)}, bf16[256,256]{1,0:T(8,128)(2,1)S(1)}, u32[]{:S(2)}, u32[]{:S(2)}) collective-permute-start(bf16[256,256]{1,0:T(8,128)(2,1)S(1)} %get-tuple-element.36), channel_id=1, source_target_pairs={{0,6},{1,7},{2,4},{3,5},{4,2},{5,3},{6,0},{7,1},{8,14},{9,15},{10,... | collective-permute-start | bytes 393224 | tf_op jit(solution)/shard_map/ppermute | solution.py:471
  17.4 14.2 %copy-start.1 = (bf16[64,64]{1,0:T(8,128)(2,1)S(1)}, bf16[64,64]{1,0:T(8,128)(2,1)}, u32[]{:S(2)}) copy-start(bf16[64,64]{1,0:T(8,128)(2,1)} %refs_10_.3) | copy-start | bytes 24580
  17.4 14.2 %copy-start.3 = (bf16[64,256]{1,0:T(8,128)(2,1)S(1)}, bf16[64,256]{1,0:T(8,128)(2,1)}, u32[]{:S(2)}) copy-start(bf16[64,256]{1,0:T(8,128)(2,1)} %constant.14.clone.refs_9_) | copy-start | bytes 98308
  17.4 38.0 %slice-start = ((s8[8388608]{0:T(1024)(128)(4,1)}), s8[4194304]{0:T(1024)(128)(4,1)S(1)}, s32[]{:S(2)}) async-start(s8[8388608]{0:T(1024)(128)(4,1)} %bitcast.17), calls=%async_computation | async-start | bytes 8388608
  21.6 6.1 %collective-permute-start.4 = (bf16[256,256]{1,0:T(8,128)(2,1)S(1)}, bf16[256,256]{1,0:T(8,128)(2,1)S(1)}, u32[]{:S(2)}, u32[]{:S(2)}) collective-permute-start(bf16[256,256]{1,0:T(8,128)(2,1)S(1)} %get-tuple-element.37.refs_0_), channel_id=1, source_target_pairs={{0,2},{1,3},{2,0},{3,1},{4,6},{5,7},{6,4},{7,5},{8,10},{9,11},{10,... | collective-permute-start | bytes 393224 | tf_op jit(solution)/shard_map/ppermute | solution.py:474
  22.9 7.2 %collective-permute-start.5 = (bf16[256,256]{1,0:T(8,128)(2,1)S(1)}, bf16[256,256]{1,0:T(8,128)(2,1)S(1)}, u32[]{:S(2)}, u32[]{:S(2)}) collective-permute-start(bf16[256,256]{1,0:T(8,128)(2,1)S(1)} %get-tuple-element.37.refs_0_), channel_id=1, source_target_pairs={{0,4},{1,5},{2,6},{3,7},{4,0},{5,1},{6,2},{7,3},{8,12},{9,13},{10,... | collective-permute-start | bytes 393224 | tf_op jit(solution)/shard_map/ppermute | solution.py:474
  23.7 6.4 %collective-permute-start.6 = (bf16[256,256]{1,0:T(8,128)(2,1)S(1)}, bf16[256,256]{1,0:T(8,128)(2,1)S(1)}, u32[]{:S(2)}, u32[]{:S(2)}) collective-permute-start(bf16[256,256]{1,0:T(8,128)(2,1)S(1)} %get-tuple-element.37.refs_0_), channel_id=1, source_target_pairs={{0,6},{1,7},{2,4},{3,5},{4,2},{5,3},{6,0},{7,1},{8,14},{9,15},{10,... | collective-permute-start | bytes 393224 | tf_op jit(solution)/shard_map/ppermute | solution.py:474
  25.1 5.5 %collective-permute-start.7 = (bf16[256,256]{1,0:T(8,128)(2,1)S(1)}, bf16[256,256]{1,0:T(8,128)(2,1)S(1)}, u32[]{:S(2)}, u32[]{:S(2)}) collective-permute-start(bf16[256,256]{1,0:T(8,128)(2,1)S(1)} %get-tuple-element.37.refs_0_), channel_id=1, source_target_pairs={{0,1},{1,0},{2,3},{3,2},{4,5},{5,4},{6,7},{7,6},{8,9},{9,8},{10,11... | collective-permute-start | bytes 393224 | tf_op jit(solution)/shard_map/ppermute | solution.py:475
  27.7 3.0 %collective-permute-start.8 = (bf16[256,256]{1,0:T(8,128)(2,1)S(1)}, bf16[256,256]{1,0:T(8,128)(2,1)S(1)}, u32[]{:S(2)}, u32[]{:S(2)}) collective-permute-start(bf16[256,256]{1,0:T(8,128)(2,1)S(1)} %collective-permute-done.4.refs_1_), channel_id=1, source_target_pairs={{0,1},{1,0},{2,3},{3,2},{4,5},{5,4},{6,7},{7,6},{8,9},{9,8},{10,11... | collective-permute-start | bytes 393224 | tf_op jit(solution)/shard_map/ppermute | solution.py:475
  30.1 1.3 %collective-permute-start.9 = (bf16[256,256]{1,0:T(8,128)(2,1)S(1)}, bf16[256,256]{1,0:T(8,128)(2,1)S(1)}, u32[]{:S(2)}, u32[]{:S(2)}) collective-permute-start(bf16[256,256]{1,0:T(8,128)(2,1)S(1)} %collective-permute-done.5.refs_2_), channel_id=1, source_target_pairs={{0,1},{1,0},{2,3},{3,2},{4,5},{5,4},{6,7},{7,6},{8,9},{9,8},{10,11... | collective-permute-start | bytes 393224 | tf_op jit(solution)/shard_map/ppermute | solution.py:475
  30.1 1.5 %collective-permute-start.10 = (bf16[256,256]{1,0:T(8,128)(2,1)S(1)}, bf16[256,256]{1,0:T(8,128)(2,1)S(1)}, u32[]{:S(2)}, u32[]{:S(2)}) collective-permute-start(bf16[256,256]{1,0:T(8,128)(2,1)S(1)} %collective-permute-done.6.refs_3_), channel_id=1, source_target_pairs={{0,1},{1,0},{2,3},{3,2},{4,5},{5,4},{6,7},{7,6},{8,9},{9,8},{10,11... | collective-permute-start | bytes 393224 | tf_op jit(solution)/shard_map/ppermute | solution.py:475
  31.6 23.8 %slice-start.1 = ((s8[8388608]{0:T(1024)(128)(4,1)}), s8[4194304]{0:T(1024)(128)(4,1)S(1)}, s32[]{:S(2)}) async-start(s8[8388608]{0:T(1024)(128)(4,1)} %bitcast.17), calls=%async_computation.1 | async-start | bytes 8388608
  43.3 2.1 %collective-permute-start.11 = (bf16[4,256,256]{2,1,0:T(8,128)(2,1)}, bf16[4,256,256]{2,1,0:T(8,128)(2,1)S(1)}, u32[]{:S(2)}, u32[]{:S(2)}) collective-permute-start(bf16[4,256,256]{2,1,0:T(8,128)(2,1)} %get-tuple-element.40), channel_id=1, source_target_pairs={{0,1},{1,0},{2,3},{3,2},{4,5},{5,4},{6,7},{7,6},{8,9},{9,8},{10,11... | collective-permute-start | bytes 1572872 | tf_op jit(solution)/shard_map/ppermute | solution.py:448
  43.6 4.5 %collective-permute-start.14 = (f32[64,64]{1,0:T(8,128)S(1)}, f32[64,64]{1,0:T(8,128)S(1)}, u32[]{:S(2)}, u32[]{:S(2)}) collective-permute-start(f32[64,64]{1,0:T(8,128)S(1)} %get-tuple-element.45), channel_id=1, source_target_pairs={{0,8},{8,0},{16,24},{24,16},{1,9},{9,1},{17,25},{25,17},{2,10},{10... | collective-permute-start | bytes 49160 | tf_op jit(solution)/shard_map/ppermute | solution.py:535
  45.8 8.4 %collective-permute-start.12 = (bf16[256,256]{1,0:T(8,128)(2,1)S(1)}, bf16[256,256]{1,0:T(8,128)(2,1)S(1)}, u32[]{:S(2)}, u32[]{:S(2)}) collective-permute-start(bf16[256,256]{1,0:T(8,128)(2,1)S(1)} %get-tuple-element.42), channel_id=1, source_target_pairs={{0,2},{1,3},{2,0},{3,1},{4,6},{5,7},{6,4},{7,5},{8,10},{9,11},{10,... | collective-permute-start | bytes 393224 | tf_op jit(solution)/shard_map/ppermute | solution.py:471
  47.2 8.3 %collective-permute-start.13 = (bf16[256,256]{1,0:T(8,128)(2,1)S(1)}, bf16[256,256]{1,0:T(8,128)(2,1)S(1)}, u32[]{:S(2)}, u32[]{:S(2)}) collective-permute-start(bf16[256,256]{1,0:T(8,128)(2,1)S(1)} %get-tuple-element.43), channel_id=1, source_target_pairs={{0,4},{1,5},{2,6},{3,7},{4,0},{5,1},{6,2},{7,3},{8,12},{9,13},{10,... | collective-permute-start | bytes 393224 | tf_op jit(solution)/shard_map/ppermute | solution.py:471
  48.1 7.4 %collective-permute-start.15 = (bf16[256,256]{1,0:T(8,128)(2,1)S(1)}, bf16[256,256]{1,0:T(8,128)(2,1)S(1)}, u32[]{:S(2)}, u32[]{:S(2)}) collective-permute-start(bf16[256,256]{1,0:T(8,128)(2,1)S(1)} %get-tuple-element.46), channel_id=1, source_target_pairs={{0,6},{1,7},{2,4},{3,5},{4,2},{5,3},{6,0},{7,1},{8,14},{9,15},{10,... | collective-permute-start | bytes 393224 | tf_op jit(solution)/shard_map/ppermute | solution.py:471
  49.4 4.8 %collective-permute-start.16 = (f32[64,64]{1,0:T(8,128)S(1)}, f32[64,64]{1,0:T(8,128)S(1)}, u32[]{:S(2)}, u32[]{:S(2)}) collective-permute-start(f32[64,64]{1,0:T(8,128)S(1)} %add.3.refs_4_), channel_id=1, source_target_pairs={{0,16},{8,24},{16,0},{24,8},{1,17},{9,25},{17,1},{25,9},{2,18},{10... | collective-permute-start | bytes 49160 | tf_op jit(solution)/shard_map/ppermute | solution.py:540
  59.6 8.9 %collective-permute-start.17 = (bf16[288,256]{1,0:T(8,128)(2,1)S(1)}, bf16[288,256]{1,0:T(8,128)(2,1)S(1)}, u32[]{:S(2)}, u32[]{:S(2)}) collective-permute-start(bf16[288,256]{1,0:T(8,128)(2,1)S(1)} %get-tuple-element.48.refs_0_), channel_id=1, source_target_pairs={{0,2},{1,3},{2,0},{3,1},{4,6},{5,7},{6,4},{7,5},{8,10},{9,11},{10,... | collective-permute-start | bytes 442376 | tf_op jit(solution)/shard_map/ppermute | solution.py:579
  60.4 8.2 %collective-permute-start.18 = (bf16[288,256]{1,0:T(8,128)(2,1)S(1)}, bf16[288,256]{1,0:T(8,128)(2,1)S(1)}, u32[]{:S(2)}, u32[]{:S(2)}) collective-permute-start(bf16[288,256]{1,0:T(8,128)(2,1)S(1)} %get-tuple-element.48.refs_0_), channel_id=1, source_target_pairs={{0,4},{1,5},{2,6},{3,7},{4,0},{5,1},{6,2},{7,3},{8,12},{9,13},{10,... | collective-permute-start | bytes 442376 | tf_op jit(solution)/shard_map/ppermute | solution.py:579
  61.7 7.0 %collective-permute-start.19 = (bf16[288,256]{1,0:T(8,128)(2,1)S(1)}, bf16[288,256]{1,0:T(8,128)(2,1)S(1)}, u32[]{:S(2)}, u32[]{:S(2)}) collective-permute-start(bf16[288,256]{1,0:T(8,128)(2,1)S(1)} %get-tuple-element.48.refs_0_), channel_id=1, source_target_pairs={{0,6},{1,7},{2,4},{3,5},{4,2},{5,3},{6,0},{7,1},{8,14},{9,15},{10,... | collective-permute-start | bytes 442376 | tf_op jit(solution)/shard_map/ppermute | solution.py:579
  63.1 8.8 %collective-permute-start.20 = (bf16[288,256]{1,0:T(8,128)(2,1)S(1)}, bf16[288,256]{1,0:T(8,128)(2,1)S(1)}, u32[]{:S(2)}, u32[]{:S(2)}) collective-permute-start(bf16[288,256]{1,0:T(8,128)(2,1)S(1)} %get-tuple-element.48.refs_0_), channel_id=1, source_target_pairs={{0,1},{1,0},{2,3},{3,2},{4,5},{5,4},{6,7},{7,6},{8,9},{9,8},{10,11... | collective-permute-start | bytes 442376 | tf_op jit(solution)/shard_map/ppermute | solution.py:582
  68.4 3.6 %copy-start.2 = (bf16[64,256]{1,0:T(8,128)(2,1)S(1)}, bf16[64,256]{1,0:T(8,128)(2,1)}, u32[]{:S(2)}) copy-start(bf16[64,256]{1,0:T(8,128)(2,1)} %constant.15.clone.refs_9_) | copy-start | bytes 98308
  68.6 3.3 %collective-permute-start.21 = (bf16[288,256]{1,0:T(8,128)(2,1)S(1)}, bf16[288,256]{1,0:T(8,128)(2,1)S(1)}, u32[]{:S(2)}, u32[]{:S(2)}) collective-permute-start(bf16[288,256]{1,0:T(8,128)(2,1)S(1)} %collective-permute-done.17.refs_1_), channel_id=1, source_target_pairs={{0,1},{1,0},{2,3},{3,2},{4,5},{5,4},{6,7},{7,6},{8,9},{9,8},{10,11... | collective-permute-start | bytes 442376 | tf_op jit(solution)/shard_map/ppermute | solution.py:582
  69.1 2.9 %collective-permute-start.22 = (bf16[288,256]{1,0:T(8,128)(2,1)S(1)}, bf16[288,256]{1,0:T(8,128)(2,1)S(1)}, u32[]{:S(2)}, u32[]{:S(2)}) collective-permute-start(bf16[288,256]{1,0:T(8,128)(2,1)S(1)} %collective-permute-done.18.refs_2_), channel_id=1, source_target_pairs={{0,1},{1,0},{2,3},{3,2},{4,5},{5,4},{6,7},{7,6},{8,9},{9,8},{10,11... | collective-permute-start | bytes 442376 | tf_op jit(solution)/shard_map/ppermute | solution.py:582
  69.1 2.9 %collective-permute-start.23 = (bf16[288,256]{1,0:T(8,128)(2,1)S(1)}, bf16[288,256]{1,0:T(8,128)(2,1)S(1)}, u32[]{:S(2)}, u32[]{:S(2)}) collective-permute-start(bf16[288,256]{1,0:T(8,128)(2,1)S(1)} %collective-permute-done.19.refs_3_), channel_id=1, source_target_pairs={{0,1},{1,0},{2,3},{3,2},{4,5},{5,4},{6,7},{7,6},{8,9},{9,8},{10,11... | collective-permute-start | bytes 442376 | tf_op jit(solution)/shard_map/ppermute | solution.py:582

commit v8 on v7

--- a/solution.py
+++ b/solution.py
@@ -474,13 +474,14 @@
         mine = [block] + [flip("mp", count, 2 * bit)(block) for bit in range(1, chips)]
         return mine + [flip("mp", count, 1)(value) for value in mine]
 
-    per = 16
-    mode_steps = modes // per
     weight_spec = pl.BlockSpec(memory_space=pl.ANY)
-    weight_scratch = [
-        pltpu.VMEM((mode_steps, zs, 1, per, channels, 2 * channels), BF16),
-        pltpu.SemaphoreType.DMA((mode_steps,)),
-    ]
+
+    def weight_scratch(per):
+        return [
+            pltpu.VMEM((modes // per, zs, 1, per, channels, 2 * channels), BF16),
+            pltpu.SemaphoreType.DMA((modes // per,)),
+        ]
+
     spread_shape = (modes * 2 * zs, columns)
     pair_shape = (modes * 2 * zs, 2 * channels)
     weight_bytes = zs * modes * channels * 2 * channels * 2
@@ -507,11 +508,11 @@
         functools.partial(mix_forward, chips, zs),
         here,
         (*terms, spectral_weight),
-        (mode_steps,),
+        (modes // 16,),
         [mode_spec] * chips + [weight_spec],
         [mode_spec, whole(spread_shape)],
         [mode_shape, jax.ShapeDtypeStruct(spread_shape, BF16)],
-        [pltpu.VMEM((2 * modes, columns), F32), pltpu.VMEM(pair_shape, F32)] + weight_scratch,
+        [pltpu.VMEM((2 * modes, columns), F32), pltpu.VMEM(pair_shape, F32)] + weight_scratch(16),
         flops=weight_bytes * 8,
         moved=weight_bytes + mode_bytes * chips,
         name="mix_forward",
@@ -543,11 +544,11 @@
         functools.partial(mix_backward, chips, zs),
         here,
         (*terms, *locals_, spectral_weight),
-        (mode_steps,),
+        (modes // KX,),
         [mode_spec] * chips + [weight_small] * len(locals_) + [weight_spec],
         [back_spec, whole(pair_shape)],
         [back_shape, jax.ShapeDtypeStruct(pair_shape, F32)],
-        [pltpu.VMEM((zs // 2, modes * 2 * zs, 128), F32)] + weight_scratch,
+        [pltpu.VMEM((zs // 2, modes * 2 * zs, 128), F32)] + weight_scratch(KX),
         flops=weight_bytes * 8,
         moved=weight_bytes + mode_bytes * chips,
         name="mix_backward",

time: 78.3 us -> 77.8 us (level)
  no operation moved by 1% of the time
where the time goes in v8:
time: 77.8 us; the launch traced here: 77.6 us
  Pallas kernels  37.3 us (48%)
  starting transfers between devices  21.6 us (28%)
  waiting for transfers between devices  17.9 us (23%)
  between operations  0.8 us (1%)
    pallas_call x9, Pallas kernels, call(): pl.pallas_call(kernel, out_shape=out_shape, grid_spec=pltpu.PrefetchScala...  37.3 us
    ppermute x6, starting transfers between devices, to_chips(): flip('mp', count, 2 * bit)(outs[bit])  8.01 us
    ppermute x6, waiting for transfers between devices, to_chips(): flip('mp', count, 2 * bit)(outs[bit])  7.74 us
    ppermute x3, waiting for transfers between devices, to_all(): flip('mp', count, 2 * bit)(block)  4.95 us
    ppermute x3, starting transfers between devices, to_all(): flip('mp', count, 2 * bit)(block)  3.55 us
    ppermute x3, starting transfers between devices, body(): flip('mp', count, 2 * bit)(back)  3.55 us
    ppermute x1, starting transfers between devices, body(): locals_ = [local_term, flip('dp', dp_count, bit)(local_term)]  2.59 us
    ppermute x1, waiting for transfers between devices, body(): locals_ = [local_term, flip('dp', dp_count, bit)(local_term)]  2.22 us
  transfers between devices with their start and end apart: 24, of which 11 were waited for; matrix products, arithmetic and copies ran while one was open for 0% of the time, Pallas kernels for 10%

profile of v8, /device:TPU:0, one launch (start us, length us, event | category | flops | bytes accessed | tf_op | source)
XLA Modules:
  0.0 77.6 jit_solution(3329214964418231097)
XLA Ops:
  0.6 0.0 copy-start
  0.6 3.2 %forward_y.1 = (bf16[4,256,256]{2,1,0:T(8,128)(2,1)S(1)}, bf16[4,256,256]{2,1,0:T(8,128)(2,1)S(1)}) custom-call(s32[1]{0:T(128)} %bitcast.here, bf16[32,256,256]{2,1,0:T(8,128)(2,1)} %bitcast.19), custom_call_target="tpu_custom_call" | custom-call | flops 268435456 | bytes 5242880 | tf_op jit(solution)/shard_map/forward_y/pallas_call | solution.py:87
  3.9 0.5 collective-permute-start
  4.4 1.5 %collective-permute-done.got_ref = bf16[4,256,256]{2,1,0:T(8,128)(2,1)S(1)} collective-permute-done((bf16[4,256,256]{2,1,0:T(8,128)(2,1)S(1)}, bf16[4,256,256]{2,1,0:T(8,128)(2,1)S(1)}, u32[]{:S(2)}, u32[]{:S(2)}) %collective-permute-start) | collective-permute-done | bytes 524320 | tf_op jit(solution)/shard_map/ppermute | solution.py:448
  6.0 0.4 forward_x.2
  6.4 2.9 %collective-permute-start.1 = (bf16[256,256]{1,0:T(8,128)(2,1)S(1)}, bf16[256,256]{1,0:T(8,128)(2,1)S(1)}, u32[]{:S(2)}, u32[]{:S(2)}) collective-permute-start(bf16[256,256]{1,0:T(8,128)(2,1)S(1)} %get-tuple-element.34), channel_id=1, source_target_pairs={{0,2},{1,3},{2,0},{3,1},{4,6},{5,7},{6,4},{7,5},{8,10},{9,11},{10,... | collective-permute-start | bytes 393224 | tf_op jit(solution)/shard_map/ppermute | solution.py:471
  9.3 1.5 %collective-permute-start.2 = (bf16[256,256]{1,0:T(8,128)(2,1)S(1)}, bf16[256,256]{1,0:T(8,128)(2,1)S(1)}, u32[]{:S(2)}, u32[]{:S(2)}) collective-permute-start(bf16[256,256]{1,0:T(8,128)(2,1)S(1)} %get-tuple-element.35), channel_id=1, source_target_pairs={{0,4},{1,5},{2,6},{3,7},{4,0},{5,1},{6,2},{7,3},{8,12},{9,13},{10,... | collective-permute-start | bytes 393224 | tf_op jit(solution)/shard_map/ppermute | solution.py:471
  10.8 0.0 collective-permute-start.3
  10.9 2.4 %collective-permute-done.1.refs_1_ = bf16[256,256]{1,0:T(8,128)(2,1)S(1)} collective-permute-done((bf16[256,256]{1,0:T(8,128)(2,1)S(1)}, bf16[256,256]{1,0:T(8,128)(2,1)S(1)}, u32[]{:S(2)}, u32[]{:S(2)}) %collective-permute-start.1) | collective-permute-done | bytes 131104 | tf_op jit(solution)/shard_map/ppermute | solution.py:471
  13.2 4.2 %collective-permute-done.2.refs_2_ = bf16[256,256]{1,0:T(8,128)(2,1)S(1)} collective-permute-done((bf16[256,256]{1,0:T(8,128)(2,1)S(1)}, bf16[256,256]{1,0:T(8,128)(2,1)S(1)}, u32[]{:S(2)}, u32[]{:S(2)}) %collective-permute-start.2) | collective-permute-done | bytes 131104 | tf_op jit(solution)/shard_map/ppermute | solution.py:471
  17.4 4.2 %mix_forward.1 = (bf16[256,256]{1,0:T(8,128)(2,1)S(1)}, bf16[1024,256]{1,0:T(8,128)(2,1)S(1)}) custom-call(s32[1]{0:T(128)} %bitcast.here, bf16[256,256]{1,0:T(8,128)(2,1)S(1)} %get-tuple-element.33.refs_0_, bf16[256,256]{1,0:T(8,128)(2,1)S(1)} %collective-permute-done.1.refs_1_, bf16[256,256]{1,0:T(8,128)(2,1)S(1)} %collective-permute-done.2.refs_2_, ...), custom_call_target="tpu_custom_call" | custom-call | flops 67108864 | bytes 8912896 | tf_op jit(solution)/shard_map/mix_forward/pallas_call | solution.py:87
  21.6 1.3 %collective-permute-start.4 = (bf16[256,256]{1,0:T(8,128)(2,1)S(1)}, bf16[256,256]{1,0:T(8,128)(2,1)S(1)}, u32[]{:S(2)}, u32[]{:S(2)}) collective-permute-start(bf16[256,256]{1,0:T(8,128)(2,1)S(1)} %get-tuple-element.37.refs_0_), channel_id=1, source_target_pairs={{0,2},{1,3},{2,0},{3,1},{4,6},{5,7},{6,4},{7,5},{8,10},{9,11},{10,... | collective-permute-start | bytes 393224 | tf_op jit(solution)/shard_map/ppermute | solution.py:474
  22.9 0.9 %collective-permute-start.5 = (bf16[256,256]{1,0:T(8,128)(2,1)S(1)}, bf16[256,256]{1,0:T(8,128)(2,1)S(1)}, u32[]{:S(2)}, u32[]{:S(2)}) collective-permute-start(bf16[256,256]{1,0:T(8,128)(2,1)S(1)} %get-tuple-element.37.refs_0_), channel_id=1, source_target_pairs={{0,4},{1,5},{2,6},{3,7},{4,0},{5,1},{6,2},{7,3},{8,12},{9,13},{10,... | collective-permute-start | bytes 393224 | tf_op jit(solution)/shard_map/ppermute | solution.py:474
  23.7 1.4 %collective-permute-start.6 = (bf16[256,256]{1,0:T(8,128)(2,1)S(1)}, bf16[256,256]{1,0:T(8,128)(2,1)S(1)}, u32[]{:S(2)}, u32[]{:S(2)}) collective-permute-start(bf16[256,256]{1,0:T(8,128)(2,1)S(1)} %get-tuple-element.37.refs_0_), channel_id=1, source_target_pairs={{0,6},{1,7},{2,4},{3,5},{4,2},{5,3},{6,0},{7,1},{8,14},{9,15},{10,... | collective-permute-start | bytes 393224 | tf_op jit(solution)/shard_map/ppermute | solution.py:474
  25.1 0.0 collective-permute-start.7
  25.1 2.5 %collective-permute-done.4.refs_1_ = bf16[256,256]{1,0:T(8,128)(2,1)S(1)} collective-permute-done((bf16[256,256]{1,0:T(8,128)(2,1)S(1)}, bf16[256,256]{1,0:T(8,128)(2,1)S(1)}, u32[]{:S(2)}, u32[]{:S(2)}) %collective-permute-start.4) | collective-permute-done | bytes 131104 | tf_op jit(solution)/shard_map/ppermute | solution.py:474
  27.7 2.4 %collective-permute-done.5.refs_2_ = bf16[256,256]{1,0:T(8,128)(2,1)S(1)} collective-permute-done((bf16[256,256]{1,0:T(8,128)(2,1)S(1)}, bf16[256,256]{1,0:T(8,128)(2,1)S(1)}, u32[]{:S(2)}, u32[]{:S(2)}) %collective-permute-start.5) | collective-permute-done | bytes 131104 | tf_op jit(solution)/shard_map/ppermute | solution.py:474
  30.1 0.0 collective-permute-start.9
  30.1 0.0 collective-permute-done.6.refs_3_
  30.1 0.5 collective-permute-start.10
  30.6 0.0 collective-permute-done.7.refs_4_
  30.6 0.0 collective-permute-done.8.refs_5_
  30.6 0.8 %collective-permute-done.9.refs_6_ = bf16[256,256]{1,0:T(8,128)(2,1)S(1)} collective-permute-done((bf16[256,256]{1,0:T(8,128)(2,1)S(1)}, bf16[256,256]{1,0:T(8,128)(2,1)S(1)}, u32[]{:S(2)}, u32[]{:S(2)}) %collective-permute-start.9) | collective-permute-done | bytes 131104 | tf_op jit(solution)/shard_map/ppermute | solution.py:475
  31.4 0.2 collective-permute-done.10.refs_7_
  31.6 11.6 %middle.1 = (bf16[32,256,256]{2,1,0:T(8,128)(2,1)}, bf16[32,256,256]{2,1,0:T(8,128)(2,1)}, bf16[4,256,256]{2,1,0:T(8,128)(2,1)S(1)}, bf16[4,256,256]{2,1,0:T(8,128)(2,1)}, f32[64,64]{1,0:T(8,128)S(1)}) custom-call(s32[1]{0:T(128)} %bitcast.here, bf16[256,256]{1,0:T(8,128)(2,1)S(1)} %get-tuple-element.37.refs_0_, ...), custom_call_target="tpu_custom_call" | custom-call | flops 2684354560 | bytes 18874368 | tf_op jit(solution)/shard_map/middle/pallas_call | solution.py:87
  43.3 0.3 collective-permute-start.11
  43.6 1.6 %collective-permute-start.14 = (f32[64,64]{1,0:T(8,128)S(1)}, f32[64,64]{1,0:T(8,128)S(1)}, u32[]{:S(2)}, u32[]{:S(2)}) collective-permute-start(f32[64,64]{1,0:T(8,128)S(1)} %get-tuple-element.45), channel_id=1, source_target_pairs={{0,8},{8,0},{16,24},{24,16},{1,9},{9,1},{17,25},{25,17},{2,10},{10... | collective-permute-start | bytes 49160 | tf_op jit(solution)/shard_map/ppermute | solution.py:536
  45.2 0.2 collective-permute-done.11.got_ref
  45.4 0.4 forward_x.3
  45.8 1.3 %collective-permute-start.12 = (bf16[256,256]{1,0:T(8,128)(2,1)S(1)}, bf16[256,256]{1,0:T(8,128)(2,1)S(1)}, u32[]{:S(2)}, u32[]{:S(2)}) collective-permute-start(bf16[256,256]{1,0:T(8,128)(2,1)S(1)} %get-tuple-element.42), channel_id=1, source_target_pairs={{0,2},{1,3},{2,0},{3,1},{4,6},{5,7},{6,4},{7,5},{8,10},{9,11},{10,... | collective-permute-start | bytes 393224 | tf_op jit(solution)/shard_map/ppermute | solution.py:471
  47.2 0.9 %collective-permute-start.13 = (bf16[256,256]{1,0:T(8,128)(2,1)S(1)}, bf16[256,256]{1,0:T(8,128)(2,1)S(1)}, u32[]{:S(2)}, u32[]{:S(2)}) collective-permute-start(bf16[256,256]{1,0:T(8,128)(2,1)S(1)} %get-tuple-element.43), channel_id=1, source_target_pairs={{0,4},{1,5},{2,6},{3,7},{4,0},{5,1},{6,2},{7,3},{8,12},{9,13},{10,... | collective-permute-start | bytes 393224 | tf_op jit(solution)/shard_map/ppermute | solution.py:471
  48.1 1.3 %collective-permute-start.15 = (bf16[256,256]{1,0:T(8,128)(2,1)S(1)}, bf16[256,256]{1,0:T(8,128)(2,1)S(1)}, u32[]{:S(2)}, u32[]{:S(2)}) collective-permute-start(bf16[256,256]{1,0:T(8,128)(2,1)S(1)} %get-tuple-element.46), channel_id=1, source_target_pairs={{0,6},{1,7},{2,4},{3,5},{4,2},{5,3},{6,0},{7,1},{8,14},{9,15},{10,... | collective-permute-start | bytes 393224 | tf_op jit(solution)/shard_map/ppermute | solution.py:471
  49.4 2.6 %collective-permute-start.16 = (f32[64,64]{1,0:T(8,128)S(1)}, f32[64,64]{1,0:T(8,128)S(1)}, u32[]{:S(2)}, u32[]{:S(2)}) collective-permute-start(f32[64,64]{1,0:T(8,128)S(1)} %add.3.refs_4_), channel_id=1, source_target_pairs={{0,16},{8,24},{16,0},{24,8},{1,17},{9,25},{17,1},{25,9},{2,18},{10... | collective-permute-start | bytes 49160 | tf_op jit(solution)/shard_map/ppermute | solution.py:541
  52.0 2.2 %collective-permute-done.16.refs_5_ = f32[64,64]{1,0:T(8,128)S(1)} collective-permute-done((f32[64,64]{1,0:T(8,128)S(1)}, f32[64,64]{1,0:T(8,128)S(1)}, u32[]{:S(2)}, u32[]{:S(2)}) %collective-permute-start.16) | collective-permute-done | bytes 16416 | tf_op jit(solution)/shard_map/ppermute | solution.py:541
  54.2 1.2 %collective-permute-done.13.refs_2_ = bf16[256,256]{1,0:T(8,128)(2,1)S(1)} collective-permute-done((bf16[256,256]{1,0:T(8,128)(2,1)S(1)}, bf16[256,256]{1,0:T(8,128)(2,1)S(1)}, u32[]{:S(2)}, u32[]{:S(2)}) %collective-permute-start.13) | collective-permute-done | bytes 131104 | tf_op jit(solution)/shard_map/ppermute | solution.py:471
  55.4 0.0 collective-permute-done.15.refs_3_
  55.4 3.6 %mix_backward.1 = (bf16[288,256]{1,0:T(8,128)(2,1)S(1)}, f32[1024,128]{1,0:T(8,128)S(1)}) custom-call(s32[1]{0:T(128)} %bitcast.here, bf16[256,256]{1,0:T(8,128)(2,1)S(1)} %get-tuple-element.41.refs_0_, bf16[256,256]{1,0:T(8,128)(2,1)S(1)} %collective-permute-done.12.refs_1_, bf16[256,256]{1,0:T(8,128)(2,1)S(1)} %collective-permute-done.13.refs_2_, ...), custom_call_target="tpu_custom_call" | custom-call | flops 67108864 | bytes 8912896 | tf_op jit(solution)/shard_map/mix_backward/pallas_call | solution.py:87
  59.1 0.8 %collective-permute-start.17 = (bf16[288,256]{1,0:T(8,128)(2,1)S(1)}, bf16[288,256]{1,0:T(8,128)(2,1)S(1)}, u32[]{:S(2)}, u32[]{:S(2)}) collective-permute-start(bf16[288,256]{1,0:T(8,128)(2,1)S(1)} %get-tuple-element.48.refs_0_), channel_id=1, source_target_pairs={{0,2},{1,3},{2,0},{3,1},{4,6},{5,7},{6,4},{7,5},{8,10},{9,11},{10,... | collective-permute-start | bytes 442376 | tf_op jit(solution)/shard_map/ppermute | solution.py:580
  59.9 1.3 %collective-permute-start.18 = (bf16[288,256]{1,0:T(8,128)(2,1)S(1)}, bf16[288,256]{1,0:T(8,128)(2,1)S(1)}, u32[]{:S(2)}, u32[]{:S(2)}) collective-permute-start(bf16[288,256]{1,0:T(8,128)(2,1)S(1)} %get-tuple-element.48.refs_0_), channel_id=1, source_target_pairs={{0,4},{1,5},{2,6},{3,7},{4,0},{5,1},{6,2},{7,3},{8,12},{9,13},{10,... | collective-permute-start | bytes 442376 | tf_op jit(solution)/shard_map/ppermute | solution.py:580
  61.2 1.4 %collective-permute-start.19 = (bf16[288,256]{1,0:T(8,128)(2,1)S(1)}, bf16[288,256]{1,0:T(8,128)(2,1)S(1)}, u32[]{:S(2)}, u32[]{:S(2)}) collective-permute-start(bf16[288,256]{1,0:T(8,128)(2,1)S(1)} %get-tuple-element.48.refs_0_), channel_id=1, source_target_pairs={{0,6},{1,7},{2,4},{3,5},{4,2},{5,3},{6,0},{7,1},{8,14},{9,15},{10,... | collective-permute-start | bytes 442376 | tf_op jit(solution)/shard_map/ppermute | solution.py:580
  62.6 5.3 %gram.2.refs_0_ = f32[4,4,32,64,128]{4,3,2,1,0:T(8,128)} custom-call(s32[1]{0:T(128)} %bitcast.here, bf16[1024,256]{1,0:T(8,128)(2,1)S(1)} %get-tuple-element.49.spread_ref, f32[1024,128]{1,0:T(8,128)S(1)} %get-tuple-element.50.pair_ref), custom_call_target="tpu_custom_call" | custom-call | flops 33554432 | bytes 8388608 | tf_op jit(solution)/shard_map/gram/pallas_call | solution.py:87
  67.9 0.0 copy-start.2
  68.0 0.2 collective-permute-done.18.refs_2_
  68.1 0.4 collective-permute-start.21
  68.6 0.1 collective-permute-start.22
  68.6 0.4 collective-permute-start.23
  69.1 2.4 %gram.3 = f32[4,4,32,64,128]{4,3,2,1,0:T(8,128)} custom-call(s32[1]{0:T(128)} %bitcast.here, bf16[1024,256]{1,0:T(8,128)(2,1)S(1)} %get-tuple-element.49.spread_ref, f32[1024,128]{1,0:T(8,128)S(1)} %get-tuple-element.50.pair_ref, f32[4,4,32,64,128]{4,3,2,1,0:T(8,128)} %gram.2.refs_0_), custom_call_target="tpu_custom_call", output_to_operand_aliasing={{}: (3, {})} | custom-call | flops 33554432 | bytes 8388608 | tf_op jit(solution)/shard_map/gram/pallas_call | solution.py:87
  71.5 6.1 %last.1 = (bf16[32,256,256]{2,1,0:T(8,128)(2,1)}, f32[64,64]{1,0:T(8,128)}) custom-call(s32[1]{0:T(128)} %bitcast.here, bf16[288,256]{1,0:T(8,128)(2,1)S(1)} %get-tuple-element.48.refs_0_, bf16[288,256]{1,0:T(8,128)(2,1)S(1)} %collective-permute-done.17.refs_1_, bf16[288,256]{1,0:T(8,128)(2,1)S(1)} %collective-permute-done.18.refs_2_, ...), custom_call_target="tpu_custom_call" | custom-call | flops 1342177280 | bytes 9437184 | tf_op jit(solution)/shard_map/last/pallas_call | solution.py:87
  (23 shorter events, 0.1 us)
Async XLA Ops:
  0.6 5.3 %copy-start = (bf16[8,256,256]{2,1,0:T(8,128)(2,1)S(1)}, bf16[8,256,256]{2,1,0:T(8,128)(2,1)}, u32[]{:S(2)}) copy-start(bf16[8,256,256]{2,1,0:T(8,128)(2,1)} %constant.12.clone.own_ref.other_ref) | copy-start | bytes 3145732
  3.9 2.1 %collective-permute-start = (bf16[4,256,256]{2,1,0:T(8,128)(2,1)S(1)}, bf16[4,256,256]{2,1,0:T(8,128)(2,1)S(1)}, u32[]{:S(2)}, u32[]{:S(2)}) collective-permute-start(bf16[4,256,256]{2,1,0:T(8,128)(2,1)S(1)} %get-tuple-element.32), channel_id=1, source_target_pairs={{0,1},{1,0},{2,3},{3,2},{4,5},{5,4},{6,7},{7,6},{8,9},{9,8},{10,11... | collective-permute-start | bytes 1572872 | tf_op jit(solution)/shard_map/ppermute | solution.py:448
  6.4 6.8 %collective-permute-start.1 = (bf16[256,256]{1,0:T(8,128)(2,1)S(1)}, bf16[256,256]{1,0:T(8,128)(2,1)S(1)}, u32[]{:S(2)}, u32[]{:S(2)}) collective-permute-start(bf16[256,256]{1,0:T(8,128)(2,1)S(1)} %get-tuple-element.34), channel_id=1, source_target_pairs={{0,2},{1,3},{2,0},{3,1},{4,6},{5,7},{6,4},{7,5},{8,10},{9,11},{10,... | collective-permute-start | bytes 393224 | tf_op jit(solution)/shard_map/ppermute | solution.py:471
  9.3 8.1 %collective-permute-start.2 = (bf16[256,256]{1,0:T(8,128)(2,1)S(1)}, bf16[256,256]{1,0:T(8,128)(2,1)S(1)}, u32[]{:S(2)}, u32[]{:S(2)}) collective-permute-start(bf16[256,256]{1,0:T(8,128)(2,1)S(1)} %get-tuple-element.35), channel_id=1, source_target_pairs={{0,4},{1,5},{2,6},{3,7},{4,0},{5,1},{6,2},{7,3},{8,12},{9,13},{10,... | collective-permute-start | bytes 393224 | tf_op jit(solution)/shard_map/ppermute | solution.py:471
  10.8 6.6 %collective-permute-start.3 = (bf16[256,256]{1,0:T(8,128)(2,1)S(1)}, bf16[256,256]{1,0:T(8,128)(2,1)S(1)}, u32[]{:S(2)}, u32[]{:S(2)}) collective-permute-start(bf16[256,256]{1,0:T(8,128)(2,1)S(1)} %get-tuple-element.36), channel_id=1, source_target_pairs={{0,6},{1,7},{2,4},{3,5},{4,2},{5,3},{6,0},{7,1},{8,14},{9,15},{10,... | collective-permute-start | bytes 393224 | tf_op jit(solution)/shard_map/ppermute | solution.py:471
  17.4 14.2 %copy-start.1 = (bf16[64,64]{1,0:T(8,128)(2,1)S(1)}, bf16[64,64]{1,0:T(8,128)(2,1)}, u32[]{:S(2)}) copy-start(bf16[64,64]{1,0:T(8,128)(2,1)} %refs_10_.3) | copy-start | bytes 24580
  17.4 14.2 %copy-start.3 = (bf16[64,256]{1,0:T(8,128)(2,1)S(1)}, bf16[64,256]{1,0:T(8,128)(2,1)}, u32[]{:S(2)}) copy-start(bf16[64,256]{1,0:T(8,128)(2,1)} %constant.14.clone.refs_9_) | copy-start | bytes 98308
  17.4 38.0 %slice-start = ((s8[8388608]{0:T(1024)(128)(4,1)}), s8[4194304]{0:T(1024)(128)(4,1)S(1)}, s32[]{:S(2)}) async-start(s8[8388608]{0:T(1024)(128)(4,1)} %bitcast.17), calls=%async_computation | async-start | bytes 8388608
  21.6 6.1 %collective-permute-start.4 = (bf16[256,256]{1,0:T(8,128)(2,1)S(1)}, bf16[256,256]{1,0:T(8,128)(2,1)S(1)}, u32[]{:S(2)}, u32[]{:S(2)}) collective-permute-start(bf16[256,256]{1,0:T(8,128)(2,1)S(1)} %get-tuple-element.37.refs_0_), channel_id=1, source_target_pairs={{0,2},{1,3},{2,0},{3,1},{4,6},{5,7},{6,4},{7,5},{8,10},{9,11},{10,... | collective-permute-start | bytes 393224 | tf_op jit(solution)/shard_map/ppermute | solution.py:474
  22.9 7.2 %collective-permute-start.5 = (bf16[256,256]{1,0:T(8,128)(2,1)S(1)}, bf16[256,256]{1,0:T(8,128)(2,1)S(1)}, u32[]{:S(2)}, u32[]{:S(2)}) collective-permute-start(bf16[256,256]{1,0:T(8,128)(2,1)S(1)} %get-tuple-element.37.refs_0_), channel_id=1, source_target_pairs={{0,4},{1,5},{2,6},{3,7},{4,0},{5,1},{6,2},{7,3},{8,12},{9,13},{10,... | collective-permute-start | bytes 393224 | tf_op jit(solution)/shard_map/ppermute | solution.py:474
  23.7 6.4 %collective-permute-start.6 = (bf16[256,256]{1,0:T(8,128)(2,1)S(1)}, bf16[256,256]{1,0:T(8,128)(2,1)S(1)}, u32[]{:S(2)}, u32[]{:S(2)}) collective-permute-start(bf16[256,256]{1,0:T(8,128)(2,1)S(1)} %get-tuple-element.37.refs_0_), channel_id=1, source_target_pairs={{0,6},{1,7},{2,4},{3,5},{4,2},{5,3},{6,0},{7,1},{8,14},{9,15},{10,... | collective-permute-start | bytes 393224 | tf_op jit(solution)/shard_map/ppermute | solution.py:474
  25.1 5.5 %collective-permute-start.7 = (bf16[256,256]{1,0:T(8,128)(2,1)S(1)}, bf16[256,256]{1,0:T(8,128)(2,1)S(1)}, u32[]{:S(2)}, u32[]{:S(2)}) collective-permute-start(bf16[256,256]{1,0:T(8,128)(2,1)S(1)} %get-tuple-element.37.refs_0_), channel_id=1, source_target_pairs={{0,1},{1,0},{2,3},{3,2},{4,5},{5,4},{6,7},{7,6},{8,9},{9,8},{10,11... | collective-permute-start | bytes 393224 | tf_op jit(solution)/shard_map/ppermute | solution.py:475
  27.7 3.0 %collective-permute-start.8 = (bf16[256,256]{1,0:T(8,128)(2,1)S(1)}, bf16[256,256]{1,0:T(8,128)(2,1)S(1)}, u32[]{:S(2)}, u32[]{:S(2)}) collective-permute-start(bf16[256,256]{1,0:T(8,128)(2,1)S(1)} %collective-permute-done.4.refs_1_), channel_id=1, source_target_pairs={{0,1},{1,0},{2,3},{3,2},{4,5},{5,4},{6,7},{7,6},{8,9},{9,8},{10,11... | collective-permute-start | bytes 393224 | tf_op jit(solution)/shard_map/ppermute | solution.py:475
  30.1 1.3 %collective-permute-start.9 = (bf16[256,256]{1,0:T(8,128)(2,1)S(1)}, bf16[256,256]{1,0:T(8,128)(2,1)S(1)}, u32[]{:S(2)}, u32[]{:S(2)}) collective-permute-start(bf16[256,256]{1,0:T(8,128)(2,1)S(1)} %collective-permute-done.5.refs_2_), channel_id=1, source_target_pairs={{0,1},{1,0},{2,3},{3,2},{4,5},{5,4},{6,7},{7,6},{8,9},{9,8},{10,11... | collective-permute-start | bytes 393224 | tf_op jit(solution)/shard_map/ppermute | solution.py:475
  30.1 1.5 %collective-permute-start.10 = (bf16[256,256]{1,0:T(8,128)(2,1)S(1)}, bf16[256,256]{1,0:T(8,128)(2,1)S(1)}, u32[]{:S(2)}, u32[]{:S(2)}) collective-permute-start(bf16[256,256]{1,0:T(8,128)(2,1)S(1)} %collective-permute-done.6.refs_3_), channel_id=1, source_target_pairs={{0,1},{1,0},{2,3},{3,2},{4,5},{5,4},{6,7},{7,6},{8,9},{9,8},{10,11... | collective-permute-start | bytes 393224 | tf_op jit(solution)/shard_map/ppermute | solution.py:475
  31.6 23.8 %slice-start.1 = ((s8[8388608]{0:T(1024)(128)(4,1)}), s8[4194304]{0:T(1024)(128)(4,1)S(1)}, s32[]{:S(2)}) async-start(s8[8388608]{0:T(1024)(128)(4,1)} %bitcast.17), calls=%async_computation.1 | async-start | bytes 8388608
  43.3 2.1 %collective-permute-start.11 = (bf16[4,256,256]{2,1,0:T(8,128)(2,1)}, bf16[4,256,256]{2,1,0:T(8,128)(2,1)S(1)}, u32[]{:S(2)}, u32[]{:S(2)}) collective-permute-start(bf16[4,256,256]{2,1,0:T(8,128)(2,1)} %get-tuple-element.40), channel_id=1, source_target_pairs={{0,1},{1,0},{2,3},{3,2},{4,5},{5,4},{6,7},{7,6},{8,9},{9,8},{10,11... | collective-permute-start | bytes 1572872 | tf_op jit(solution)/shard_map/ppermute | solution.py:448
  43.6 4.5 %collective-permute-start.14 = (f32[64,64]{1,0:T(8,128)S(1)}, f32[64,64]{1,0:T(8,128)S(1)}, u32[]{:S(2)}, u32[]{:S(2)}) collective-permute-start(f32[64,64]{1,0:T(8,128)S(1)} %get-tuple-element.45), channel_id=1, source_target_pairs={{0,8},{8,0},{16,24},{24,16},{1,9},{9,1},{17,25},{25,17},{2,10},{10... | collective-permute-start | bytes 49160 | tf_op jit(solution)/shard_map/ppermute | solution.py:536
  45.8 8.4 %collective-permute-start.12 = (bf16[256,256]{1,0:T(8,128)(2,1)S(1)}, bf16[256,256]{1,0:T(8,128)(2,1)S(1)}, u32[]{:S(2)}, u32[]{:S(2)}) collective-permute-start(bf16[256,256]{1,0:T(8,128)(2,1)S(1)} %get-tuple-element.42), channel_id=1, source_target_pairs={{0,2},{1,3},{2,0},{3,1},{4,6},{5,7},{6,4},{7,5},{8,10},{9,11},{10,... | collective-permute-start | bytes 393224 | tf_op jit(solution)/shard_map/ppermute | solution.py:471
  47.2 8.3 %collective-permute-start.13 = (bf16[256,256]{1,0:T(8,128)(2,1)S(1)}, bf16[256,256]{1,0:T(8,128)(2,1)S(1)}, u32[]{:S(2)}, u32[]{:S(2)}) collective-permute-start(bf16[256,256]{1,0:T(8,128)(2,1)S(1)} %get-tuple-element.43), channel_id=1, source_target_pairs={{0,4},{1,5},{2,6},{3,7},{4,0},{5,1},{6,2},{7,3},{8,12},{9,13},{10,... | collective-permute-start | bytes 393224 | tf_op jit(solution)/shard_map/ppermute | solution.py:471
  48.1 7.4 %collective-permute-start.15 = (bf16[256,256]{1,0:T(8,128)(2,1)S(1)}, bf16[256,256]{1,0:T(8,128)(2,1)S(1)}, u32[]{:S(2)}, u32[]{:S(2)}) collective-permute-start(bf16[256,256]{1,0:T(8,128)(2,1)S(1)} %get-tuple-element.46), channel_id=1, source_target_pairs={{0,6},{1,7},{2,4},{3,5},{4,2},{5,3},{6,0},{7,1},{8,14},{9,15},{10,... | collective-permute-start | bytes 393224 | tf_op jit(solution)/shard_map/ppermute | solution.py:471
  49.4 4.8 %collective-permute-start.16 = (f32[64,64]{1,0:T(8,128)S(1)}, f32[64,64]{1,0:T(8,128)S(1)}, u32[]{:S(2)}, u32[]{:S(2)}) collective-permute-start(f32[64,64]{1,0:T(8,128)S(1)} %add.3.refs_4_), channel_id=1, source_target_pairs={{0,16},{8,24},{16,0},{24,8},{1,17},{9,25},{17,1},{25,9},{2,18},{10... | collective-permute-start | bytes 49160 | tf_op jit(solution)/shard_map/ppermute | solution.py:541
  59.1 8.9 %collective-permute-start.17 = (bf16[288,256]{1,0:T(8,128)(2,1)S(1)}, bf16[288,256]{1,0:T(8,128)(2,1)S(1)}, u32[]{:S(2)}, u32[]{:S(2)}) collective-permute-start(bf16[288,256]{1,0:T(8,128)(2,1)S(1)} %get-tuple-element.48.refs_0_), channel_id=1, source_target_pairs={{0,2},{1,3},{2,0},{3,1},{4,6},{5,7},{6,4},{7,5},{8,10},{9,11},{10,... | collective-permute-start | bytes 442376 | tf_op jit(solution)/shard_map/ppermute | solution.py:580
  59.9 8.2 %collective-permute-start.18 = (bf16[288,256]{1,0:T(8,128)(2,1)S(1)}, bf16[288,256]{1,0:T(8,128)(2,1)S(1)}, u32[]{:S(2)}, u32[]{:S(2)}) collective-permute-start(bf16[288,256]{1,0:T(8,128)(2,1)S(1)} %get-tuple-element.48.refs_0_), channel_id=1, source_target_pairs={{0,4},{1,5},{2,6},{3,7},{4,0},{5,1},{6,2},{7,3},{8,12},{9,13},{10,... | collective-permute-start | bytes 442376 | tf_op jit(solution)/shard_map/ppermute | solution.py:580
  61.2 7.0 %collective-permute-start.19 = (bf16[288,256]{1,0:T(8,128)(2,1)S(1)}, bf16[288,256]{1,0:T(8,128)(2,1)S(1)}, u32[]{:S(2)}, u32[]{:S(2)}) collective-permute-start(bf16[288,256]{1,0:T(8,128)(2,1)S(1)} %get-tuple-element.48.refs_0_), channel_id=1, source_target_pairs={{0,6},{1,7},{2,4},{3,5},{4,2},{5,3},{6,0},{7,1},{8,14},{9,15},{10,... | collective-permute-start | bytes 442376 | tf_op jit(solution)/shard_map/ppermute | solution.py:580
  62.6 8.8 %collective-permute-start.20 = (bf16[288,256]{1,0:T(8,128)(2,1)S(1)}, bf16[288,256]{1,0:T(8,128)(2,1)S(1)}, u32[]{:S(2)}, u32[]{:S(2)}) collective-permute-start(bf16[288,256]{1,0:T(8,128)(2,1)S(1)} %get-tuple-element.48.refs_0_), channel_id=1, source_target_pairs={{0,1},{1,0},{2,3},{3,2},{4,5},{5,4},{6,7},{7,6},{8,9},{9,8},{10,11... | collective-permute-start | bytes 442376 | tf_op jit(solution)/shard_map/ppermute | solution.py:583
  67.9 3.6 %copy-start.2 = (bf16[64,256]{1,0:T(8,128)(2,1)S(1)}, bf16[64,256]{1,0:T(8,128)(2,1)}, u32[]{:S(2)}) copy-start(bf16[64,256]{1,0:T(8,128)(2,1)} %constant.15.clone.refs_9_) | copy-start | bytes 98308
  68.1 3.3 %collective-permute-start.21 = (bf16[288,256]{1,0:T(8,128)(2,1)S(1)}, bf16[288,256]{1,0:T(8,128)(2,1)S(1)}, u32[]{:S(2)}, u32[]{:S(2)}) collective-permute-start(bf16[288,256]{1,0:T(8,128)(2,1)S(1)} %collective-permute-done.17.refs_1_), channel_id=1, source_target_pairs={{0,1},{1,0},{2,3},{3,2},{4,5},{5,4},{6,7},{7,6},{8,9},{9,8},{10,11... | collective-permute-start | bytes 442376 | tf_op jit(solution)/shard_map/ppermute | solution.py:583
  68.6 2.9 %collective-permute-start.22 = (bf16[288,256]{1,0:T(8,128)(2,1)S(1)}, bf16[288,256]{1,0:T(8,128)(2,1)S(1)}, u32[]{:S(2)}, u32[]{:S(2)}) collective-permute-start(bf16[288,256]{1,0:T(8,128)(2,1)S(1)} %collective-permute-done.18.refs_2_), channel_id=1, source_target_pairs={{0,1},{1,0},{2,3},{3,2},{4,5},{5,4},{6,7},{7,6},{8,9},{9,8},{10,11... | collective-permute-start | bytes 442376 | tf_op jit(solution)/shard_map/ppermute | solution.py:583
  68.6 2.8 %collective-permute-start.23 = (bf16[288,256]{1,0:T(8,128)(2,1)S(1)}, bf16[288,256]{1,0:T(8,128)(2,1)S(1)}, u32[]{:S(2)}, u32[]{:S(2)}) collective-permute-start(bf16[288,256]{1,0:T(8,128)(2,1)S(1)} %collective-permute-done.19.refs_3_), channel_id=1, source_target_pairs={{0,1},{1,0},{2,3},{3,2},{4,5},{5,4},{6,7},{7,6},{8,9},{9,8},{10,11... | collective-permute-start | bytes 442376 | tf_op jit(solution)/shard_map/ppermute | solution.py:583
